TPU v7x, 512 devices: a whole 4x8x8 slice. The times are simulated.
512 devices in a mesh: expert: 32 (over x, z_hi, core), tensor: 8 (over y), dp: 2 (over z_lo).
Axes of the slice: x: 4, y: 8, z: 8 (z_hi: 4, z_lo: 2; z = z_hi * 2 + z_lo), core: 2. Of those that a mesh axis runs over, the one named last changes fastest.
Arguments:
- tokens: bfloat16 [6144, 5120], P(('dp', 'expert'), 'tensor'), parts along dimension 0, may hold values from -6 to 6
- routes: int32 [6144, 6], P(('dp', 'expert')), parts along dimension 0, may hold values from 0 to 31, all different within a row; in each aligned block of 96 rows (0 to 95, 96 to 191, ...) at most 18 rows name the same one
- gates: float32 [6144, 6], P(('dp', 'expert')), parts along dimension 0, may hold values from 0.05 to 0.6
- gate_up: bfloat16 [32, 5120, 2, 1024], P('expert', None, None, 'tensor'), may hold values from -0.078125 to 0.078125
- down_weight: bfloat16 [32, 5120, 1024], P('expert', None, 'tensor'), may hold values from -0.1875 to 0.1875
- old_map: int32 [32], replicated, may hold values from 0 to 31, each once
- new_map: int32 [32], replicated, may hold values from 0 to 31, each once
Outputs:
- mixed: bfloat16 [6144, 5120], P(('dp', 'expert'), 'tensor'), parts along dimension 0
There are 2 independent parts, one for each index of `dp`. A program takes and returns all parts, laid end to end along the dimension named above; an argument that names none is the same for every part. Nothing has to cross between parts.
Inputs may be any that keep to these rules, and one draw needn't show every extreme that they name: `routes`: each row names 6 different slots; in each aligned block of 96 rows (the rows of one index of expert) no slot is named by more than 18 rows; since each row names 6 different slots, every slot is then named by exactly 18 rows of every block. `old_map`: each expert appears exactly once. `new_map`: each expert appears exactly once.
All inputs are finite; a program needn't handle non-finite values.
Results may differ from a plain program's by a relative error of at most 0.0058.
Values may be sent and summed in bfloat16 or wider, within the bound.
No kernel may reach another device: no remote copies, remote signals or barrier semaphores. Data moves between devices by JAX's collectives and lax.ppermute only.
A program may use at most 64 MiB of HBM per device.

v0:
```python
import jax
import jax.numpy as jnp
from jax import lax
from jax.sharding import Mesh
from jax.sharding import PartitionSpec as P

EXPERT = ("expert_0", "expert_1", "expert_2")
DP_EXPERT = ("dp", "expert_0", "expert_1", "expert_2")


def in_blocks(x, dim, size):
    lengths = x.shape
    parts = x.reshape(*lengths[:dim], size, lengths[dim] // size, *lengths[dim + 1 :])
    return jnp.moveaxis(parts, dim, 0)


def laid_out(parts, dim):
    parts = jnp.moveaxis(parts, 0, dim)
    lengths = parts.shape
    return parts.reshape(*lengths[:dim], lengths[dim] * lengths[dim + 1], *lengths[dim + 2 :])


def exchange_in_order(parts, axes, order):
    lengths = [lax.axis_size(a) for a in axes]
    parts = parts.reshape(*lengths, *parts.shape[1:])
    for k in order:
        parts = lax.all_to_all(parts, axes[k], split_axis=k, concat_axis=k, tiled=True)
    return parts.reshape(-1, *parts.shape[len(axes) :])


def core_and_chips(x, groups, order, split_dim, concat_dim):
    size = lax.axis_size(groups[0]) * lax.axis_size(groups[1])
    parts = in_blocks(x, split_dim, size)
    return laid_out(exchange_in_order(parts, groups, order), concat_dim)


def from_everyone(x, axis):
    size = lax.axis_size(axis)
    return lax.all_to_all(jnp.broadcast_to(x[None], (size, *x.shape)), axis, 0, 0, tiled=True)


def collect(x, axis, dim):
    parts = from_everyone(x, axis)
    return laid_out(parts, dim)


def local(tokens, routes, gates, gate_up, down_weight, old_map, new_map):
    experts = lax.axis_size(EXPERT)
    tensor_count = lax.axis_size("tensor")
    tok_rows = tokens.shape[0]
    feature_part = tokens.shape[1]
    picks_row = routes.shape[1]
    capacity = (tok_rows * picks_row + experts - 1) // experts
    width = gate_up.shape[1]
    hidden = down_weight.shape[2]
    buffer_rows = experts * capacity
    slot_ids = jnp.arange(experts, dtype=jnp.int32)
    holder = jnp.sum(jnp.where(new_map[:, None] == old_map[None, :], slot_ids[None, :], 0), axis=1)
    weight_in = gate_up.reshape(width, 2 * hidden)
    weight_out = down_weight.reshape(width, hidden)
    target = jnp.sum(
        jnp.where(routes[:, :, None] == slot_ids[None, None, :], holder[None, None, :], 0), axis=2
    )
    flat_target = target.reshape(-1)
    onehot = (flat_target[:, None] == slot_ids[None, :]).astype(jnp.int32)
    earlier = jnp.cumsum(onehot, axis=0) - onehot
    position = jnp.sum(earlier * onehot, axis=1)
    slot_index = flat_target * capacity + position
    columns = jnp.arange(buffer_rows, dtype=jnp.int32)
    matches = (slot_index[:, None] == columns[None, :]).reshape(tok_rows, picks_row, buffer_rows)
    assign = jnp.sum(matches.astype(jnp.float32), axis=1).astype(jnp.bfloat16)
    combine_weights = jnp.sum(jnp.where(matches, gates[:, :, None], 0.0), axis=1)
    outgoing = lax.dot_general(
        assign, tokens, (((0,), (0,)), ((), ())), preferred_element_type=jnp.float32
    )
    outgoing = outgoing.astype(jnp.bfloat16).reshape(experts, capacity, feature_part)
    arrived = core_and_chips(outgoing, (("expert_0", "expert_1"), "expert_2"), (1, 0), 0, 0)
    piece = lax.all_gather(arrived, "tensor", axis=2, tiled=True)
    flat_piece = piece.reshape(buffer_rows, piece.shape[2])
    projected = jnp.dot(flat_piece, weight_in, preferred_element_type=jnp.float32)
    activation = (jax.nn.silu(projected[:, :hidden]) * projected[:, hidden:]).astype(jnp.bfloat16)
    down_parts = weight_out.reshape(tensor_count, width // tensor_count, hidden)
    down_mine = lax.all_to_all(
        down_parts, "tensor", split_axis=0, concat_axis=2, tiled=True
    ).reshape(width // tensor_count, tensor_count * hidden)
    summed = lax.dot_general(
        collect(activation, "tensor", 1),
        down_mine,
        (((1,), (1,)), ((), ())),
        preferred_element_type=jnp.float32,
    )
    expert_out = summed.astype(jnp.bfloat16).reshape(experts, capacity, feature_part)
    returned = lax.all_to_all(expert_out, EXPERT, split_axis=0, concat_axis=0, tiled=True)
    gathered_back = returned.reshape(buffer_rows, feature_part).astype(jnp.float32)
    mixed = jnp.dot(
        combine_weights,
        gathered_back,
        precision=lax.Precision.HIGHEST,
        preferred_element_type=jnp.float32,
    )
    return mixed.astype(jnp.bfloat16)


def solution(mesh):
    split = Mesh(
        mesh.devices.reshape(4, 4, 2, mesh.shape["tensor"], mesh.shape["dp"]),
        ("expert_0", "expert_1", "expert_2", "tensor", "dp"),
    )
    in_specs = (
        P(DP_EXPERT, "tensor"),
        P(DP_EXPERT, None),
        P(DP_EXPERT, None),
        P(EXPERT, None, None, "tensor"),
        P(EXPERT, None, "tensor"),
        P(),
        P(),
    )
    out_specs = P(DP_EXPERT, "tensor")
    return jax.shard_map(local, mesh=split, in_specs=in_specs, out_specs=out_specs, check_vma=False)
```

profile of v0, /device:TPU:64, one launch (start us, length us, event | category | flops | bytes accessed | tf_op | source)
XLA Modules:
  0.0 253.1 jit_solution(2696037991912060983)
XLA Ops:
  6.5 0.9 select_reduce_fusion.2
  7.4 0.8 select_reduce_fusion.1
  8.5 1.5 reduce-window.6
  10.0 0.3 slice_reduce_fusion
  10.6 1.1 convert_reduce_fusion
  11.7 0.4 convolution_convert_fusion.1
  12.4 4.3 %all_to_all.35 = bf16[16,2,1,18,640]{4,0,3,2,1:T(8,128)(2,1)S(1)} all-to-all(bf16[16,2,1,18,640]{4,0,3,2,1:T(8,128)(2,1)S(1)} %copy.41), channel_id=1, replica_groups=mesh['expert_0'=4,'expert_1'=4,'expert_2'=2,'tensor'=8,'dp'=2] {'expert_2'}, dimensions={1} | all-to-all | bytes 1474560 | tf_op jit(solution)/shard_map/all_to_all | solution.py:27
  16.7 0.6 copy.42
  17.3 35.1 %all_to_all.36 = bf16[16,2,1,18,640]{4,1,3,2,0:T(2,128)(2,1)S(1)} all-to-all(bf16[16,2,1,18,640]{4,1,3,2,0:T(2,128)(2,1)S(1)} %copy.42), channel_id=1, replica_groups=mesh['expert_0'=4,'expert_1'=4,'expert_2'=2,'tensor'=8,'dp'=2] {'expert_..., dimensions={0} | all-to-all | bytes 1474560 | tf_op jit(solution)/shard_map/all_to_all | solution.py:27
  52.4 0.5 copy.43
  52.9 1.1 reshape_reshape.6
  54.1 7.1 %all-to-all-start.3 = ((bf16[8,640,128]{2,1,0:T(8,128)(2,1)}), bf16[8,640,128]{2,1,0:T(8,128)(2,1)S(1)}, u32[]{:S(2)}, u32[]{:S(2)}) async-start(bf16[8,640,128]{2,1,0:T(8,128)(2,1)} %bitcast.2), calls=%async_computation.3 | async-start | bytes 2621440 | tf_op jit(solution)/shard_map/all_to_all | solution.py:83
  61.2 86.8 %all-gather.2.cloned.1.call-done = bf16[32,18,5120]{2,0,1:T(8,128)(2,1)} async-done(((bf16[32,18,640]{2,0,1:T(8,128)(2,1)}), bf16[32,18,5120]{2,0,1:T(8,128)(2,1)}) %all-gather.2.cloned.1.call-update) | async-done | bytes 5898256 | tf_op jit(solution)/shard_map/all_gather | solution.py:78
  148.0 9.2 %copy.44 = bf16[32,18,5120]{2,1,0:T(8,128)(2,1)} copy(bf16[32,18,5120]{2,0,1:T(8,128)(2,1)} %all-gather.2.cloned.1.call-done) | data formatting | bytes 11796480 | tf_op jit(solution)/shard_map/all_gather | solution.py:78
  157.1 8.8 %reshape.57 = bf16[576,5120]{1,0:T(8,128)(2,1)} reshape(bf16[32,18,5120]{2,1,0:T(8,128)(2,1)} %copy.44) | data formatting | bytes 11796480 | tf_op jit(solution)/shard_map/reshape | solution.py:79
  165.9 5.2 %fusion = f32[576,256]{1,0:T(8,128)S(1)} fusion(bf16[576,5120]{1,0:T(8,128)(2,1)} %reshape.57, bf16[640,8,2,128]{3,2,1,0:T(2,128)(2,1)} %bitcast.42), kind=kOutput, calls=%fused_computation | convolution fusion | flops 1509949440 | bytes 9109504 | tf_op jit(solution)/shard_map/dot_general | solution.py:80
  171.2 1.2 broadcast_in_dim.58
  172.4 4.5 %all-to-all-start.2 = ((bf16[8,576,128]{2,1,0:T(8,128)(2,1)}), bf16[8,576,128]{2,1,0:T(8,128)(2,1)}, u32[]{:S(2)}, u32[]{:S(2)}) async-start(bf16[8,576,128]{2,1,0:T(8,128)(2,1)} %broadcast_in_dim.58), calls=%async_computation.2 | async-start | bytes 2359296 | tf_op jit(solution)/shard_map/all_to_all | solution.py:39
  176.9 0.7 copy.46
  177.6 31.1 %all-to-all-done.2 = bf16[8,576,128]{2,1,0:T(8,128)(2,1)} async-done(((bf16[8,576,128]{2,1,0:T(8,128)(2,1)}), bf16[8,576,128]{2,1,0:T(8,128)(2,1)}, u32[]{:S(2)}, u32[]{:S(2)}) %all-to-all-start.2) | async-done | bytes 1179680 | tf_op jit(solution)/shard_map/all_to_all | solution.py:39
  208.8 3.3 %convolution_convert_fusion = bf16[576,640]{1,0:T(8,128)(2,1)} fusion(bf16[640,1024]{0,1:T(8,128)(2,1)S(1)} %bitcast.40, bf16[8,576,128]{2,1,0:T(8,128)(2,1)} %all-to-all-done.2), kind=kOutput, calls=%fused_computation.6 | convolution fusion | flops 755343360 | bytes 3227648 | tf_op jit(solution)/shard_map/dot_general | solution.py:86
  212.0 1.3 reshape.61
  213.3 31.5 %all_to_all.37 = bf16[32,18,640]{2,1,0:T(8,128)(2,1)S(1)} all-to-all(bf16[32,18,640]{2,1,0:T(8,128)(2,1)S(1)} %reshape.61), channel_id=1, replica_groups=mesh['expert_0'=4,'expert_1'=4,'expert_2'=2,'tensor'=8,'dp'=2] {'expert_..., dimensions={0} | all-to-all | bytes 1474560 | tf_op jit(solution)/shard_map/all_to_all | solution.py:93
  245.0 1.2 convolution_convert_fusion.2
  (19 shorter events, 1.3 us)
Async XLA Ops:
  6.5 5.1 %copy-start = (bf16[96,640]{1,0:T(8,128)(2,1)S(1)}, bf16[96,640]{1,0:T(8,128)(2,1)}, u32[]{:S(2)}) copy-start(bf16[96,640]{1,0:T(8,128)(2,1)} %param.7) | copy-start | bytes 368644
  6.5 141.4 %all-gather.2.cloned.1.call-start = ((), (), s32[]{:S(2)}) async-start(), calls=%async_computation.5 | async-start | bytes 6635520 | tf_op jit(solution)/shard_map/all_gather | solution.py:78
  54.1 117.1 %all-to-all-start.3 = ((bf16[8,640,128]{2,1,0:T(8,128)(2,1)}), bf16[8,640,128]{2,1,0:T(8,128)(2,1)S(1)}, u32[]{:S(2)}, u32[]{:S(2)}) async-start(bf16[8,640,128]{2,1,0:T(8,128)(2,1)} %bitcast.2), calls=%async_computation.3 | async-start | bytes 2621440 | tf_op jit(solution)/shard_map/all_to_all | solution.py:83
  172.4 36.4 %all-to-all-start.2 = ((bf16[8,576,128]{2,1,0:T(8,128)(2,1)}), bf16[8,576,128]{2,1,0:T(8,128)(2,1)}, u32[]{:S(2)}, u32[]{:S(2)}) async-start(bf16[8,576,128]{2,1,0:T(8,128)(2,1)} %broadcast_in_dim.58), calls=%async_computation.2 | async-start | bytes 2359296 | tf_op jit(solution)/shard_map/all_to_all | solution.py:39
Sparse Core Ops, SparseCore 0:
  54.2 93.7 all-gather.1
where the time goes:
time: 254 us; the launch traced here: 253 us
  waiting for transfers between devices  118 us (46%)
  blocking collectives  70.8 us (28%)
  local copies, waits for them, and re-layouts  24.6 us (10%)
  between operations  13.5 us (5%)
  starting transfers between devices  11.7 us (5%)
  matrix products  10 us (4%)
  other arithmetic  4.47 us (2%)
    all_gather x1, waiting for transfers between devices, local(): piece = lax.all_gather(arrived, 'tensor', axis=2, tiled=True)  86.8 us
    all_to_all x2, blocking collectives, exchange_in_order(): lax.all_to_all(parts, axes[k], split_axis=k, concat_axis=k, tiled=True)  39.4 us
    all_to_all x1, blocking collectives, local(): lax.all_to_all(expert_out, EXPERT, split_axis=0, concat_axis=0, tiled=True)  31.5 us
    all_to_all x1, waiting for transfers between devices, from_everyone(): lax.all_to_all(jnp.broadcast_to(x[None], (size, *x.shape)), axis, 0, 0, t...  31.1 us
    all_gather x1, local copies, waits for them, and re-layouts, local(): piece = lax.all_gather(arrived, 'tensor', axis=2, tiled=True)  9.16 us
    reshape x1, local copies, waits for them, and re-layouts, local(): flat_piece = piece.reshape(buffer_rows, piece.shape[2])  8.78 us
    all_to_all x1, starting transfers between devices, local(): lax.all_to_all(down_parts, 'tensor', split_axis=0, concat_axis=2, tiled=T...  7.11 us
    dot_general x1, matrix products, local(): jnp.dot(flat_piece, weight_in, preferred_element_type=jnp.float32)  5.15 us
  transfers between devices with their start and end apart: 3, of which 2 were waited for; matrix products, arithmetic and copies ran while one was open for 9% of the time, Pallas kernels for 0%

commit v1 on v0

v1 whole, which is shorter than its diff:
```python
import jax
import jax.numpy as jnp
from jax import lax
from jax.sharding import Mesh
from jax.sharding import PartitionSpec as P


EXPERT = ("expert_0", "expert_1", "expert_2")
CHIPS = ("expert_0", "expert_1")
DP_EXPERT = ("dp", "expert_0", "expert_1", "expert_2")


def dot(a, b, dims=((1,), (0,))):
    return lax.dot_general(a, b, (dims, ((), ())), preferred_element_type=jnp.float32)


def ring_pairs(size, step):
    return [(i, (i + step) % size) for i in range(size)]


def ring(x, size, use):
    forward = [(i, (i + 1) % size) for i in range(size)]
    backward = [(i, (i - 1) % size) for i in range(size)]
    rows = x.shape[0]
    use(x, 0, slice(0, rows))
    up = down = x
    for step in range(1, size // 2):
        up = lax.ppermute(up, "tensor", forward)
        down = lax.ppermute(down, "tensor", backward)
        use(up, -step, slice(0, rows))
        use(down, step, slice(0, rows))
    half = rows // 2
    use(lax.ppermute(up[:half], "tensor", forward), size // 2, slice(0, half))
    use(lax.ppermute(down[half:], "tensor", backward), size // 2, slice(half, rows))


def local(tokens, routes, gates, gate_up, down_weight, old_map, new_map):
    experts = lax.axis_size(EXPERT)
    chips = lax.axis_size(CHIPS)
    size = lax.axis_size("tensor")
    me = lax.axis_index("tensor")
    tok_rows, part = tokens.shape
    picks = routes.shape[1]
    capacity = (tok_rows * picks + experts - 1) // experts
    width = gate_up.shape[1]
    hidden = down_weight.shape[2]
    bf16 = jnp.bfloat16

    down_parts = down_weight.reshape(size, width // size, hidden)
    down_from = {}
    for step in (1, 7, 2, 6, 3, 5, 4):
        block = lax.dynamic_index_in_dim(down_parts, lax.rem(me + step, size), 0, keepdims=False)
        down_from[size - step] = lax.ppermute(block, "tensor", ring_pairs(size, step))
    down_from[0] = lax.dynamic_index_in_dim(down_parts, me, 0, keepdims=False)

    slot_ids = jnp.arange(experts, dtype=jnp.int32)
    holder = jnp.sum(jnp.where(new_map[:, None] == old_map[None, :], slot_ids[None, :], 0), axis=1)
    target = jnp.sum(
        jnp.where(routes[:, :, None] == slot_ids[None, None, :], holder[None, None, :], 0), axis=2
    )
    hits = target[:, :, None] == slot_ids[None, None, :]
    member = jnp.any(hits, axis=1)
    weight = jnp.sum(jnp.where(hits, gates[:, :, None], 0.0), axis=1)
    ones = jnp.tril(jnp.ones((tok_rows, tok_rows), bf16), -1)
    position = dot(ones, member.astype(bf16)).astype(jnp.int32)
    place = jnp.where(member, position, -1)
    cap_ids = jnp.arange(capacity, dtype=jnp.int32)
    order = jnp.arange(experts).reshape(chips, 2).T.reshape(-1)
    matches = place[:, order][:, :, None] == cap_ids[None, None, :]
    assign = matches.astype(bf16).reshape(tok_rows, experts * capacity)
    combine = jnp.where(matches, weight[:, order][:, :, None], 0.0).reshape(tok_rows, experts * capacity)
    outgoing = dot(assign, tokens, ((0,), (0,))).astype(bf16)

    weight_in = gate_up.reshape(size, part, 2 * hidden)

    def gathered(x):
        pieces = []

        def use(block, distance, rows_of):
            w = lax.dynamic_index_in_dim(weight_in, lax.rem(me + distance + size, size), 0, keepdims=False)
            pieces.append((dot(block, w), rows_of))

        ring(x, size, use)
        total = sum(p for p, s in pieces[:-2])
        total = total + jnp.concatenate([pieces[-2][0], pieces[-1][0]], axis=0)
        return (jax.nn.silu(total[:, :hidden]) * total[:, hidden:]).astype(bf16)

    def expert_rows(x):
        act = gathered(x)
        pieces = []

        def use(block, distance, rows_of):
            pieces.append((dot(block, down_from[distance % size], ((1,), (1,))), rows_of))

        ring(act, size, use)
        total = sum(p for p, s in pieces[:-2])
        total = total + jnp.concatenate([pieces[-2][0], pieces[-1][0]], axis=0)
        return total.astype(bf16)

    own_core = lax.axis_index("expert_2")
    both = outgoing.reshape(2, chips * capacity, part)
    mine = lax.dynamic_index_in_dim(both, own_core, 0, keepdims=False)
    other = lax.dynamic_index_in_dim(both, 1 - own_core, 0, keepdims=False)
    swap = [(0, 1), (1, 0)]
    other = lax.ppermute(other, "expert_2", swap)

    def over_chips(x):
        x = x.reshape(chips, capacity, part)
        x = lax.all_to_all(x, CHIPS, 0, 0, tiled=True)
        return x.reshape(chips * capacity, part)

    back_mine = over_chips(expert_rows(over_chips(mine)))
    back_other = over_chips(expert_rows(over_chips(other)))
    back_other = lax.ppermute(back_other, "expert_2", swap)
    combine = combine.reshape(tok_rows, 2, chips * capacity)
    take = lambda i: lax.dynamic_index_in_dim(combine, i, 1, keepdims=False)

    def mix(c, rows):
        return jnp.dot(
            c, rows.astype(jnp.float32), precision=lax.Precision.HIGHEST, preferred_element_type=jnp.float32
        )

    return (mix(take(own_core), back_mine) + mix(take(1 - own_core), back_other)).astype(bf16)


def solution(mesh):
    split = Mesh(
        mesh.devices.reshape(4, 4, 2, mesh.shape["tensor"], mesh.shape["dp"]),
        ("expert_0", "expert_1", "expert_2", "tensor", "dp"),
    )
    in_specs = (
        P(DP_EXPERT, "tensor"),
        P(DP_EXPERT, None),
        P(DP_EXPERT, None),
        P(EXPERT, None, None, "tensor"),
        P(EXPERT, None, "tensor"),
        P(),
        P(),
    )
    return jax.shard_map(local, mesh=split, in_specs=in_specs, out_specs=P(DP_EXPERT, "tensor"), check_vma=False)
```

time: 254 us -> 278 us (1.094)
  the two profiles are of different devices: /device:TPU:64 before, /device:TPU:88 now
where the time goes in v1:
time: 278 us; the launch traced here: 276 us
  starting transfers between devices  166 us (60%)
  waiting for transfers between devices  71.6 us (26%)
  matrix products  20.7 us (7%)
  local copies, waits for them, and re-layouts  14.1 us (5%)
    ppermute x12, starting transfers between devices, ring(): up = lax.ppermute(up, 'tensor', forward)  53.2 us
    all_to_all x4, waiting for transfers between devices, over_chips(): x = lax.all_to_all(x, CHIPS, 0, 0, tiled=True)  37.1 us
    ppermute x12, starting transfers between devices, ring(): down = lax.ppermute(down, 'tensor', backward)  29.2 us
    all_to_all x4, starting transfers between devices, over_chips(): x = lax.all_to_all(x, CHIPS, 0, 0, tiled=True)  28.8 us
    ppermute x7, starting transfers between devices, local(): lax.ppermute(block, 'tensor', ring_pairs(size, step))  26.7 us
    dot_general x38, matrix products, dot(): lax.dot_general(a, b, (dims, ((), ())), preferred_element_type=jnp.float32)  19 us
    ppermute x12, waiting for transfers between devices, ring(): down = lax.ppermute(down, 'tensor', backward)  16.3 us
    ppermute x4, starting transfers between devices, ring(): use(lax.ppermute(up[:half], 'tensor', forward), size // 2, slice(0, half))  15.9 us
  transfers between devices with their start and end apart: 45, of which 13 were waited for; matrix products, arithmetic and copies ran while one was open for 11% of the time, Pallas kernels for 0%

profile of v1, /device:TPU:88, one launch (start us, length us, event | category | flops | bytes accessed | tf_op | source)
XLA Modules:
  0.0 275.8 jit_solution(5883221139608213698)
XLA Ops:
  4.2 12.0 %all-to-all-start = ((bf16[16,18,640]{2,1,0:T(8,128)(2,1)}), bf16[16,18,640]{2,1,0:T(8,128)(2,1)S(1)}, u32[]{:S(2)}, u32[]{:S(2)}) async-start(bf16[16,18,640]{2,1,0:T(8,128)(2,1)} %reshape.104), calls=%async_computation | async-start | bytes 983040 | tf_op jit(solution)/shard_map/all_to_all | solution.py:109
  20.7 13.4 %all-to-all-done = bf16[16,18,640]{2,1,0:T(8,128)(2,1)S(1)} async-done(((bf16[16,18,640]{2,1,0:T(8,128)(2,1)}), bf16[16,18,640]{2,1,0:T(8,128)(2,1)S(1)}, u32[]{:S(2)}, u32[]{:S(2)}) %all-to-all-start) | async-done | bytes 368672 | tf_op jit(solution)/shard_map/all_to_all | solution.py:109
  34.1 4.2 %all-to-all-start.2 = ((bf16[16,18,640]{2,1,0:T(8,128)(2,1)}), bf16[16,18,640]{2,1,0:T(8,128)(2,1)}, u32[]{:S(2)}, u32[]{:S(2)}) async-start(bf16[16,18,640]{2,1,0:T(8,128)(2,1)} %reshape.110), calls=%async_computation.2 | async-start | bytes 983040 | tf_op jit(solution)/shard_map/all_to_all | solution.py:109
  38.5 4.7 %collective-permute-start = (bf16[288,640]{1,0:T(8,128)(2,1)S(1)}, bf16[288,640]{1,0:T(8,128)(2,1)}, u32[]{:S(2)}, u32[]{:S(2)}) collective-permute-start(bf16[288,640]{1,0:T(8,128)(2,1)S(1)} %reshape.105), channel_id=1, source_target_pairs={{0,2},{2,4},{4,6},{6,8},{8,10},{10,12},{12,14},{14,0},{1,3},{3,5},... | collective-permute-start | bytes 1105928 | tf_op jit(solution)/shard_map/ppermute | solution.py:28
  59.4 5.0 %collective-permute-start.24 = (bf16[288,640]{1,0:T(8,128)(2,1)}, bf16[288,640]{1,0:T(8,128)(2,1)S(1)}, u32[]{:S(2)}, u32[]{:S(2)}) collective-permute-start(bf16[288,640]{1,0:T(8,128)(2,1)} %reshape.111), channel_id=1, source_target_pairs={{0,2},{2,4},{4,6},{6,8},{8,10},{10,12},{12,14},{14,0},{1,3},{3,5},... | collective-permute-start | bytes 1105928 | tf_op jit(solution)/shard_map/ppermute | solution.py:28
  75.6 5.3 %collective-permute-start.26 = (bf16[288,640]{1,0:T(8,128)(2,1)S(1)}, bf16[288,640]{1,0:T(8,128)(2,1)S(1)}, u32[]{:S(2)}, u32[]{:S(2)}) collective-permute-start(bf16[288,640]{1,0:T(8,128)(2,1)S(1)} %collective-permute-done.24), channel_id=1, source_target_pairs={{0,2},{2,4},{4,6},{6,8},{8,10},{10,12},{12,14},{14,0},{1,3},{3,5},... | collective-permute-start | bytes 1105928 | tf_op jit(solution)/shard_map/ppermute | solution.py:28
  86.0 5.1 %collective-permute-start.4 = (bf16[288,640]{1,0:T(8,128)(2,1)S(1)}, bf16[288,640]{1,0:T(8,128)(2,1)S(1)}, u32[]{:S(2)}, u32[]{:S(2)}) collective-permute-start(bf16[288,640]{1,0:T(8,128)(2,1)S(1)} %collective-permute-done.2), channel_id=1, source_target_pairs={{0,2},{2,4},{4,6},{6,8},{8,10},{10,12},{12,14},{14,0},{1,3},{3,5},... | collective-permute-start | bytes 1105928 | tf_op jit(solution)/shard_map/ppermute | solution.py:28
  91.7 4.5 %collective-permute-done.5 = bf16[288,640]{1,0:T(8,128)(2,1)S(1)} collective-permute-done((bf16[288,640]{1,0:T(8,128)(2,1)S(1)}, bf16[288,640]{1,0:T(8,128)(2,1)S(1)}, u32[]{:S(2)}, u32[]{:S(2)}) %collective-permute-start.5) | collective-permute-done | bytes 368672 | tf_op jit(solution)/shard_map/ppermute | solution.py:29
  100.1 6.0 %collective-permute-start.13 = (bf16[640,128]{1,0:T(8,128)(2,1)S(1)}, bf16[640,128]{1,0:T(8,128)(2,1)S(1)}, u32[]{:S(2)}, u32[]{:S(2)}) collective-permute-start(bf16[640,128]{1,0:T(8,128)(2,1)S(1)} %copy-done.8), channel_id=1, source_target_pairs={{0,4},{2,6},{4,8},{6,10},{8,12},{10,14},{12,0},{14,2},{1,5},{3,7},... | collective-permute-start | bytes 491528 | tf_op jit(solution)/shard_map/ppermute | solution.py:53
  109.6 5.6 %collective-permute-done.7 = bf16[144,640]{1,0:T(8,128)(2,1)S(1)} collective-permute-done((bf16[144,640]{1,0:T(8,128)(2,1)S(1)}, bf16[144,640]{1,0:T(8,128)(2,1)S(1)}, u32[]{:S(2)}, u32[]{:S(2)}) %collective-permute-start.7) | collective-permute-done | bytes 184352 | tf_op jit(solution)/shard_map/ppermute | solution.py:34
  118.1 4.5 %collective-permute-done.6 = bf16[144,640]{1,0:T(8,128)(2,1)S(1)} collective-permute-done((bf16[144,640]{1,0:T(8,128)(2,1)S(1)}, bf16[144,640]{1,0:T(8,128)(2,1)S(1)}, u32[]{:S(2)}, u32[]{:S(2)}) %collective-permute-start.6) | collective-permute-done | bytes 184352 | tf_op jit(solution)/shard_map/ppermute | solution.py:33
  135.9 5.8 %collective-permute-start.19 = (bf16[640,128]{1,0:T(8,128)(2,1)S(1)}, bf16[640,128]{1,0:T(8,128)(2,1)S(1)}, u32[]{:S(2)}, u32[]{:S(2)}) collective-permute-start(bf16[640,128]{1,0:T(8,128)(2,1)S(1)} %copy-done.7), channel_id=1, source_target_pairs={{0,10},{2,12},{4,14},{6,0},{8,2},{10,4},{12,6},{14,8},{1,11},{3,13... | collective-permute-start | bytes 491528 | tf_op jit(solution)/shard_map/ppermute | solution.py:53
  144.0 4.8 %collective-permute-start.14 = (bf16[288,128]{1,0:T(8,128)(2,1)S(1)}, bf16[288,128]{1,0:T(8,128)(2,1)S(1)}, u32[]{:S(2)}, u32[]{:S(2)}) collective-permute-start(bf16[288,128]{1,0:T(8,128)(2,1)S(1)} %collective-permute-done.10), channel_id=1, source_target_pairs={{0,14},{2,0},{4,2},{6,4},{8,6},{10,8},{12,10},{14,12},{1,15},{3,1}... | collective-permute-start | bytes 221192 | tf_op jit(solution)/shard_map/ppermute | solution.py:29
  168.0 4.7 %collective-permute-start.17 = (bf16[640,128]{1,0:T(8,128)(2,1)S(1)}, bf16[640,128]{1,0:T(8,128)(2,1)S(1)}, u32[]{:S(2)}, u32[]{:S(2)}) collective-permute-start(bf16[640,128]{1,0:T(8,128)(2,1)S(1)} %copy-done.5), channel_id=1, source_target_pairs={{0,6},{2,8},{4,10},{6,12},{8,14},{10,0},{12,2},{14,4},{1,7},{3,9},... | collective-permute-start | bytes 491528 | tf_op jit(solution)/shard_map/ppermute | solution.py:53
  175.4 5.0 %collective-permute-start.30 = (bf16[144,640]{1,0:T(8,128)(2,1)S(1)}, bf16[144,640]{1,0:T(8,128)(2,1)S(1)}, u32[]{:S(2)}, u32[]{:S(2)}) collective-permute-start(bf16[144,640]{1,0:T(8,128)(2,1)S(1)} %slice.58), channel_id=1, source_target_pairs={{0,2},{2,4},{4,6},{6,8},{8,10},{10,12},{12,14},{14,0},{1,3},{3,5},... | collective-permute-start | bytes 552968 | tf_op jit(solution)/shard_map/ppermute | solution.py:33
  193.0 5.1 %collective-permute-start.34 = (bf16[288,128]{1,0:T(8,128)(2,1)S(1)}, bf16[288,128]{1,0:T(8,128)(2,1)S(1)}, u32[]{:S(2)}, u32[]{:S(2)}) collective-permute-start(bf16[288,128]{1,0:T(8,128)(2,1)S(1)} %collective-permute-done.32), channel_id=1, source_target_pairs={{0,2},{2,4},{4,6},{6,8},{8,10},{10,12},{12,14},{14,0},{1,3},{3,5},... | collective-permute-start | bytes 221192 | tf_op jit(solution)/shard_map/ppermute | solution.py:28
  201.5 5.3 %collective-permute-done.35 = bf16[288,128]{1,0:T(8,128)(2,1)S(1)} collective-permute-done((bf16[288,128]{1,0:T(8,128)(2,1)S(1)}, bf16[288,128]{1,0:T(8,128)(2,1)S(1)}, u32[]{:S(2)}, u32[]{:S(2)}) %collective-permute-start.35) | collective-permute-done | bytes 73760 | tf_op jit(solution)/shard_map/ppermute | solution.py:29
  209.0 5.1 %collective-permute-start.36 = (bf16[288,128]{1,0:T(8,128)(2,1)S(1)}, bf16[288,128]{1,0:T(8,128)(2,1)S(1)}, u32[]{:S(2)}, u32[]{:S(2)}) collective-permute-start(bf16[288,128]{1,0:T(8,128)(2,1)S(1)} %collective-permute-done.34), channel_id=1, source_target_pairs={{0,2},{2,4},{4,6},{6,8},{8,10},{10,12},{12,14},{14,0},{1,3},{3,5},... | collective-permute-start | bytes 221192 | tf_op jit(solution)/shard_map/ppermute | solution.py:28
  218.0 5.5 %collective-permute-start.38 = (bf16[144,128]{1,0:T(8,128)(2,1)S(1)}, bf16[144,128]{1,0:T(8,128)(2,1)S(1)}, u32[]{:S(2)}, u32[]{:S(2)}) collective-permute-start(bf16[144,128]{1,0:T(8,128)(2,1)S(1)} %slice.62), channel_id=1, source_target_pairs={{0,2},{2,4},{4,6},{6,8},{8,10},{10,12},{12,14},{14,0},{1,3},{3,5},... | collective-permute-start | bytes 110600 | tf_op jit(solution)/shard_map/ppermute | solution.py:33
  226.1 4.7 %collective-permute-done.39 = bf16[144,128]{1,0:T(8,128)(2,1)S(1)} collective-permute-done((bf16[144,128]{1,0:T(8,128)(2,1)S(1)}, bf16[144,128]{1,0:T(8,128)(2,1)S(1)}, u32[]{:S(2)}, u32[]{:S(2)}) %collective-permute-start.39) | collective-permute-done | bytes 36896 | tf_op jit(solution)/shard_map/ppermute | solution.py:34
  232.3 7.1 %all-to-all-start.3 = ((bf16[16,18,640]{2,1,0:T(8,128)(2,1)}), bf16[16,18,640]{2,1,0:T(8,128)(2,1)S(1)}, u32[]{:S(2)}, u32[]{:S(2)}) async-start(bf16[16,18,640]{2,1,0:T(8,128)(2,1)} %reshape.112), calls=%async_computation.3 | async-start | bytes 983040 | tf_op jit(solution)/shard_map/all_to_all | solution.py:109
  241.8 13.3 %all-to-all-done.3 = bf16[16,18,640]{2,1,0:T(8,128)(2,1)S(1)} async-done(((bf16[16,18,640]{2,1,0:T(8,128)(2,1)}), bf16[16,18,640]{2,1,0:T(8,128)(2,1)S(1)}, u32[]{:S(2)}, u32[]{:S(2)}) %all-to-all-start.3) | async-done | bytes 368672 | tf_op jit(solution)/shard_map/all_to_all | solution.py:109
  255.1 5.5 %all-to-all-start.1 = ((bf16[16,18,640]{2,1,0:T(8,128)(2,1)}), bf16[16,18,640]{2,1,0:T(8,128)(2,1)S(1)}, u32[]{:S(2)}, u32[]{:S(2)}) async-start(bf16[16,18,640]{2,1,0:T(8,128)(2,1)} %reshape.108), calls=%async_computation.1 | async-start | bytes 983040 | tf_op jit(solution)/shard_map/all_to_all | solution.py:109
  263.6 10.4 %all-to-all-done.1 = bf16[16,18,640]{2,1,0:T(8,128)(2,1)S(1)} async-done(((bf16[16,18,640]{2,1,0:T(8,128)(2,1)}), bf16[16,18,640]{2,1,0:T(8,128)(2,1)S(1)}, u32[]{:S(2)}, u32[]{:S(2)}) %all-to-all-start.1) | async-done | bytes 368672 | tf_op jit(solution)/shard_map/all_to_all | solution.py:109
  (172 shorter events, 121.9 us)
Async XLA Ops:
  4.2 29.9 %all-to-all-start = ((bf16[16,18,640]{2,1,0:T(8,128)(2,1)}), bf16[16,18,640]{2,1,0:T(8,128)(2,1)S(1)}, u32[]{:S(2)}, u32[]{:S(2)}) async-start(bf16[16,18,640]{2,1,0:T(8,128)(2,1)} %reshape.104), calls=%async_computation | async-start | bytes 983040 | tf_op jit(solution)/shard_map/all_to_all | solution.py:109
  34.1 21.3 %all-to-all-start.2 = ((bf16[16,18,640]{2,1,0:T(8,128)(2,1)}), bf16[16,18,640]{2,1,0:T(8,128)(2,1)}, u32[]{:S(2)}, u32[]{:S(2)}) async-start(bf16[16,18,640]{2,1,0:T(8,128)(2,1)} %reshape.110), calls=%async_computation.2 | async-start | bytes 983040 | tf_op jit(solution)/shard_map/all_to_all | solution.py:109
  38.5 25.9 %collective-permute-start = (bf16[288,640]{1,0:T(8,128)(2,1)S(1)}, bf16[288,640]{1,0:T(8,128)(2,1)}, u32[]{:S(2)}, u32[]{:S(2)}) collective-permute-start(bf16[288,640]{1,0:T(8,128)(2,1)S(1)} %reshape.105), channel_id=1, source_target_pairs={{0,2},{2,4},{4,6},{6,8},{8,10},{10,12},{12,14},{14,0},{1,3},{3,5},... | collective-permute-start | bytes 1105928 | tf_op jit(solution)/shard_map/ppermute | solution.py:28
  44.3 84.0 %collective-permute-start.9 = (bf16[640,128]{1,0:T(8,128)(2,1)}, bf16[640,128]{1,0:T(8,128)(2,1)}, u32[]{:S(2)}, u32[]{:S(2)}) collective-permute-start(bf16[640,128]{1,0:T(8,128)(2,1)} %get-tuple-element.11), channel_id=1, source_target_pairs={{0,2},{2,4},{4,6},{6,8},{8,10},{10,12},{12,14},{14,0},{1,3},{3,5},... | collective-permute-start | bytes 491528 | tf_op jit(solution)/shard_map/ppermute | solution.py:53
  51.1 17.9 %collective-permute-start.1 = (bf16[288,640]{1,0:T(8,128)(2,1)S(1)}, bf16[288,640]{1,0:T(8,128)(2,1)}, u32[]{:S(2)}, u32[]{:S(2)}) collective-permute-start(bf16[288,640]{1,0:T(8,128)(2,1)S(1)} %reshape.105), channel_id=1, source_target_pairs={{0,14},{2,0},{4,2},{6,4},{8,6},{10,8},{12,10},{14,12},{1,15},{3,1}... | collective-permute-start | bytes 1105928 | tf_op jit(solution)/shard_map/ppermute | solution.py:29
  57.3 15.7 %collective-permute-start.25 = (bf16[288,640]{1,0:T(8,128)(2,1)}, bf16[288,640]{1,0:T(8,128)(2,1)S(1)}, u32[]{:S(2)}, u32[]{:S(2)}) collective-permute-start(bf16[288,640]{1,0:T(8,128)(2,1)} %reshape.111), channel_id=1, source_target_pairs={{0,14},{2,0},{4,2},{6,4},{8,6},{10,8},{12,10},{14,12},{1,15},{3,1}... | collective-permute-start | bytes 1105928 | tf_op jit(solution)/shard_map/ppermute | solution.py:29
  59.4 15.8 %collective-permute-start.24 = (bf16[288,640]{1,0:T(8,128)(2,1)}, bf16[288,640]{1,0:T(8,128)(2,1)S(1)}, u32[]{:S(2)}, u32[]{:S(2)}) collective-permute-start(bf16[288,640]{1,0:T(8,128)(2,1)} %reshape.111), channel_id=1, source_target_pairs={{0,2},{2,4},{4,6},{6,8},{8,10},{10,12},{12,14},{14,0},{1,3},{3,5},... | collective-permute-start | bytes 1105928 | tf_op jit(solution)/shard_map/ppermute | solution.py:28
  64.5 21.5 %collective-permute-start.2 = (bf16[288,640]{1,0:T(8,128)(2,1)}, bf16[288,640]{1,0:T(8,128)(2,1)S(1)}, u32[]{:S(2)}, u32[]{:S(2)}) collective-permute-start(bf16[288,640]{1,0:T(8,128)(2,1)} %collective-permute-done), channel_id=1, source_target_pairs={{0,2},{2,4},{4,6},{6,8},{8,10},{10,12},{12,14},{14,0},{1,3},{3,5},... | collective-permute-start | bytes 1105928 | tf_op jit(solution)/shard_map/ppermute | solution.py:28
  69.0 14.8 %collective-permute-start.3 = (bf16[288,640]{1,0:T(8,128)(2,1)}, bf16[288,640]{1,0:T(8,128)(2,1)S(1)}, u32[]{:S(2)}, u32[]{:S(2)}) collective-permute-start(bf16[288,640]{1,0:T(8,128)(2,1)} %collective-permute-done.1), channel_id=1, source_target_pairs={{0,14},{2,0},{4,2},{6,4},{8,6},{10,8},{12,10},{14,12},{1,15},{3,1}... | collective-permute-start | bytes 1105928 | tf_op jit(solution)/shard_map/ppermute | solution.py:29
  73.0 27.1 %collective-permute-start.27 = (bf16[288,640]{1,0:T(8,128)(2,1)S(1)}, bf16[288,640]{1,0:T(8,128)(2,1)S(1)}, u32[]{:S(2)}, u32[]{:S(2)}) collective-permute-start(bf16[288,640]{1,0:T(8,128)(2,1)S(1)} %collective-permute-done.25), channel_id=1, source_target_pairs={{0,14},{2,0},{4,2},{6,4},{8,6},{10,8},{12,10},{14,12},{1,15},{3,1}... | collective-permute-start | bytes 1105928 | tf_op jit(solution)/shard_map/ppermute | solution.py:29
  75.6 30.9 %collective-permute-start.26 = (bf16[288,640]{1,0:T(8,128)(2,1)S(1)}, bf16[288,640]{1,0:T(8,128)(2,1)S(1)}, u32[]{:S(2)}, u32[]{:S(2)}) collective-permute-start(bf16[288,640]{1,0:T(8,128)(2,1)S(1)} %collective-permute-done.24), channel_id=1, source_target_pairs={{0,2},{2,4},{4,6},{6,8},{8,10},{10,12},{12,14},{14,0},{1,3},{3,5},... | collective-permute-start | bytes 1105928 | tf_op jit(solution)/shard_map/ppermute | solution.py:28
  96.2 39.7 %collective-permute-start.11 = (bf16[640,128]{1,0:T(8,128)(2,1)S(1)}, bf16[640,128]{1,0:T(8,128)(2,1)S(1)}, u32[]{:S(2)}, u32[]{:S(2)}) collective-permute-start(bf16[640,128]{1,0:T(8,128)(2,1)S(1)} %copy-done.10), channel_id=1, source_target_pairs={{0,14},{2,0},{4,2},{6,4},{8,6},{10,8},{12,10},{14,12},{1,15},{3,1}... | collective-permute-start | bytes 491528 | tf_op jit(solution)/shard_map/ppermute | solution.py:53
  98.2 51.0 %collective-permute-start.15 = (bf16[640,128]{1,0:T(8,128)(2,1)S(1)}, bf16[640,128]{1,0:T(8,128)(2,1)S(1)}, u32[]{:S(2)}, u32[]{:S(2)}) collective-permute-start(bf16[640,128]{1,0:T(8,128)(2,1)S(1)} %copy-done.9), channel_id=1, source_target_pairs={{0,12},{2,14},{4,0},{6,2},{8,4},{10,6},{12,8},{14,10},{1,13},{3,15... | collective-permute-start | bytes 491528 | tf_op jit(solution)/shard_map/ppermute | solution.py:53
  100.1 56.5 %collective-permute-start.13 = (bf16[640,128]{1,0:T(8,128)(2,1)S(1)}, bf16[640,128]{1,0:T(8,128)(2,1)S(1)}, u32[]{:S(2)}, u32[]{:S(2)}) collective-permute-start(bf16[640,128]{1,0:T(8,128)(2,1)S(1)} %copy-done.8), channel_id=1, source_target_pairs={{0,4},{2,6},{4,8},{6,10},{8,12},{10,14},{12,0},{14,2},{1,5},{3,7},... | collective-permute-start | bytes 491528 | tf_op jit(solution)/shard_map/ppermute | solution.py:53
  128.3 95.5 %collective-permute-start.21 = (bf16[640,128]{1,0:T(8,128)(2,1)S(1)}, bf16[640,128]{1,0:T(8,128)(2,1)S(1)}, u32[]{:S(2)}, u32[]{:S(2)}) collective-permute-start(bf16[640,128]{1,0:T(8,128)(2,1)S(1)} %copy-done.6), channel_id=1, source_target_pairs={{0,8},{2,10},{4,12},{6,14},{8,0},{10,2},{12,4},{14,6},{1,9},{3,11}... | collective-permute-start | bytes 491528 | tf_op jit(solution)/shard_map/ppermute | solution.py:53
  135.9 45.1 %collective-permute-start.19 = (bf16[640,128]{1,0:T(8,128)(2,1)S(1)}, bf16[640,128]{1,0:T(8,128)(2,1)S(1)}, u32[]{:S(2)}, u32[]{:S(2)}) collective-permute-start(bf16[640,128]{1,0:T(8,128)(2,1)S(1)} %copy-done.7), channel_id=1, source_target_pairs={{0,10},{2,12},{4,14},{6,0},{8,2},{10,4},{12,6},{14,8},{1,11},{3,13... | collective-permute-start | bytes 491528 | tf_op jit(solution)/shard_map/ppermute | solution.py:53
  149.2 16.6 %collective-permute-start.29 = (bf16[288,640]{1,0:T(8,128)(2,1)S(1)}, bf16[288,640]{1,0:T(8,128)(2,1)S(1)}, u32[]{:S(2)}, u32[]{:S(2)}) collective-permute-start(bf16[288,640]{1,0:T(8,128)(2,1)S(1)} %collective-permute-done.27), channel_id=1, source_target_pairs={{0,14},{2,0},{4,2},{6,4},{8,6},{10,8},{12,10},{14,12},{1,15},{3,1}... | collective-permute-start | bytes 1105928 | tf_op jit(solution)/shard_map/ppermute | solution.py:29
  168.0 63.1 %collective-permute-start.17 = (bf16[640,128]{1,0:T(8,128)(2,1)S(1)}, bf16[640,128]{1,0:T(8,128)(2,1)S(1)}, u32[]{:S(2)}, u32[]{:S(2)}) collective-permute-start(bf16[640,128]{1,0:T(8,128)(2,1)S(1)} %copy-done.5), channel_id=1, source_target_pairs={{0,6},{2,8},{4,10},{6,12},{8,14},{10,0},{12,2},{14,4},{1,7},{3,9},... | collective-permute-start | bytes 491528 | tf_op jit(solution)/shard_map/ppermute | solution.py:53
  181.0 58.3 %collective-permute-start.20 = (bf16[144,128]{1,0:T(8,128)(2,1)}, bf16[144,128]{1,0:T(8,128)(2,1)}, u32[]{:S(2)}, u32[]{:S(2)}) collective-permute-start(bf16[144,128]{1,0:T(8,128)(2,1)} %slice.56), channel_id=1, source_target_pairs={{0,2},{2,4},{4,6},{6,8},{8,10},{10,12},{12,14},{14,0},{1,3},{3,5},... | collective-permute-start | bytes 110600 | tf_op jit(solution)/shard_map/ppermute | solution.py:33
  193.0 16.0 %collective-permute-start.34 = (bf16[288,128]{1,0:T(8,128)(2,1)S(1)}, bf16[288,128]{1,0:T(8,128)(2,1)S(1)}, u32[]{:S(2)}, u32[]{:S(2)}) collective-permute-start(bf16[288,128]{1,0:T(8,128)(2,1)S(1)} %collective-permute-done.32), channel_id=1, source_target_pairs={{0,2},{2,4},{4,6},{6,8},{8,10},{10,12},{12,14},{14,0},{1,3},{3,5},... | collective-permute-start | bytes 221192 | tf_op jit(solution)/shard_map/ppermute | solution.py:28
  216.1 24.3 %collective-permute-start.22 = (bf16[144,128]{1,0:T(8,128)(2,1)}, bf16[144,128]{1,0:T(8,128)(2,1)S(1)}, u32[]{:S(2)}, u32[]{:S(2)}) collective-permute-start(bf16[144,128]{1,0:T(8,128)(2,1)} %slice.57), channel_id=1, source_target_pairs={{0,14},{2,0},{4,2},{6,4},{8,6},{10,8},{12,10},{14,12},{1,15},{3,1}... | collective-permute-start | bytes 110600 | tf_op jit(solution)/shard_map/ppermute | solution.py:34
  232.3 22.8 %all-to-all-start.3 = ((bf16[16,18,640]{2,1,0:T(8,128)(2,1)}), bf16[16,18,640]{2,1,0:T(8,128)(2,1)S(1)}, u32[]{:S(2)}, u32[]{:S(2)}) async-start(bf16[16,18,640]{2,1,0:T(8,128)(2,1)} %reshape.112), calls=%async_computation.3 | async-start | bytes 983040 | tf_op jit(solution)/shard_map/all_to_all | solution.py:109
  255.1 18.9 %all-to-all-start.1 = ((bf16[16,18,640]{2,1,0:T(8,128)(2,1)}), bf16[16,18,640]{2,1,0:T(8,128)(2,1)S(1)}, u32[]{:S(2)}, u32[]{:S(2)}) async-start(bf16[16,18,640]{2,1,0:T(8,128)(2,1)} %reshape.108), calls=%async_computation.1 | async-start | bytes 983040 | tf_op jit(solution)/shard_map/all_to_all | solution.py:109
  261.6 13.1 %collective-permute-start.40 = (bf16[288,640]{1,0:T(8,128)(2,1)S(1)}, bf16[288,640]{1,0:T(8,128)(2,1)S(1)}, u32[]{:S(2)}, u32[]{:S(2)}) collective-permute-start(bf16[288,640]{1,0:T(8,128)(2,1)S(1)} %reshape.113), channel_id=1, source_target_pairs={{0,16},{16,0},{1,17},{17,1},{2,18},{18,2},{3,19},{19,3},{4,20},{20... | collective-permute-start | bytes 1105928 | tf_op jit(solution)/shard_map/ppermute | solution.py:114
  (33 other events, 422.4 us)

commit v2 on v1

v2 whole, which is shorter than its diff:
```python
import jax
import jax.numpy as jnp
from jax import lax
from jax.sharding import Mesh
from jax.sharding import PartitionSpec as P


EXPERT = ("expert_0", "expert_1", "expert_2")
DP_EXPERT = ("dp", "expert_0", "expert_1", "expert_2")


def dot(a, b, dims=((1,), (0,))):
    return lax.dot_general(a, b, (dims, ((), ())), preferred_element_type=jnp.float32)


def shift(size, step):
    return [(i, (i + step) % size) for i in range(size)]


def ring(x, size, use):
    rows = x.shape[0]
    use(x, 0, 0)
    up = down = x
    for step in range(1, size // 2):
        up = lax.ppermute(up, "tensor", shift(size, 1))
        down = lax.ppermute(down, "tensor", shift(size, -1))
        use(up, -step, 0)
        use(down, step, 0)
    half = rows // 2
    use(lax.ppermute(up[:half], "tensor", shift(size, 1)), size // 2, 0)
    use(lax.ppermute(down[half:], "tensor", shift(size, -1)), size // 2, half)


def down_rows(down_weight, size, part, hidden):
    me, pair = lax.axis_index("tensor"), lax.axis_index("dp")
    blocks = down_weight.reshape(size, part, hidden)
    steps = ((1, 2, -3), (-1, -2, 3))
    got = []
    for first, second in zip(*steps):
        step = jnp.where(pair == 0, first, second)
        block = lax.dynamic_index_in_dim(blocks, lax.rem(me + step + size, size), 0, keepdims=False)
        perm = [(2 * i, 2 * ((i + first) % size)) for i in range(size)]
        perm += [(2 * i + 1, 2 * ((i + second) % size) + 1) for i in range(size)]
        got.append(lax.ppermute(block, ("tensor", "dp"), perm))
    half = part // 2
    far = lax.rem(me + size // 2, size)
    block = lax.dynamic_slice(blocks, (far, pair * half, 0), (1, half, hidden))[0]
    got.append(lax.ppermute(block, "tensor", shift(size, size // 2)))
    got = jnp.concatenate(got, axis=0)
    other = lax.ppermute(got, "dp", [(0, 1), (1, 0)])
    a = jnp.where(pair == 0, got, other)
    b = jnp.where(pair == 0, other, got)
    own = lax.dynamic_index_in_dim(blocks, me, 0, keepdims=False)
    piece = lambda x, i: x[i * part : (i + 1) * part]
    far = jnp.concatenate([a[3 * part :], b[3 * part :]], axis=0)
    near = [own, piece(b, 0), piece(b, 1), piece(a, 2), far, piece(b, 2), piece(a, 1), piece(a, 0)]
    twice = jnp.stack(near + near)
    return lax.dynamic_slice_in_dim(twice, lax.rem(size - me, size), size, 0)


def local(tokens, routes, gates, gate_up, down_weight, old_map, new_map):
    experts = lax.axis_size(EXPERT)
    size = lax.axis_size("tensor")
    me = lax.axis_index("tensor")
    tok_rows, part = tokens.shape
    picks = routes.shape[1]
    capacity = (tok_rows * picks + experts - 1) // experts
    hidden = down_weight.shape[2]
    rows = experts * capacity
    bf16 = jnp.bfloat16

    slot_ids = jnp.arange(experts, dtype=jnp.int32)
    holder = jnp.sum(jnp.where(new_map[:, None] == old_map[None, :], slot_ids[None, :], 0), axis=1)
    target = jnp.sum(
        jnp.where(routes[:, :, None] == slot_ids[None, None, :], holder[None, None, :], 0), axis=2
    )
    hits = target[:, :, None] == slot_ids[None, None, :]
    member = jnp.any(hits, axis=1)
    weight = jnp.sum(jnp.where(hits, gates[:, :, None], 0.0), axis=1)
    ones = jnp.tril(jnp.ones((tok_rows, tok_rows), bf16), -1)
    position = dot(ones, member.astype(bf16)).astype(jnp.int32)
    place = jnp.where(member, position, -1)
    cap_ids = jnp.arange(capacity, dtype=jnp.int32)
    matches = place[:, :, None] == cap_ids[None, None, :]
    assign = matches.astype(bf16).reshape(tok_rows, rows)
    combine = jnp.where(matches, weight[:, :, None], 0.0).reshape(tok_rows, rows)
    outgoing = dot(assign, tokens, ((0,), (0,))).astype(bf16)

    def exchange(x):
        x = x.reshape(experts, capacity // 2, 2, part)
        x = lax.all_to_all(x, EXPERT, 0, 0, tiled=True)
        return x.reshape(rows, part)

    arrived = exchange(outgoing)
    down_mine = down_rows(down_weight, size, part, hidden)

    weight_in = gate_up.reshape(size, part, 2 * hidden)

    def projected(x):
        pieces = []

        def use(block, distance, start):
            w = lax.dynamic_index_in_dim(weight_in, lax.rem(me + distance + size, size), 0, keepdims=False)
            pieces.append(dot(block, w))

        ring(x, size, use)
        total = sum(pieces[:-2]) + jnp.concatenate(pieces[-2:], axis=0)
        return (jax.nn.silu(total[:, :hidden]) * total[:, hidden:]).astype(bf16)

    half = rows // 2
    act_a, act_b = projected(arrived[:half]), projected(arrived[half:])
    all_a = lax.all_to_all(jnp.broadcast_to(act_a[None], (size, half, hidden)), "tensor", 0, 0, tiled=True)
    all_b = lax.all_gather(act_b, "tensor")

    def outputs(act):
        return dot(act, down_mine, ((0, 2), (0, 2))).astype(bf16)

    expert_out = jnp.concatenate([outputs(all_a), outputs(all_b)], axis=0)
    returned = exchange(expert_out)
    mixed = jnp.dot(
        combine,
        returned.astype(jnp.float32),
        precision=lax.Precision.HIGHEST,
        preferred_element_type=jnp.float32,
    )
    return mixed.astype(bf16)


def solution(mesh):
    split = Mesh(
        mesh.devices.reshape(4, 4, 2, mesh.shape["tensor"], mesh.shape["dp"]),
        ("expert_0", "expert_1", "expert_2", "tensor", "dp"),
    )
    in_specs = (
        P(DP_EXPERT, "tensor"),
        P(DP_EXPERT, None),
        P(DP_EXPERT, None),
        P(EXPERT, None, None, "tensor"),
        P(EXPERT, None, "tensor"),
        P(),
        P(),
    )
    return jax.shard_map(local, mesh=split, in_specs=in_specs, out_specs=P(DP_EXPERT, "tensor"), check_vma=False)
```

time: 278 us -> 222 us (0.80)
  the two profiles are of different devices: /device:TPU:88 before, /device:TPU:24 now
where the time goes in v2:
time: 222 us; the launch traced here: 220 us
  starting transfers between devices  104 us (47%)
  waiting for transfers between devices  39.7 us (18%)
  blocking collectives  28.3 us (13%)
  local copies, waits for them, and re-layouts  28.2 us (13%)
  matrix products  15.4 us (7%)
  other arithmetic  4.56 us (2%)
    all_to_all x2, waiting for transfers between devices, exchange(): x = lax.all_to_all(x, EXPERT, 0, 0, tiled=True)  30.2 us
    ppermute x6, starting transfers between devices, ring(): up = lax.ppermute(up, 'tensor', shift(size, 1))  29.9 us
    all_gather x1, blocking collectives, local(): all_b = lax.all_gather(act_b, 'tensor')  28.3 us
    all_to_all x2, starting transfers between devices, exchange(): x = lax.all_to_all(x, EXPERT, 0, 0, tiled=True)  18.1 us
    dot_general x22, matrix products, dot(): lax.dot_general(a, b, (dims, ((), ())), preferred_element_type=jnp.float32)  14.1 us
    ppermute x6, starting transfers between devices, ring(): down = lax.ppermute(down, 'tensor', shift(size, -1))  12.5 us
    ppermute x3, starting transfers between devices, down_rows(): got.append(lax.ppermute(block, ('tensor', 'dp'), perm))  11.3 us
    unnamed x23, local copies, waits for them, and re-layouts  11.1 us
  transfers between devices with their start and end apart: 24, of which 5 were waited for; matrix products, arithmetic and copies ran while one was open for 18% of the time, Pallas kernels for 0%

profile of v2, /device:TPU:24, one launch (start us, length us, event | category | flops | bytes accessed | tf_op | source)
XLA Modules:
  0.0 220.4 jit_solution(4226731346368238840)
XLA Ops:
  0.9 5.0 %collective-permute-start.11 = (bf16[320,128]{1,0:T(8,128)(2,1)S(1)}, bf16[320,128]{1,0:T(8,128)(2,1)S(1)}, u32[]{:S(2)}, u32[]{:S(2)}) collective-permute-start(bf16[320,128]{1,0:T(8,128)(2,1)S(1)} %dynamic-slice_bitcast_fusion.3), channel_id=1, source_target_pairs={{0,8},{2,10},{4,12},{6,14},{8,0},{10,2},{12,4},{14,6},{1,9},{3,11}... | collective-permute-start | bytes 245768 | tf_op jit(solution)/shard_map/ppermute | solution.py:48
  7.9 4.8 %collective-permute-start.10 = (bf16[640,128]{1,0:T(8,128)(2,1)S(1)}, bf16[640,128]{1,0:T(8,128)(2,1)S(1)}, u32[]{:S(2)}, u32[]{:S(2)}) collective-permute-start(bf16[640,128]{1,0:T(8,128)(2,1)S(1)} %get-tuple-element.5), channel_id=1, source_target_pairs={{0,10},{2,12},{4,14},{6,0},{8,2},{10,4},{12,6},{14,8},{1,7},{3,9},... | collective-permute-start | bytes 491528 | tf_op jit(solution)/shard_map/ppermute | solution.py:44
  12.7 3.9 %collective-permute-start.9 = (bf16[640,128]{1,0:T(8,128)(2,1)S(1)}, bf16[640,128]{1,0:T(8,128)(2,1)S(1)}, u32[]{:S(2)}, u32[]{:S(2)}) collective-permute-start(bf16[640,128]{1,0:T(8,128)(2,1)S(1)} %get-tuple-element.7), channel_id=1, source_target_pairs={{0,4},{2,6},{4,8},{6,10},{8,12},{10,14},{12,0},{14,2},{1,13},{3,15... | collective-permute-start | bytes 491528 | tf_op jit(solution)/shard_map/ppermute | solution.py:44
  16.6 2.6 %collective-permute-start.8 = (bf16[640,128]{1,0:T(8,128)(2,1)S(1)}, bf16[640,128]{1,0:T(8,128)(2,1)S(1)}, u32[]{:S(2)}, u32[]{:S(2)}) collective-permute-start(bf16[640,128]{1,0:T(8,128)(2,1)S(1)} %get-tuple-element.8), channel_id=1, source_target_pairs={{0,2},{2,4},{4,6},{6,8},{8,10},{10,12},{12,14},{14,0},{1,15},{3,1}... | collective-permute-start | bytes 491528 | tf_op jit(solution)/shard_map/ppermute | solution.py:44
  21.0 7.3 %collective-permute-done.8 = bf16[640,128]{1,0:T(8,128)(2,1)S(1)} collective-permute-done((bf16[640,128]{1,0:T(8,128)(2,1)S(1)}, bf16[640,128]{1,0:T(8,128)(2,1)S(1)}, u32[]{:S(2)}, u32[]{:S(2)}) %collective-permute-start.8) | collective-permute-done | bytes 163872 | tf_op jit(solution)/shard_map/ppermute | solution.py:44
  31.0 3.0 %collective-permute-start.12 = (bf16[2240,128]{1,0:T(8,128)(2,1)}, bf16[2240,128]{1,0:T(8,128)(2,1)}, u32[]{:S(2)}, u32[]{:S(2)}) collective-permute-start(bf16[2240,128]{1,0:T(8,128)(2,1)} %constant_dynamic-update-slice_fusion), channel_id=1, source_target_pairs={{0,1},{1,0},{2,3},{3,2},{4,5},{5,4},{6,7},{7,6},{8,9},{9,8},{10,11... | collective-permute-start | bytes 1720328 | tf_op jit(solution)/shard_map/ppermute | solution.py:50
  35.8 12.3 %all-to-all-start = ((bf16[32,9,2,640]{3,2,1,0:T(2,128)(2,1)}), bf16[32,9,2,640]{3,2,1,0:T(2,128)(2,1)S(1)}, u32[]{:S(2)}, u32[]{:S(2)}) async-start(bf16[32,9,2,640]{3,2,1,0:T(2,128)(2,1)} %reshape.67), calls=%async_computation | async-start | bytes 1474560 | tf_op jit(solution)/shard_map/all_to_all | solution.py:91
  48.1 4.2 %reshape.68 = bf16[8,640,256]{2,1,0:T(8,128)(2,1)S(1)} reshape(bf16[1,5120,2,128]{3,2,1,0:T(2,128)(2,1)} %param.10) | data formatting | bytes 5242880 | tf_op jit(solution)/shard_map/reshape | solution.py:97
  64.8 7.1 %all-to-all-done = bf16[32,9,2,640]{3,2,1,0:T(2,128)(2,1)S(1)} async-done(((bf16[32,9,2,640]{3,2,1,0:T(2,128)(2,1)}), bf16[32,9,2,640]{3,2,1,0:T(2,128)(2,1)S(1)}, u32[]{:S(2)}, u32[]{:S(2)}) %all-to-all-start) | async-done | bytes 737312 | tf_op jit(solution)/shard_map/all_to_all | solution.py:91
  74.3 2.9 %collective-permute-start.14 = (bf16[288,640]{1,0:T(8,128)(2,1)S(1)}, bf16[288,640]{1,0:T(8,128)(2,1)}, u32[]{:S(2)}, u32[]{:S(2)}) collective-permute-start(bf16[288,640]{1,0:T(8,128)(2,1)S(1)} %slice.75), channel_id=1, source_target_pairs={{0,14},{2,0},{4,2},{6,4},{8,6},{10,8},{12,10},{14,12},{1,15},{3,1}... | collective-permute-start | bytes 1105928 | tf_op jit(solution)/shard_map/ppermute | solution.py:26
  77.2 4.2 %collective-permute-start.13 = (bf16[288,640]{1,0:T(8,128)(2,1)S(1)}, bf16[288,640]{1,0:T(8,128)(2,1)}, u32[]{:S(2)}, u32[]{:S(2)}) collective-permute-start(bf16[288,640]{1,0:T(8,128)(2,1)S(1)} %slice.75), channel_id=1, source_target_pairs={{0,2},{2,4},{4,6},{6,8},{8,10},{10,12},{12,14},{14,0},{1,3},{3,5},... | collective-permute-start | bytes 1105928 | tf_op jit(solution)/shard_map/ppermute | solution.py:25
  82.5 1.9 collective-permute-start.1
  84.5 5.1 %collective-permute-start = (bf16[288,640]{1,0:T(8,128)(2,1)S(1)}, bf16[288,640]{1,0:T(8,128)(2,1)S(1)}, u32[]{:S(2)}, u32[]{:S(2)}) collective-permute-start(bf16[288,640]{1,0:T(8,128)(2,1)S(1)} %slice.61), channel_id=1, source_target_pairs={{0,2},{2,4},{4,6},{6,8},{8,10},{10,12},{12,14},{14,0},{1,3},{3,5},... | collective-permute-start | bytes 1105928 | tf_op jit(solution)/shard_map/ppermute | solution.py:25
  92.1 5.1 %collective-permute-start.15 = (bf16[288,640]{1,0:T(8,128)(2,1)}, bf16[288,640]{1,0:T(8,128)(2,1)S(1)}, u32[]{:S(2)}, u32[]{:S(2)}) collective-permute-start(bf16[288,640]{1,0:T(8,128)(2,1)} %collective-permute-done.13), channel_id=1, source_target_pairs={{0,2},{2,4},{4,6},{6,8},{8,10},{10,12},{12,14},{14,0},{1,3},{3,5},... | collective-permute-start | bytes 1105928 | tf_op jit(solution)/shard_map/ppermute | solution.py:25
  99.2 5.1 %collective-permute-start.2 = (bf16[288,640]{1,0:T(8,128)(2,1)S(1)}, bf16[288,640]{1,0:T(8,128)(2,1)S(1)}, u32[]{:S(2)}, u32[]{:S(2)}) collective-permute-start(bf16[288,640]{1,0:T(8,128)(2,1)S(1)} %collective-permute-done), channel_id=1, source_target_pairs={{0,2},{2,4},{4,6},{6,8},{8,10},{10,12},{12,14},{14,0},{1,3},{3,5},... | collective-permute-start | bytes 1105928 | tf_op jit(solution)/shard_map/ppermute | solution.py:25
  109.5 5.1 %collective-permute-start.17 = (bf16[288,640]{1,0:T(8,128)(2,1)S(1)}, bf16[288,640]{1,0:T(8,128)(2,1)S(1)}, u32[]{:S(2)}, u32[]{:S(2)}) collective-permute-start(bf16[288,640]{1,0:T(8,128)(2,1)S(1)} %collective-permute-done.15), channel_id=1, source_target_pairs={{0,2},{2,4},{4,6},{6,8},{8,10},{10,12},{12,14},{14,0},{1,3},{3,5},... | collective-permute-start | bytes 1105928 | tf_op jit(solution)/shard_map/ppermute | solution.py:25
  116.6 5.1 %collective-permute-start.4 = (bf16[288,640]{1,0:T(8,128)(2,1)S(1)}, bf16[288,640]{1,0:T(8,128)(2,1)S(1)}, u32[]{:S(2)}, u32[]{:S(2)}) collective-permute-start(bf16[288,640]{1,0:T(8,128)(2,1)S(1)} %collective-permute-done.2), channel_id=1, source_target_pairs={{0,2},{2,4},{4,6},{6,8},{8,10},{10,12},{12,14},{14,0},{1,3},{3,5},... | collective-permute-start | bytes 1105928 | tf_op jit(solution)/shard_map/ppermute | solution.py:25
  127.0 5.1 %collective-permute-start.19 = (bf16[144,640]{1,0:T(8,128)(2,1)}, bf16[144,640]{1,0:T(8,128)(2,1)}, u32[]{:S(2)}, u32[]{:S(2)}) collective-permute-start(bf16[144,640]{1,0:T(8,128)(2,1)} %slice.94), channel_id=1, source_target_pairs={{0,2},{2,4},{4,6},{6,8},{8,10},{10,12},{12,14},{14,0},{1,3},{3,5},... | collective-permute-start | bytes 552968 | tf_op jit(solution)/shard_map/ppermute | solution.py:30
  134.1 5.1 %collective-permute-start.6 = (bf16[144,640]{1,0:T(8,128)(2,1)S(1)}, bf16[144,640]{1,0:T(8,128)(2,1)S(1)}, u32[]{:S(2)}, u32[]{:S(2)}) collective-permute-start(bf16[144,640]{1,0:T(8,128)(2,1)S(1)} %slice.81), channel_id=1, source_target_pairs={{0,2},{2,4},{4,6},{6,8},{8,10},{10,12},{12,14},{14,0},{1,3},{3,5},... | collective-permute-start | bytes 552968 | tf_op jit(solution)/shard_map/ppermute | solution.py:30
  143.8 9.7 %all-to-all-start.1 = ((bf16[8,288,128]{2,1,0:T(8,128)(2,1)}), bf16[8,288,128]{2,1,0:T(8,128)(2,1)}, u32[]{:S(2)}, u32[]{:S(2)}) async-start(bf16[8,288,128]{2,1,0:T(8,128)(2,1)} %broadcast_in_dim.88), calls=%async_computation.1 | async-start | bytes 1179648 | tf_op jit(solution)/shard_map/all_to_all | solution.py:112
  157.4 28.3 %all-gather = bf16[2304,128]{1,0:T(8,128)(2,1)S(1)} all-gather(bf16[288,128]{1,0:T(8,128)(2,1)S(1)} %fusion.59), channel_id=2, replica_groups=mesh['expert_0'=4,'expert_1'=4,'expert_2'=2,'tensor'=8,'dp'=2] {'tensor'}, dimensions={0}, use_global_device_ids=true | all-gather | bytes 663552 | tf_op jit(solution)/shard_map/all_gather | solution.py:113
  186.3 2.2 fusion
  189.7 5.9 %all-to-all-start.2 = ((bf16[32,9,2,640]{3,2,1,0:T(2,128)(2,1)}), bf16[32,9,2,640]{3,2,1,0:T(2,128)(2,1)S(1)}, u32[]{:S(2)}, u32[]{:S(2)}) async-start(bf16[32,9,2,640]{3,2,1,0:T(2,128)(2,1)} %reshape.70), calls=%async_computation.2 | async-start | bytes 1474560 | tf_op jit(solution)/shard_map/all_to_all | solution.py:91
  195.8 23.1 %all-to-all-done.2 = bf16[32,9,2,640]{3,2,1,0:T(2,128)(2,1)S(1)} async-done(((bf16[32,9,2,640]{3,2,1,0:T(2,128)(2,1)}), bf16[32,9,2,640]{3,2,1,0:T(2,128)(2,1)S(1)}, u32[]{:S(2)}, u32[]{:S(2)}) %all-to-all-start.2) | async-done | bytes 737312 | tf_op jit(solution)/shard_map/all_to_all | solution.py:91
  (106 shorter events, 55.6 us)
Async XLA Ops:
  0.9 29.4 %collective-permute-start.11 = (bf16[320,128]{1,0:T(8,128)(2,1)S(1)}, bf16[320,128]{1,0:T(8,128)(2,1)S(1)}, u32[]{:S(2)}, u32[]{:S(2)}) collective-permute-start(bf16[320,128]{1,0:T(8,128)(2,1)S(1)} %dynamic-slice_bitcast_fusion.3), channel_id=1, source_target_pairs={{0,8},{2,10},{4,12},{6,14},{8,0},{10,2},{12,4},{14,6},{1,9},{3,11}... | collective-permute-start | bytes 245768 | tf_op jit(solution)/shard_map/ppermute | solution.py:48
  7.9 21.8 %collective-permute-start.10 = (bf16[640,128]{1,0:T(8,128)(2,1)S(1)}, bf16[640,128]{1,0:T(8,128)(2,1)S(1)}, u32[]{:S(2)}, u32[]{:S(2)}) collective-permute-start(bf16[640,128]{1,0:T(8,128)(2,1)S(1)} %get-tuple-element.5), channel_id=1, source_target_pairs={{0,10},{2,12},{4,14},{6,0},{8,2},{10,4},{12,6},{14,8},{1,7},{3,9},... | collective-permute-start | bytes 491528 | tf_op jit(solution)/shard_map/ppermute | solution.py:44
  12.7 16.3 %collective-permute-start.9 = (bf16[640,128]{1,0:T(8,128)(2,1)S(1)}, bf16[640,128]{1,0:T(8,128)(2,1)S(1)}, u32[]{:S(2)}, u32[]{:S(2)}) collective-permute-start(bf16[640,128]{1,0:T(8,128)(2,1)S(1)} %get-tuple-element.7), channel_id=1, source_target_pairs={{0,4},{2,6},{4,8},{6,10},{8,12},{10,14},{12,0},{14,2},{1,13},{3,15... | collective-permute-start | bytes 491528 | tf_op jit(solution)/shard_map/ppermute | solution.py:44
  16.6 11.7 %collective-permute-start.8 = (bf16[640,128]{1,0:T(8,128)(2,1)S(1)}, bf16[640,128]{1,0:T(8,128)(2,1)S(1)}, u32[]{:S(2)}, u32[]{:S(2)}) collective-permute-start(bf16[640,128]{1,0:T(8,128)(2,1)S(1)} %get-tuple-element.8), channel_id=1, source_target_pairs={{0,2},{2,4},{4,6},{6,8},{8,10},{10,12},{12,14},{14,0},{1,15},{3,1}... | collective-permute-start | bytes 491528 | tf_op jit(solution)/shard_map/ppermute | solution.py:44
  31.0 21.4 %collective-permute-start.12 = (bf16[2240,128]{1,0:T(8,128)(2,1)}, bf16[2240,128]{1,0:T(8,128)(2,1)}, u32[]{:S(2)}, u32[]{:S(2)}) collective-permute-start(bf16[2240,128]{1,0:T(8,128)(2,1)} %constant_dynamic-update-slice_fusion), channel_id=1, source_target_pairs={{0,1},{1,0},{2,3},{3,2},{4,5},{5,4},{6,7},{7,6},{8,9},{9,8},{10,11... | collective-permute-start | bytes 1720328 | tf_op jit(solution)/shard_map/ppermute | solution.py:50
  35.8 36.0 %all-to-all-start = ((bf16[32,9,2,640]{3,2,1,0:T(2,128)(2,1)}), bf16[32,9,2,640]{3,2,1,0:T(2,128)(2,1)S(1)}, u32[]{:S(2)}, u32[]{:S(2)}) async-start(bf16[32,9,2,640]{3,2,1,0:T(2,128)(2,1)} %reshape.67), calls=%async_computation | async-start | bytes 1474560 | tf_op jit(solution)/shard_map/all_to_all | solution.py:91
  74.3 15.9 %collective-permute-start.14 = (bf16[288,640]{1,0:T(8,128)(2,1)S(1)}, bf16[288,640]{1,0:T(8,128)(2,1)}, u32[]{:S(2)}, u32[]{:S(2)}) collective-permute-start(bf16[288,640]{1,0:T(8,128)(2,1)S(1)} %slice.75), channel_id=1, source_target_pairs={{0,14},{2,0},{4,2},{6,4},{8,6},{10,8},{12,10},{14,12},{1,15},{3,1}... | collective-permute-start | bytes 1105928 | tf_op jit(solution)/shard_map/ppermute | solution.py:26
  77.2 14.9 %collective-permute-start.13 = (bf16[288,640]{1,0:T(8,128)(2,1)S(1)}, bf16[288,640]{1,0:T(8,128)(2,1)}, u32[]{:S(2)}, u32[]{:S(2)}) collective-permute-start(bf16[288,640]{1,0:T(8,128)(2,1)S(1)} %slice.75), channel_id=1, source_target_pairs={{0,2},{2,4},{4,6},{6,8},{8,10},{10,12},{12,14},{14,0},{1,3},{3,5},... | collective-permute-start | bytes 1105928 | tf_op jit(solution)/shard_map/ppermute | solution.py:25
  82.5 14.8 %collective-permute-start.1 = (bf16[288,640]{1,0:T(8,128)(2,1)S(1)}, bf16[288,640]{1,0:T(8,128)(2,1)S(1)}, u32[]{:S(2)}, u32[]{:S(2)}) collective-permute-start(bf16[288,640]{1,0:T(8,128)(2,1)S(1)} %slice.61), channel_id=1, source_target_pairs={{0,14},{2,0},{4,2},{6,4},{8,6},{10,8},{12,10},{14,12},{1,15},{3,1}... | collective-permute-start | bytes 1105928 | tf_op jit(solution)/shard_map/ppermute | solution.py:26
  84.5 14.8 %collective-permute-start = (bf16[288,640]{1,0:T(8,128)(2,1)S(1)}, bf16[288,640]{1,0:T(8,128)(2,1)S(1)}, u32[]{:S(2)}, u32[]{:S(2)}) collective-permute-start(bf16[288,640]{1,0:T(8,128)(2,1)S(1)} %slice.61), channel_id=1, source_target_pairs={{0,2},{2,4},{4,6},{6,8},{8,10},{10,12},{12,14},{14,0},{1,3},{3,5},... | collective-permute-start | bytes 1105928 | tf_op jit(solution)/shard_map/ppermute | solution.py:25
  90.2 17.3 %collective-permute-start.16 = (bf16[288,640]{1,0:T(8,128)(2,1)}, bf16[288,640]{1,0:T(8,128)(2,1)S(1)}, u32[]{:S(2)}, u32[]{:S(2)}) collective-permute-start(bf16[288,640]{1,0:T(8,128)(2,1)} %collective-permute-done.14), channel_id=1, source_target_pairs={{0,14},{2,0},{4,2},{6,4},{8,6},{10,8},{12,10},{14,12},{1,15},{3,1}... | collective-permute-start | bytes 1105928 | tf_op jit(solution)/shard_map/ppermute | solution.py:26
  92.1 17.3 %collective-permute-start.15 = (bf16[288,640]{1,0:T(8,128)(2,1)}, bf16[288,640]{1,0:T(8,128)(2,1)S(1)}, u32[]{:S(2)}, u32[]{:S(2)}) collective-permute-start(bf16[288,640]{1,0:T(8,128)(2,1)} %collective-permute-done.13), channel_id=1, source_target_pairs={{0,2},{2,4},{4,6},{6,8},{8,10},{10,12},{12,14},{14,0},{1,3},{3,5},... | collective-permute-start | bytes 1105928 | tf_op jit(solution)/shard_map/ppermute | solution.py:25
  97.3 17.3 %collective-permute-start.3 = (bf16[288,640]{1,0:T(8,128)(2,1)S(1)}, bf16[288,640]{1,0:T(8,128)(2,1)S(1)}, u32[]{:S(2)}, u32[]{:S(2)}) collective-permute-start(bf16[288,640]{1,0:T(8,128)(2,1)S(1)} %collective-permute-done.1), channel_id=1, source_target_pairs={{0,14},{2,0},{4,2},{6,4},{8,6},{10,8},{12,10},{14,12},{1,15},{3,1}... | collective-permute-start | bytes 1105928 | tf_op jit(solution)/shard_map/ppermute | solution.py:26
  99.2 17.3 %collective-permute-start.2 = (bf16[288,640]{1,0:T(8,128)(2,1)S(1)}, bf16[288,640]{1,0:T(8,128)(2,1)S(1)}, u32[]{:S(2)}, u32[]{:S(2)}) collective-permute-start(bf16[288,640]{1,0:T(8,128)(2,1)S(1)} %collective-permute-done), channel_id=1, source_target_pairs={{0,2},{2,4},{4,6},{6,8},{8,10},{10,12},{12,14},{14,0},{1,3},{3,5},... | collective-permute-start | bytes 1105928 | tf_op jit(solution)/shard_map/ppermute | solution.py:25
  107.5 16.1 %collective-permute-start.18 = (bf16[288,640]{1,0:T(8,128)(2,1)S(1)}, bf16[288,640]{1,0:T(8,128)(2,1)S(1)}, u32[]{:S(2)}, u32[]{:S(2)}) collective-permute-start(bf16[288,640]{1,0:T(8,128)(2,1)S(1)} %collective-permute-done.16), channel_id=1, source_target_pairs={{0,14},{2,0},{4,2},{6,4},{8,6},{10,8},{12,10},{14,12},{1,15},{3,1}... | collective-permute-start | bytes 1105928 | tf_op jit(solution)/shard_map/ppermute | solution.py:26
  109.5 16.8 %collective-permute-start.17 = (bf16[288,640]{1,0:T(8,128)(2,1)S(1)}, bf16[288,640]{1,0:T(8,128)(2,1)S(1)}, u32[]{:S(2)}, u32[]{:S(2)}) collective-permute-start(bf16[288,640]{1,0:T(8,128)(2,1)S(1)} %collective-permute-done.15), channel_id=1, source_target_pairs={{0,2},{2,4},{4,6},{6,8},{8,10},{10,12},{12,14},{14,0},{1,3},{3,5},... | collective-permute-start | bytes 1105928 | tf_op jit(solution)/shard_map/ppermute | solution.py:25
  114.6 17.5 %collective-permute-start.5 = (bf16[288,640]{1,0:T(8,128)(2,1)S(1)}, bf16[288,640]{1,0:T(8,128)(2,1)S(1)}, u32[]{:S(2)}, u32[]{:S(2)}) collective-permute-start(bf16[288,640]{1,0:T(8,128)(2,1)S(1)} %collective-permute-done.3), channel_id=1, source_target_pairs={{0,14},{2,0},{4,2},{6,4},{8,6},{10,8},{12,10},{14,12},{1,15},{3,1}... | collective-permute-start | bytes 1105928 | tf_op jit(solution)/shard_map/ppermute | solution.py:26
  116.6 17.5 %collective-permute-start.4 = (bf16[288,640]{1,0:T(8,128)(2,1)S(1)}, bf16[288,640]{1,0:T(8,128)(2,1)S(1)}, u32[]{:S(2)}, u32[]{:S(2)}) collective-permute-start(bf16[288,640]{1,0:T(8,128)(2,1)S(1)} %collective-permute-done.2), channel_id=1, source_target_pairs={{0,2},{2,4},{4,6},{6,8},{8,10},{10,12},{12,14},{14,0},{1,3},{3,5},... | collective-permute-start | bytes 1105928 | tf_op jit(solution)/shard_map/ppermute | solution.py:25
  124.3 29.2 %collective-permute-start.20 = (bf16[144,640]{1,0:T(8,128)(2,1)}, bf16[144,640]{1,0:T(8,128)(2,1)}, u32[]{:S(2)}, u32[]{:S(2)}) collective-permute-start(bf16[144,640]{1,0:T(8,128)(2,1)} %slice.95), channel_id=1, source_target_pairs={{0,14},{2,0},{4,2},{6,4},{8,6},{10,8},{12,10},{14,12},{1,15},{3,1}... | collective-permute-start | bytes 552968 | tf_op jit(solution)/shard_map/ppermute | solution.py:31
  127.0 27.8 %collective-permute-start.19 = (bf16[144,640]{1,0:T(8,128)(2,1)}, bf16[144,640]{1,0:T(8,128)(2,1)}, u32[]{:S(2)}, u32[]{:S(2)}) collective-permute-start(bf16[144,640]{1,0:T(8,128)(2,1)} %slice.94), channel_id=1, source_target_pairs={{0,2},{2,4},{4,6},{6,8},{8,10},{10,12},{12,14},{14,0},{1,3},{3,5},... | collective-permute-start | bytes 552968 | tf_op jit(solution)/shard_map/ppermute | solution.py:30
  132.2 8.6 %collective-permute-start.7 = (bf16[144,640]{1,0:T(8,128)(2,1)S(1)}, bf16[144,640]{1,0:T(8,128)(2,1)S(1)}, u32[]{:S(2)}, u32[]{:S(2)}) collective-permute-start(bf16[144,640]{1,0:T(8,128)(2,1)S(1)} %slice.82), channel_id=1, source_target_pairs={{0,14},{2,0},{4,2},{6,4},{8,6},{10,8},{12,10},{14,12},{1,15},{3,1}... | collective-permute-start | bytes 552968 | tf_op jit(solution)/shard_map/ppermute | solution.py:31
  134.1 8.2 %collective-permute-start.6 = (bf16[144,640]{1,0:T(8,128)(2,1)S(1)}, bf16[144,640]{1,0:T(8,128)(2,1)S(1)}, u32[]{:S(2)}, u32[]{:S(2)}) collective-permute-start(bf16[144,640]{1,0:T(8,128)(2,1)S(1)} %slice.81), channel_id=1, source_target_pairs={{0,2},{2,4},{4,6},{6,8},{8,10},{10,12},{12,14},{14,0},{1,3},{3,5},... | collective-permute-start | bytes 552968 | tf_op jit(solution)/shard_map/ppermute | solution.py:30
  143.8 42.5 %all-to-all-start.1 = ((bf16[8,288,128]{2,1,0:T(8,128)(2,1)}), bf16[8,288,128]{2,1,0:T(8,128)(2,1)}, u32[]{:S(2)}, u32[]{:S(2)}) async-start(bf16[8,288,128]{2,1,0:T(8,128)(2,1)} %broadcast_in_dim.88), calls=%async_computation.1 | async-start | bytes 1179648 | tf_op jit(solution)/shard_map/all_to_all | solution.py:112
  189.7 29.1 %all-to-all-start.2 = ((bf16[32,9,2,640]{3,2,1,0:T(2,128)(2,1)}), bf16[32,9,2,640]{3,2,1,0:T(2,128)(2,1)S(1)}, u32[]{:S(2)}, u32[]{:S(2)}) async-start(bf16[32,9,2,640]{3,2,1,0:T(2,128)(2,1)} %reshape.70), calls=%async_computation.2 | async-start | bytes 1474560 | tf_op jit(solution)/shard_map/all_to_all | solution.py:91
  (4 other events, 90.1 us)

commit v3 on v2

--- a/solution.py
+++ b/solution.py
@@ -17,45 +17,28 @@
     return [(i, (i + step) % size) for i in range(size)]
 
 
-def ring(x, size, use):
-    rows = x.shape[0]
-    use(x, 0, 0)
+def ring(x, size, last, use):
+    use(x, 0)
     up = down = x
     for step in range(1, size // 2):
         up = lax.ppermute(up, "tensor", shift(size, 1))
         down = lax.ppermute(down, "tensor", shift(size, -1))
-        use(up, -step, 0)
-        use(down, step, 0)
-    half = rows // 2
-    use(lax.ppermute(up[:half], "tensor", shift(size, 1)), size // 2, 0)
-    use(lax.ppermute(down[half:], "tensor", shift(size, -1)), size // 2, half)
+        use(up, -step)
+        use(down, step)
+    far = lax.ppermute(up if last > 0 else down, "tensor", shift(size, last))
+    use(far, size // 2)
 
 
 def down_rows(down_weight, size, part, hidden):
-    me, pair = lax.axis_index("tensor"), lax.axis_index("dp")
+    pair = lax.axis_index("dp")
+    half = part // 2
     blocks = down_weight.reshape(size, part, hidden)
-    steps = ((1, 2, -3), (-1, -2, 3))
-    got = []
-    for first, second in zip(*steps):
-        step = jnp.where(pair == 0, first, second)
-        block = lax.dynamic_index_in_dim(blocks, lax.rem(me + step + size, size), 0, keepdims=False)
-        perm = [(2 * i, 2 * ((i + first) % size)) for i in range(size)]
-        perm += [(2 * i + 1, 2 * ((i + second) % size) + 1) for i in range(size)]
-        got.append(lax.ppermute(block, ("tensor", "dp"), perm))
-    half = part // 2
-    far = lax.rem(me + size // 2, size)
-    block = lax.dynamic_slice(blocks, (far, pair * half, 0), (1, half, hidden))[0]
-    got.append(lax.ppermute(block, "tensor", shift(size, size // 2)))
-    got = jnp.concatenate(got, axis=0)
-    other = lax.ppermute(got, "dp", [(0, 1), (1, 0)])
-    a = jnp.where(pair == 0, got, other)
-    b = jnp.where(pair == 0, other, got)
-    own = lax.dynamic_index_in_dim(blocks, me, 0, keepdims=False)
-    piece = lambda x, i: x[i * part : (i + 1) * part]
-    far = jnp.concatenate([a[3 * part :], b[3 * part :]], axis=0)
-    near = [own, piece(b, 0), piece(b, 1), piece(a, 2), far, piece(b, 2), piece(a, 1), piece(a, 0)]
-    twice = jnp.stack(near + near)
-    return lax.dynamic_slice_in_dim(twice, lax.rem(size - me, size), size, 0)
+    mine = lax.dynamic_slice_in_dim(blocks, pair * half, half, 1)
+    mine = lax.all_to_all(mine, "tensor", 0, 0, tiled=True)
+    other = lax.ppermute(mine, "dp", [(0, 1), (1, 0)])
+    low = jnp.where(pair == 0, mine, other)
+    high = jnp.where(pair == 0, other, mine)
+    return jnp.concatenate([low, high], axis=1)
 
 
 def local(tokens, routes, gates, gate_up, down_weight, old_map, new_map):
@@ -91,24 +74,24 @@
         x = lax.all_to_all(x, EXPERT, 0, 0, tiled=True)
         return x.reshape(rows, part)
 
-    arrived = exchange(outgoing)
+    arrived = lax.optimization_barrier(exchange(outgoing))
     down_mine = down_rows(down_weight, size, part, hidden)
 
     weight_in = gate_up.reshape(size, part, 2 * hidden)
 
-    def projected(x):
+    def projected(x, last):
         pieces = []
 
-        def use(block, distance, start):
+        def use(block, distance):
             w = lax.dynamic_index_in_dim(weight_in, lax.rem(me + distance + size, size), 0, keepdims=False)
             pieces.append(dot(block, w))
 
-        ring(x, size, use)
-        total = sum(pieces[:-2]) + jnp.concatenate(pieces[-2:], axis=0)
+        ring(x, size, last, use)
+        total = sum(pieces)
         return (jax.nn.silu(total[:, :hidden]) * total[:, hidden:]).astype(bf16)
 
     half = rows // 2
-    act_a, act_b = projected(arrived[:half]), projected(arrived[half:])
+    act_a, act_b = projected(arrived[:half], 1), projected(arrived[half:], -1)
     all_a = lax.all_to_all(jnp.broadcast_to(act_a[None], (size, half, hidden)), "tensor", 0, 0, tiled=True)
     all_b = lax.all_gather(act_b, "tensor")
 

time: 222 us -> 210 us (0.946)
  the two profiles are of different devices: /device:TPU:24 before, /device:TPU:25 now
where the time goes in v3:
time: 210 us; the launch traced here: 209 us
  starting transfers between devices  92 us (44%)
  waiting for transfers between devices  58.6 us (28%)
  blocking collectives  27.5 us (13%)
  matrix products  15.7 us (7%)
  local copies, waits for them, and re-layouts  11.6 us (6%)
  other arithmetic  2.78 us (1%)
    all_to_all x2, waiting for transfers between devices, exchange(): x = lax.all_to_all(x, EXPERT, 0, 0, tiled=True)  35.4 us
    all_to_all x2, starting transfers between devices, exchange(): x = lax.all_to_all(x, EXPERT, 0, 0, tiled=True)  28.9 us
    all_gather x1, blocking collectives, local(): all_b = lax.all_gather(act_b, 'tensor')  27.5 us
    ppermute x6, starting transfers between devices, ring(): up = lax.ppermute(up, 'tensor', shift(size, 1))  25.8 us
    dot_general x20, matrix products, dot(): lax.dot_general(a, b, (dims, ((), ())), preferred_element_type=jnp.float32)  14.5 us
    all_to_all x1, waiting for transfers between devices, down_rows(): mine = lax.all_to_all(mine, 'tensor', 0, 0, tiled=True)  12.1 us
    ppermute x6, starting transfers between devices, ring(): down = lax.ppermute(down, 'tensor', shift(size, -1))  11.8 us
    all_to_all x1, starting transfers between devices, local(): lax.all_to_all(jnp.broadcast_to(act_a[None], (size, half, hidden)), 'tens...  10.3 us
  transfers between devices with their start and end apart: 19, of which 7 were waited for; matrix products, arithmetic and copies ran while one was open for 11% of the time, Pallas kernels for 0%

profile of v3, /device:TPU:25, one launch (start us, length us, event | category | flops | bytes accessed | tf_op | source)
XLA Modules:
  0.0 208.8 jit_solution(11959384988830815105)
XLA Ops:
  2.2 6.8 %all-to-all-start.2 = ((bf16[8,320,128]{2,1,0:T(8,128)(2,1)}), bf16[8,320,128]{2,1,0:T(8,128)(2,1)S(1)}, u32[]{:S(2)}, u32[]{:S(2)}) async-start(bf16[8,320,128]{2,1,0:T(8,128)(2,1)} %constant_dynamic-slice_fusion), calls=%async_computation.2 | async-start | bytes 1310720 | tf_op jit(solution)/shard_map/all_to_all | solution.py:37
  11.3 12.1 %all-to-all-done.2 = bf16[8,320,128]{2,1,0:T(8,128)(2,1)S(1)} async-done(((bf16[8,320,128]{2,1,0:T(8,128)(2,1)}), bf16[8,320,128]{2,1,0:T(8,128)(2,1)S(1)}, u32[]{:S(2)}, u32[]{:S(2)}) %all-to-all-start.2) | async-done | bytes 655392 | tf_op jit(solution)/shard_map/all_to_all | solution.py:37
  23.4 16.0 %all-to-all-start = ((bf16[32,9,2,640]{3,2,1,0:T(2,128)(2,1)}), bf16[32,9,2,640]{3,2,1,0:T(2,128)(2,1)S(1)}, u32[]{:S(2)}, u32[]{:S(2)}) async-start(bf16[32,9,2,640]{3,2,1,0:T(2,128)(2,1)} %reshape.67), calls=%async_computation | async-start | bytes 1474560 | tf_op jit(solution)/shard_map/all_to_all | solution.py:74
  39.4 5.3 %reshape.69 = bf16[8,640,256]{2,1,0:T(8,128)(2,1)} reshape(bf16[1,5120,2,128]{3,2,1,0:T(2,128)(2,1)} %param.10) | data formatting | bytes 5242880 | tf_op jit(solution)/shard_map/reshape | solution.py:80
  44.7 3.1 %collective-permute-start.7 = (bf16[8,320,128]{2,1,0:T(8,128)(2,1)S(1)}, bf16[8,320,128]{2,1,0:T(8,128)(2,1)}, u32[]{:S(2)}, u32[]{:S(2)}) collective-permute-start(bf16[8,320,128]{2,1,0:T(8,128)(2,1)S(1)} %all-to-all-done.2), channel_id=1, source_target_pairs={{0,1},{1,0},{2,3},{3,2},{4,5},{5,4},{6,7},{7,6},{8,9},{9,8},{10,11... | collective-permute-start | bytes 1966088 | tf_op jit(solution)/shard_map/ppermute | solution.py:38
  47.8 13.2 %all-to-all-done = bf16[32,9,2,640]{3,2,1,0:T(2,128)(2,1)S(1)} async-done(((bf16[32,9,2,640]{3,2,1,0:T(2,128)(2,1)}), bf16[32,9,2,640]{3,2,1,0:T(2,128)(2,1)S(1)}, u32[]{:S(2)}, u32[]{:S(2)}) %all-to-all-start) | async-done | bytes 737312 | tf_op jit(solution)/shard_map/all_to_all | solution.py:74
  61.3 3.2 %collective-permute-start = (bf16[288,640]{1,0:T(8,128)(2,1)S(1)}, bf16[288,640]{1,0:T(8,128)(2,1)S(1)}, u32[]{:S(2)}, u32[]{:S(2)}) collective-permute-start(bf16[288,640]{1,0:T(8,128)(2,1)S(1)} %get-tuple-element.7), channel_id=1, source_target_pairs={{0,2},{2,4},{4,6},{6,8},{8,10},{10,12},{12,14},{14,0},{1,3},{3,5},... | collective-permute-start | bytes 1105928 | tf_op jit(solution)/shard_map/ppermute | solution.py:24
  64.6 2.2 %collective-permute-start.1 = (bf16[288,640]{1,0:T(8,128)(2,1)S(1)}, bf16[288,640]{1,0:T(8,128)(2,1)S(1)}, u32[]{:S(2)}, u32[]{:S(2)}) collective-permute-start(bf16[288,640]{1,0:T(8,128)(2,1)S(1)} %get-tuple-element.7), channel_id=1, source_target_pairs={{0,14},{2,0},{4,2},{6,4},{8,6},{10,8},{12,10},{14,12},{1,15},{3,1}... | collective-permute-start | bytes 1105928 | tf_op jit(solution)/shard_map/ppermute | solution.py:25
  66.8 4.3 %collective-permute-start.8 = (bf16[288,640]{1,0:T(8,128)(2,1)S(1)}, bf16[288,640]{1,0:T(8,128)(2,1)S(1)}, u32[]{:S(2)}, u32[]{:S(2)}) collective-permute-start(bf16[288,640]{1,0:T(8,128)(2,1)S(1)} %get-tuple-element.8), channel_id=1, source_target_pairs={{0,2},{2,4},{4,6},{6,8},{8,10},{10,12},{12,14},{14,0},{1,3},{3,5},... | collective-permute-start | bytes 1105928 | tf_op jit(solution)/shard_map/ppermute | solution.py:24
  71.1 1.9 collective-permute-start.9
  75.5 2.7 %collective-permute-done.1 = bf16[288,640]{1,0:T(8,128)(2,1)S(1)} collective-permute-done((bf16[288,640]{1,0:T(8,128)(2,1)S(1)}, bf16[288,640]{1,0:T(8,128)(2,1)S(1)}, u32[]{:S(2)}, u32[]{:S(2)}) %collective-permute-start.1) | collective-permute-done | bytes 368672 | tf_op jit(solution)/shard_map/ppermute | solution.py:25
  80.2 4.6 %collective-permute-start.2 = (bf16[288,640]{1,0:T(8,128)(2,1)S(1)}, bf16[288,640]{1,0:T(8,128)(2,1)S(1)}, u32[]{:S(2)}, u32[]{:S(2)}) collective-permute-start(bf16[288,640]{1,0:T(8,128)(2,1)S(1)} %collective-permute-done), channel_id=1, source_target_pairs={{0,2},{2,4},{4,6},{6,8},{8,10},{10,12},{12,14},{14,0},{1,3},{3,5},... | collective-permute-start | bytes 1105928 | tf_op jit(solution)/shard_map/ppermute | solution.py:24
  88.1 4.6 %collective-permute-start.10 = (bf16[288,640]{1,0:T(8,128)(2,1)S(1)}, bf16[288,640]{1,0:T(8,128)(2,1)}, u32[]{:S(2)}, u32[]{:S(2)}) collective-permute-start(bf16[288,640]{1,0:T(8,128)(2,1)S(1)} %collective-permute-done.8), channel_id=1, source_target_pairs={{0,2},{2,4},{4,6},{6,8},{8,10},{10,12},{12,14},{14,0},{1,3},{3,5},... | collective-permute-start | bytes 1105928 | tf_op jit(solution)/shard_map/ppermute | solution.py:24
  93.9 2.2 %broadcast_select_fusion.1 = (bf16[8,320,128]{2,1,0:T(8,128)(2,1)}, bf16[8,320,128]{2,1,0:T(8,128)(2,1)}) fusion(bf16[8,320,128]{2,1,0:T(8,128)(2,1)S(1)} %all-to-all-done.2, bf16[8,320,128]{2,1,0:T(8,128)(2,1)} %collective-permute-done.7, pred[]{:T(512)S(6)} %eq.92), kind=kLoop, calls=%fused_computation.25 | loop fusion | flops 655360 | bytes 2621441 | tf_op jit(solution)/shard_map/jit(_where)/select_n | solution.py:39
  98.1 4.6 %collective-permute-start.4 = (bf16[288,640]{1,0:T(8,128)(2,1)S(1)}, bf16[288,640]{1,0:T(8,128)(2,1)S(1)}, u32[]{:S(2)}, u32[]{:S(2)}) collective-permute-start(bf16[288,640]{1,0:T(8,128)(2,1)S(1)} %collective-permute-done.2), channel_id=1, source_target_pairs={{0,2},{2,4},{4,6},{6,8},{8,10},{10,12},{12,14},{14,0},{1,3},{3,5},... | collective-permute-start | bytes 1105928 | tf_op jit(solution)/shard_map/ppermute | solution.py:24
  102.7 1.9 collective-permute-start.13
  104.9 4.6 %collective-permute-start.12 = (bf16[288,640]{1,0:T(8,128)(2,1)}, bf16[288,640]{1,0:T(8,128)(2,1)}, u32[]{:S(2)}, u32[]{:S(2)}) collective-permute-start(bf16[288,640]{1,0:T(8,128)(2,1)} %collective-permute-done.10), channel_id=1, source_target_pairs={{0,2},{2,4},{4,6},{6,8},{8,10},{10,12},{12,14},{14,0},{1,3},{3,5},... | collective-permute-start | bytes 1105928 | tf_op jit(solution)/shard_map/ppermute | solution.py:24
  111.4 3.5 %collective-permute-start.6 = (bf16[288,640]{1,0:T(8,128)(2,1)S(1)}, bf16[288,640]{1,0:T(8,128)(2,1)S(1)}, u32[]{:S(2)}, u32[]{:S(2)}) collective-permute-start(bf16[288,640]{1,0:T(8,128)(2,1)S(1)} %collective-permute-done.4), channel_id=1, source_target_pairs={{0,2},{2,4},{4,6},{6,8},{8,10},{10,12},{12,14},{14,0},{1,3},{3,5},... | collective-permute-start | bytes 1105928 | tf_op jit(solution)/shard_map/ppermute | solution.py:28
  116.7 1.9 collective-permute-start.14
  120.5 5.2 %collective-permute-done.6 = bf16[288,640]{1,0:T(8,128)(2,1)S(1)} collective-permute-done((bf16[288,640]{1,0:T(8,128)(2,1)S(1)}, bf16[288,640]{1,0:T(8,128)(2,1)S(1)}, u32[]{:S(2)}, u32[]{:S(2)}) %collective-permute-start.6) | collective-permute-done | bytes 368672 | tf_op jit(solution)/shard_map/ppermute | solution.py:28
  126.9 10.3 %all-to-all-start.1 = ((bf16[8,288,128]{2,1,0:T(8,128)(2,1)}), bf16[8,288,128]{2,1,0:T(8,128)(2,1)}, u32[]{:S(2)}, u32[]{:S(2)}) async-start(bf16[8,288,128]{2,1,0:T(8,128)(2,1)} %broadcast_in_dim.88), calls=%async_computation.1 | async-start | bytes 1179648 | tf_op jit(solution)/shard_map/all_to_all | solution.py:95
  140.1 27.5 %all-gather = bf16[2304,128]{1,0:T(8,128)(2,1)S(1)} all-gather(bf16[288,128]{1,0:T(8,128)(2,1)S(1)} %fusion.47), channel_id=2, replica_groups=mesh['expert_0'=4,'expert_1'=4,'expert_2'=2,'tensor'=8,'dp'=2] {'tensor'}, dimensions={0}, use_global_device_ids=true | all-gather | bytes 663552 | tf_op jit(solution)/shard_map/all_gather | solution.py:96
  172.0 12.9 %all-to-all-start.3 = ((bf16[32,9,2,640]{3,2,1,0:T(2,128)(2,1)}), bf16[32,9,2,640]{3,2,1,0:T(2,128)(2,1)S(1)}, u32[]{:S(2)}, u32[]{:S(2)}) async-start(bf16[32,9,2,640]{3,2,1,0:T(2,128)(2,1)} %reshape.71), calls=%async_computation.3 | async-start | bytes 1474560 | tf_op jit(solution)/shard_map/all_to_all | solution.py:74
  185.0 22.2 %all-to-all-done.3 = bf16[32,9,2,640]{3,2,1,0:T(2,128)(2,1)S(1)} async-done(((bf16[32,9,2,640]{3,2,1,0:T(2,128)(2,1)}), bf16[32,9,2,640]{3,2,1,0:T(2,128)(2,1)S(1)}, u32[]{:S(2)}, u32[]{:S(2)}) %all-to-all-start.3) | async-done | bytes 737312 | tf_op jit(solution)/shard_map/all_to_all | solution.py:74
  (79 shorter events, 31.4 us)
Async XLA Ops:
  0.0 9.7 %copy-start.5 = (bf16[96,640]{1,0:T(8,128)(2,1)S(1)}, bf16[96,640]{1,0:T(8,128)(2,1)}, u32[]{:S(2)}) copy-start(bf16[96,640]{1,0:T(8,128)(2,1)} %param.7) | copy-start | bytes 368644
  2.2 21.1 %all-to-all-start.2 = ((bf16[8,320,128]{2,1,0:T(8,128)(2,1)}), bf16[8,320,128]{2,1,0:T(8,128)(2,1)S(1)}, u32[]{:S(2)}, u32[]{:S(2)}) async-start(bf16[8,320,128]{2,1,0:T(8,128)(2,1)} %constant_dynamic-slice_fusion), calls=%async_computation.2 | async-start | bytes 1310720 | tf_op jit(solution)/shard_map/all_to_all | solution.py:37
  23.4 37.6 %all-to-all-start = ((bf16[32,9,2,640]{3,2,1,0:T(2,128)(2,1)}), bf16[32,9,2,640]{3,2,1,0:T(2,128)(2,1)S(1)}, u32[]{:S(2)}, u32[]{:S(2)}) async-start(bf16[32,9,2,640]{3,2,1,0:T(2,128)(2,1)} %reshape.67), calls=%async_computation | async-start | bytes 1474560 | tf_op jit(solution)/shard_map/all_to_all | solution.py:74
  44.7 49.2 %collective-permute-start.7 = (bf16[8,320,128]{2,1,0:T(8,128)(2,1)S(1)}, bf16[8,320,128]{2,1,0:T(8,128)(2,1)}, u32[]{:S(2)}, u32[]{:S(2)}) collective-permute-start(bf16[8,320,128]{2,1,0:T(8,128)(2,1)S(1)} %all-to-all-done.2), channel_id=1, source_target_pairs={{0,1},{1,0},{2,3},{3,2},{4,5},{5,4},{6,7},{7,6},{8,9},{9,8},{10,11... | collective-permute-start | bytes 1966088 | tf_op jit(solution)/shard_map/ppermute | solution.py:38
  61.3 31.4 %copy-start.1 = (bf16[8,640,256]{2,1,0:T(8,128)(2,1)S(1)}, bf16[8,640,256]{2,1,0:T(8,128)(2,1)}, u32[]{:S(2)}) copy-start(bf16[8,640,256]{2,1,0:T(8,128)(2,1)} %reshape.69) | copy-start | bytes 7864324
  61.3 18.8 %collective-permute-start = (bf16[288,640]{1,0:T(8,128)(2,1)S(1)}, bf16[288,640]{1,0:T(8,128)(2,1)S(1)}, u32[]{:S(2)}, u32[]{:S(2)}) collective-permute-start(bf16[288,640]{1,0:T(8,128)(2,1)S(1)} %get-tuple-element.7), channel_id=1, source_target_pairs={{0,2},{2,4},{4,6},{6,8},{8,10},{10,12},{12,14},{14,0},{1,3},{3,5},... | collective-permute-start | bytes 1105928 | tf_op jit(solution)/shard_map/ppermute | solution.py:24
  64.6 13.7 %collective-permute-start.1 = (bf16[288,640]{1,0:T(8,128)(2,1)S(1)}, bf16[288,640]{1,0:T(8,128)(2,1)S(1)}, u32[]{:S(2)}, u32[]{:S(2)}) collective-permute-start(bf16[288,640]{1,0:T(8,128)(2,1)S(1)} %get-tuple-element.7), channel_id=1, source_target_pairs={{0,14},{2,0},{4,2},{6,4},{8,6},{10,8},{12,10},{14,12},{1,15},{3,1}... | collective-permute-start | bytes 1105928 | tf_op jit(solution)/shard_map/ppermute | solution.py:25
  66.8 21.3 %collective-permute-start.8 = (bf16[288,640]{1,0:T(8,128)(2,1)S(1)}, bf16[288,640]{1,0:T(8,128)(2,1)S(1)}, u32[]{:S(2)}, u32[]{:S(2)}) collective-permute-start(bf16[288,640]{1,0:T(8,128)(2,1)S(1)} %get-tuple-element.8), channel_id=1, source_target_pairs={{0,2},{2,4},{4,6},{6,8},{8,10},{10,12},{12,14},{14,0},{1,3},{3,5},... | collective-permute-start | bytes 1105928 | tf_op jit(solution)/shard_map/ppermute | solution.py:24
  71.1 15.1 %collective-permute-start.9 = (bf16[288,640]{1,0:T(8,128)(2,1)S(1)}, bf16[288,640]{1,0:T(8,128)(2,1)S(1)}, u32[]{:S(2)}, u32[]{:S(2)}) collective-permute-start(bf16[288,640]{1,0:T(8,128)(2,1)S(1)} %get-tuple-element.8), channel_id=1, source_target_pairs={{0,14},{2,0},{4,2},{6,4},{8,6},{10,8},{12,10},{14,12},{1,15},{3,1}... | collective-permute-start | bytes 1105928 | tf_op jit(solution)/shard_map/ppermute | solution.py:25
  78.3 17.9 %collective-permute-start.3 = (bf16[288,640]{1,0:T(8,128)(2,1)S(1)}, bf16[288,640]{1,0:T(8,128)(2,1)S(1)}, u32[]{:S(2)}, u32[]{:S(2)}) collective-permute-start(bf16[288,640]{1,0:T(8,128)(2,1)S(1)} %collective-permute-done.1), channel_id=1, source_target_pairs={{0,14},{2,0},{4,2},{6,4},{8,6},{10,8},{12,10},{14,12},{1,15},{3,1}... | collective-permute-start | bytes 1105928 | tf_op jit(solution)/shard_map/ppermute | solution.py:25
  80.2 17.9 %collective-permute-start.2 = (bf16[288,640]{1,0:T(8,128)(2,1)S(1)}, bf16[288,640]{1,0:T(8,128)(2,1)S(1)}, u32[]{:S(2)}, u32[]{:S(2)}) collective-permute-start(bf16[288,640]{1,0:T(8,128)(2,1)S(1)} %collective-permute-done), channel_id=1, source_target_pairs={{0,2},{2,4},{4,6},{6,8},{8,10},{10,12},{12,14},{14,0},{1,3},{3,5},... | collective-permute-start | bytes 1105928 | tf_op jit(solution)/shard_map/ppermute | solution.py:24
  86.2 16.5 %collective-permute-start.11 = (bf16[288,640]{1,0:T(8,128)(2,1)S(1)}, bf16[288,640]{1,0:T(8,128)(2,1)S(1)}, u32[]{:S(2)}, u32[]{:S(2)}) collective-permute-start(bf16[288,640]{1,0:T(8,128)(2,1)S(1)} %collective-permute-done.9), channel_id=1, source_target_pairs={{0,14},{2,0},{4,2},{6,4},{8,6},{10,8},{12,10},{14,12},{1,15},{3,1}... | collective-permute-start | bytes 1105928 | tf_op jit(solution)/shard_map/ppermute | solution.py:25
  88.1 16.8 %collective-permute-start.10 = (bf16[288,640]{1,0:T(8,128)(2,1)S(1)}, bf16[288,640]{1,0:T(8,128)(2,1)}, u32[]{:S(2)}, u32[]{:S(2)}) collective-permute-start(bf16[288,640]{1,0:T(8,128)(2,1)S(1)} %collective-permute-done.8), channel_id=1, source_target_pairs={{0,2},{2,4},{4,6},{6,8},{8,10},{10,12},{12,14},{14,0},{1,3},{3,5},... | collective-permute-start | bytes 1105928 | tf_op jit(solution)/shard_map/ppermute | solution.py:24
  96.1 23.7 %collective-permute-start.5 = (bf16[288,640]{1,0:T(8,128)(2,1)S(1)}, bf16[288,640]{1,0:T(8,128)(2,1)S(1)}, u32[]{:S(2)}, u32[]{:S(2)}) collective-permute-start(bf16[288,640]{1,0:T(8,128)(2,1)S(1)} %collective-permute-done.3), channel_id=1, source_target_pairs={{0,14},{2,0},{4,2},{6,4},{8,6},{10,8},{12,10},{14,12},{1,15},{3,1}... | collective-permute-start | bytes 1105928 | tf_op jit(solution)/shard_map/ppermute | solution.py:25
  98.1 13.3 %collective-permute-start.4 = (bf16[288,640]{1,0:T(8,128)(2,1)S(1)}, bf16[288,640]{1,0:T(8,128)(2,1)S(1)}, u32[]{:S(2)}, u32[]{:S(2)}) collective-permute-start(bf16[288,640]{1,0:T(8,128)(2,1)S(1)} %collective-permute-done.2), channel_id=1, source_target_pairs={{0,2},{2,4},{4,6},{6,8},{8,10},{10,12},{12,14},{14,0},{1,3},{3,5},... | collective-permute-start | bytes 1105928 | tf_op jit(solution)/shard_map/ppermute | solution.py:24
  102.7 14.0 %collective-permute-start.13 = (bf16[288,640]{1,0:T(8,128)(2,1)S(1)}, bf16[288,640]{1,0:T(8,128)(2,1)}, u32[]{:S(2)}, u32[]{:S(2)}) collective-permute-start(bf16[288,640]{1,0:T(8,128)(2,1)S(1)} %collective-permute-done.11), channel_id=1, source_target_pairs={{0,14},{2,0},{4,2},{6,4},{8,6},{10,8},{12,10},{14,12},{1,15},{3,1}... | collective-permute-start | bytes 1105928 | tf_op jit(solution)/shard_map/ppermute | solution.py:25
  104.9 32.3 %collective-permute-start.12 = (bf16[288,640]{1,0:T(8,128)(2,1)}, bf16[288,640]{1,0:T(8,128)(2,1)}, u32[]{:S(2)}, u32[]{:S(2)}) collective-permute-start(bf16[288,640]{1,0:T(8,128)(2,1)} %collective-permute-done.10), channel_id=1, source_target_pairs={{0,2},{2,4},{4,6},{6,8},{8,10},{10,12},{12,14},{14,0},{1,3},{3,5},... | collective-permute-start | bytes 1105928 | tf_op jit(solution)/shard_map/ppermute | solution.py:24
  111.4 14.3 %collective-permute-start.6 = (bf16[288,640]{1,0:T(8,128)(2,1)S(1)}, bf16[288,640]{1,0:T(8,128)(2,1)S(1)}, u32[]{:S(2)}, u32[]{:S(2)}) collective-permute-start(bf16[288,640]{1,0:T(8,128)(2,1)S(1)} %collective-permute-done.4), channel_id=1, source_target_pairs={{0,2},{2,4},{4,6},{6,8},{8,10},{10,12},{12,14},{14,0},{1,3},{3,5},... | collective-permute-start | bytes 1105928 | tf_op jit(solution)/shard_map/ppermute | solution.py:28
  116.7 22.0 %collective-permute-start.14 = (bf16[288,640]{1,0:T(8,128)(2,1)}, bf16[288,640]{1,0:T(8,128)(2,1)}, u32[]{:S(2)}, u32[]{:S(2)}) collective-permute-start(bf16[288,640]{1,0:T(8,128)(2,1)} %collective-permute-done.13), channel_id=1, source_target_pairs={{0,14},{2,0},{4,2},{6,4},{8,6},{10,8},{12,10},{14,12},{1,15},{3,1}... | collective-permute-start | bytes 1105928 | tf_op jit(solution)/shard_map/ppermute | solution.py:28
  126.9 40.6 %copy-start.2 = (bf16[8,320,128]{2,1,0:T(8,128)(2,1)S(1)}, bf16[8,320,128]{2,1,0:T(8,128)(2,1)}, u32[]{:S(2)}) copy-start(bf16[8,320,128]{2,1,0:T(8,128)(2,1)} %get-tuple-element.5) | copy-start | bytes 1966084
  126.9 40.6 %copy-start.3 = (bf16[8,320,128]{2,1,0:T(8,128)(2,1)S(1)}, bf16[8,320,128]{2,1,0:T(8,128)(2,1)}, u32[]{:S(2)}) copy-start(bf16[8,320,128]{2,1,0:T(8,128)(2,1)} %get-tuple-element.6) | copy-start | bytes 1966084
  126.9 42.0 %all-to-all-start.1 = ((bf16[8,288,128]{2,1,0:T(8,128)(2,1)}), bf16[8,288,128]{2,1,0:T(8,128)(2,1)}, u32[]{:S(2)}, u32[]{:S(2)}) async-start(bf16[8,288,128]{2,1,0:T(8,128)(2,1)} %broadcast_in_dim.88), calls=%async_computation.1 | async-start | bytes 1179648 | tf_op jit(solution)/shard_map/all_to_all | solution.py:95
  170.7 14.2 %copy-start.7 = (f32[96,6]{0,1:T(8,128)S(1)}, f32[96,6]{0,1:T(8,128)}, u32[]{:S(2)}) copy-start(f32[96,6]{0,1:T(8,128)} %param.9) | copy-start | bytes 6916
  172.0 35.3 %all-to-all-start.3 = ((bf16[32,9,2,640]{3,2,1,0:T(2,128)(2,1)}), bf16[32,9,2,640]{3,2,1,0:T(2,128)(2,1)S(1)}, u32[]{:S(2)}, u32[]{:S(2)}) async-start(bf16[32,9,2,640]{3,2,1,0:T(2,128)(2,1)} %reshape.71), calls=%async_computation.3 | async-start | bytes 1474560 | tf_op jit(solution)/shard_map/all_to_all | solution.py:74
  (5 other events, 30.3 us)

commit v4 on v3

--- a/solution.py
+++ b/solution.py
@@ -1,6 +1,10 @@
+import functools
+
 import jax
 import jax.numpy as jnp
 from jax import lax
+from jax.experimental import pallas as pl
+from jax.experimental.pallas import tpu as pltpu
 from jax.sharding import Mesh
 from jax.sharding import PartitionSpec as P
 
@@ -29,16 +33,74 @@
     use(far, size // 2)
 
 
+def pack_kernel(first, second, third, fourth, out):
+    rows = first.shape[0]
+    for i, ref in enumerate((first, second, third)):
+        out[i * rows : (i + 1) * rows, :] = ref[...]
+    out[3 * rows :, :] = fourth[...]
+
+
+def place_kernel(size, place, own, mine, other, out):
+    rows = own.shape[0]
+    me = place[0]
+
+    def put(distance, value, start=0):
+        at = lax.rem(me + distance, size)
+        out[pl.ds(at, 1), start : start + value.shape[0], :] = value[None]
+
+    def fill(a, b):
+        put(1, b[0:rows, :])
+        put(2, b[rows : 2 * rows, :])
+        put(size - 3, b[2 * rows : 3 * rows, :])
+        put(size - 1, a[0:rows, :])
+        put(size - 2, a[rows : 2 * rows, :])
+        put(3, a[2 * rows : 3 * rows, :])
+        put(size // 2, a[3 * rows :, :])
+        put(size // 2, b[3 * rows :, :], rows // 2)
+
+    put(0, own[...])
+
+    @pl.when(place[1] == 0)
+    def _():
+        fill(mine, other)
+
+    @pl.when(place[1] == 1)
+    def _():
+        fill(other, mine)
+
+
 def down_rows(down_weight, size, part, hidden):
-    pair = lax.axis_index("dp")
+    me, pair = lax.axis_index("tensor"), lax.axis_index("dp")
+    blocks = down_weight.reshape(size, part, hidden)
+    steps = ((1, 2, -3), (-1, -2, 3))
+    got = []
+    for first, second in zip(*steps):
+        step = jnp.where(pair == 0, first, second)
+        block = lax.dynamic_index_in_dim(blocks, lax.rem(me + step + size, size), 0, keepdims=False)
+        perm = [(2 * i, 2 * ((i + first) % size)) for i in range(size)]
+        perm += [(2 * i + 1, 2 * ((i + second) % size) + 1) for i in range(size)]
+        got.append(lax.ppermute(block, ("tensor", "dp"), perm))
     half = part // 2
-    blocks = down_weight.reshape(size, part, hidden)
-    mine = lax.dynamic_slice_in_dim(blocks, pair * half, half, 1)
-    mine = lax.all_to_all(mine, "tensor", 0, 0, tiled=True)
+    far = lax.rem(me + size // 2, size)
+    block = lax.dynamic_slice(blocks, (far, pair * half, 0), (1, half, hidden))[0]
+    got.append(lax.ppermute(block, "tensor", shift(size, size // 2)))
+    vmem = pl.BlockSpec(memory_space=pltpu.VMEM)
+    mine = pl.pallas_call(
+        pack_kernel,
+        out_shape=jax.ShapeDtypeStruct((3 * part + half, hidden), blocks.dtype),
+        in_specs=[vmem] * 4,
+        out_specs=vmem,
+        name="pack",
+    )(*got)
     other = lax.ppermute(mine, "dp", [(0, 1), (1, 0)])
-    low = jnp.where(pair == 0, mine, other)
-    high = jnp.where(pair == 0, other, mine)
-    return jnp.concatenate([low, high], axis=1)
+    own = lax.dynamic_index_in_dim(blocks, me, 0, keepdims=False)
+    return pl.pallas_call(
+        functools.partial(place_kernel, size),
+        out_shape=jax.ShapeDtypeStruct(blocks.shape, blocks.dtype),
+        in_specs=[pl.BlockSpec(memory_space=pltpu.SMEM)] + [vmem] * 3,
+        out_specs=vmem,
+        name="place",
+    )(jnp.stack([me, pair]).astype(jnp.int32), own, mine, other)
 
 
 def local(tokens, routes, gates, gate_up, down_weight, old_map, new_map):
@@ -77,14 +139,14 @@
     arrived = lax.optimization_barrier(exchange(outgoing))
     down_mine = down_rows(down_weight, size, part, hidden)
 
-    weight_in = gate_up.reshape(size, part, 2 * hidden)
+    weight_in = gate_up.reshape(size, part, 2, hidden)
 
     def projected(x, last):
         pieces = []
 
         def use(block, distance):
             w = lax.dynamic_index_in_dim(weight_in, lax.rem(me + distance + size, size), 0, keepdims=False)
-            pieces.append(dot(block, w))
+            pieces.append(dot(block, w.reshape(part, 2 * hidden)))
 
         ring(x, size, last, use)
         total = sum(pieces)

time: 210 us -> 210 us (level)
  the two profiles are of different devices: /device:TPU:25 before, /device:TPU:64 now
where the time goes in v4:
time: 210 us; the launch traced here: 208 us
  starting transfers between devices  91.5 us (44%)
  waiting for transfers between devices  56.9 us (27%)
  blocking collectives  30.2 us (14%)
  local copies, waits for them, and re-layouts  10.9 us (5%)
  matrix products  10.8 us (5%)
  Pallas kernels  4.43 us (2%)
  other arithmetic  2.51 us (1%)
    all_gather x1, blocking collectives, local(): all_b = lax.all_gather(act_b, 'tensor')  30.2 us
    all_to_all x2, waiting for transfers between devices, exchange(): x = lax.all_to_all(x, EXPERT, 0, 0, tiled=True)  23.3 us
    all_to_all x2, starting transfers between devices, exchange(): x = lax.all_to_all(x, EXPERT, 0, 0, tiled=True)  21.9 us
    ppermute x6, starting transfers between devices, ring(): down = lax.ppermute(down, 'tensor', shift(size, -1))  20.4 us
    ppermute x6, starting transfers between devices, ring(): up = lax.ppermute(up, 'tensor', shift(size, 1))  18.6 us
    ppermute x3, starting transfers between devices, down_rows(): got.append(lax.ppermute(block, ('tensor', 'dp'), perm))  11.3 us
    ppermute x1, waiting for transfers between devices, down_rows(): other = lax.ppermute(mine, 'dp', [(0, 1), (1, 0)])  11.1 us
    ppermute x6, waiting for transfers between devices, ring(): down = lax.ppermute(down, 'tensor', shift(size, -1))  9.66 us
  transfers between devices with their start and end apart: 22, of which 9 were waited for; matrix products, arithmetic and copies ran while one was open for 7% of the time, Pallas kernels for 2%

profile of v4, /device:TPU:64, one launch (start us, length us, event | category | flops | bytes accessed | tf_op | source)
XLA Modules:
  0.0 208.0 jit_solution(7082344014362709135)
XLA Ops:
  3.7 12.3 %all-to-all-start = ((bf16[32,9,2,640]{3,2,1,0:T(2,128)(2,1)}), bf16[32,9,2,640]{3,2,1,0:T(2,128)(2,1)S(1)}, u32[]{:S(2)}, u32[]{:S(2)}) async-start(bf16[32,9,2,640]{3,2,1,0:T(2,128)(2,1)} %reshape.107), calls=%async_computation | async-start | bytes 1474560 | tf_op jit(solution)/shard_map/all_to_all | solution.py:136
  16.7 5.4 %collective-permute-start.7 = (bf16[640,128]{1,0:T(8,128)(2,1)S(1)}, bf16[640,128]{1,0:T(8,128)(2,1)S(1)}, u32[]{:S(2)}, u32[]{:S(2)}) collective-permute-start(bf16[640,128]{1,0:T(8,128)(2,1)S(1)} %get-tuple-element.15), channel_id=1, source_target_pairs={{0,2},{2,4},{4,6},{6,8},{8,10},{10,12},{12,14},{14,0},{1,15},{3,1}... | collective-permute-start | bytes 491528 | tf_op jit(solution)/shard_map/ppermute | solution.py:82
  22.1 4.0 %collective-permute-start.8 = (bf16[640,128]{1,0:T(8,128)(2,1)S(1)}, bf16[640,128]{1,0:T(8,128)(2,1)S(1)}, u32[]{:S(2)}, u32[]{:S(2)}) collective-permute-start(bf16[640,128]{1,0:T(8,128)(2,1)S(1)} %get-tuple-element.14), channel_id=1, source_target_pairs={{0,4},{2,6},{4,8},{6,10},{8,12},{10,14},{12,0},{14,2},{1,13},{3,15... | collective-permute-start | bytes 491528 | tf_op jit(solution)/shard_map/ppermute | solution.py:82
  28.1 6.5 %collective-permute-start.10 = (bf16[320,128]{1,0:T(8,128)(2,1)S(1)}, bf16[320,128]{1,0:T(8,128)(2,1)S(1)}, u32[]{:S(2)}, u32[]{:S(2)}) collective-permute-start(bf16[320,128]{1,0:T(8,128)(2,1)S(1)} %dynamic-slice_bitcast_fusion.4), channel_id=1, source_target_pairs={{0,8},{2,10},{4,12},{6,14},{8,0},{10,2},{12,4},{14,6},{1,9},{3,11}... | collective-permute-start | bytes 245768 | tf_op jit(solution)/shard_map/ppermute | solution.py:86
  34.6 9.6 %collective-permute-done.10.fourth = bf16[320,128]{1,0:T(8,128)(2,1)S(1)} collective-permute-done((bf16[320,128]{1,0:T(8,128)(2,1)S(1)}, bf16[320,128]{1,0:T(8,128)(2,1)S(1)}, u32[]{:S(2)}, u32[]{:S(2)}) %collective-permute-start.10) | collective-permute-done | bytes 81952 | tf_op jit(solution)/shard_map/ppermute | solution.py:86
  50.5 3.5 %constant_dynamic-slice_fusion = (bf16[1,640,2,128]{3,2,1,0:T(2,128)(2,1)S(1)}, bf16[1,640,2,128]{3,2,1,0:T(2,128)(2,1)S(1)}, bf16[1,640,2,128]{3,2,1,0:T(2,128)...) fusion(bf16[8,640,2,128]{3,2,1,0:T(2,128)(2,1)} %bitcast.119, ...), kind=kLoop, calls=%fused_computation.85 | loop fusion | bytes 5242912 | tf_op jit(solution)/shard_map/jit(dynamic_index_in_dim)/dynamic_slice | solution.py:148
  54.0 11.1 %collective-permute-done.11.other = bf16[2240,128]{1,0:T(8,128)(2,1)} collective-permute-done((bf16[2240,128]{1,0:T(8,128)(2,1)}, bf16[2240,128]{1,0:T(8,128)(2,1)}, u32[]{:S(2)}, u32[]{:S(2)}) %collective-permute-start.11) | collective-permute-done | bytes 573472 | tf_op jit(solution)/shard_map/ppermute | solution.py:95
  69.9 4.0 %collective-permute-start = (bf16[288,640]{1,0:T(8,128)(2,1)S(1)}, bf16[288,640]{1,0:T(8,128)(2,1)S(1)}, u32[]{:S(2)}, u32[]{:S(2)}) collective-permute-start(bf16[288,640]{1,0:T(8,128)(2,1)S(1)} %get-tuple-element.17), channel_id=1, source_target_pairs={{0,2},{2,4},{4,6},{6,8},{8,10},{10,12},{12,14},{14,0},{1,3},{3,5},... | collective-permute-start | bytes 1105928 | tf_op jit(solution)/shard_map/ppermute | solution.py:28
  73.9 3.1 %collective-permute-start.1 = (bf16[288,640]{1,0:T(8,128)(2,1)S(1)}, bf16[288,640]{1,0:T(8,128)(2,1)S(1)}, u32[]{:S(2)}, u32[]{:S(2)}) collective-permute-start(bf16[288,640]{1,0:T(8,128)(2,1)S(1)} %get-tuple-element.17), channel_id=1, source_target_pairs={{0,14},{2,0},{4,2},{6,4},{8,6},{10,8},{12,10},{14,12},{1,15},{3,1}... | collective-permute-start | bytes 1105928 | tf_op jit(solution)/shard_map/ppermute | solution.py:29
  77.0 3.3 %collective-permute-start.12 = (bf16[288,640]{1,0:T(8,128)(2,1)S(1)}, bf16[288,640]{1,0:T(8,128)(2,1)S(1)}, u32[]{:S(2)}, u32[]{:S(2)}) collective-permute-start(bf16[288,640]{1,0:T(8,128)(2,1)S(1)} %get-tuple-element.18), channel_id=1, source_target_pairs={{0,2},{2,4},{4,6},{6,8},{8,10},{10,12},{12,14},{14,0},{1,3},{3,5},... | collective-permute-start | bytes 1105928 | tf_op jit(solution)/shard_map/ppermute | solution.py:28
  80.2 3.8 %collective-permute-start.13 = (bf16[288,640]{1,0:T(8,128)(2,1)S(1)}, bf16[288,640]{1,0:T(8,128)(2,1)S(1)}, u32[]{:S(2)}, u32[]{:S(2)}) collective-permute-start(bf16[288,640]{1,0:T(8,128)(2,1)S(1)} %get-tuple-element.18), channel_id=1, source_target_pairs={{0,14},{2,0},{4,2},{6,4},{8,6},{10,8},{12,10},{14,12},{1,15},{3,1}... | collective-permute-start | bytes 1105928 | tf_op jit(solution)/shard_map/ppermute | solution.py:29
  84.6 3.1 %collective-permute-done.1 = bf16[288,640]{1,0:T(8,128)(2,1)S(1)} collective-permute-done((bf16[288,640]{1,0:T(8,128)(2,1)S(1)}, bf16[288,640]{1,0:T(8,128)(2,1)S(1)}, u32[]{:S(2)}, u32[]{:S(2)}) %collective-permute-start.1) | collective-permute-done | bytes 368672 | tf_op jit(solution)/shard_map/ppermute | solution.py:29
  87.7 3.1 %collective-permute-start.3 = (bf16[288,640]{1,0:T(8,128)(2,1)S(1)}, bf16[288,640]{1,0:T(8,128)(2,1)S(1)}, u32[]{:S(2)}, u32[]{:S(2)}) collective-permute-start(bf16[288,640]{1,0:T(8,128)(2,1)S(1)} %collective-permute-done.1), channel_id=1, source_target_pairs={{0,14},{2,0},{4,2},{6,4},{8,6},{10,8},{12,10},{14,12},{1,15},{3,1}... | collective-permute-start | bytes 1105928 | tf_op jit(solution)/shard_map/ppermute | solution.py:29
  90.8 2.8 %collective-permute-start.2 = (bf16[288,640]{1,0:T(8,128)(2,1)S(1)}, bf16[288,640]{1,0:T(8,128)(2,1)S(1)}, u32[]{:S(2)}, u32[]{:S(2)}) collective-permute-start(bf16[288,640]{1,0:T(8,128)(2,1)S(1)} %collective-permute-done), channel_id=1, source_target_pairs={{0,2},{2,4},{4,6},{6,8},{8,10},{10,12},{12,14},{14,0},{1,3},{3,5},... | collective-permute-start | bytes 1105928 | tf_op jit(solution)/shard_map/ppermute | solution.py:28
  93.6 3.9 %collective-permute-start.14 = (bf16[288,640]{1,0:T(8,128)(2,1)S(1)}, bf16[288,640]{1,0:T(8,128)(2,1)S(1)}, u32[]{:S(2)}, u32[]{:S(2)}) collective-permute-start(bf16[288,640]{1,0:T(8,128)(2,1)S(1)} %collective-permute-done.12), channel_id=1, source_target_pairs={{0,2},{2,4},{4,6},{6,8},{8,10},{10,12},{12,14},{14,0},{1,3},{3,5},... | collective-permute-start | bytes 1105928 | tf_op jit(solution)/shard_map/ppermute | solution.py:28
  98.1 3.1 %collective-permute-start.15 = (bf16[288,640]{1,0:T(8,128)(2,1)S(1)}, bf16[288,640]{1,0:T(8,128)(2,1)S(1)}, u32[]{:S(2)}, u32[]{:S(2)}) collective-permute-start(bf16[288,640]{1,0:T(8,128)(2,1)S(1)} %collective-permute-done.13), channel_id=1, source_target_pairs={{0,14},{2,0},{4,2},{6,4},{8,6},{10,8},{12,10},{14,12},{1,15},{3,1}... | collective-permute-start | bytes 1105928 | tf_op jit(solution)/shard_map/ppermute | solution.py:29
  103.5 3.1 %collective-permute-start.5 = (bf16[288,640]{1,0:T(8,128)(2,1)S(1)}, bf16[288,640]{1,0:T(8,128)(2,1)S(1)}, u32[]{:S(2)}, u32[]{:S(2)}) collective-permute-start(bf16[288,640]{1,0:T(8,128)(2,1)S(1)} %collective-permute-done.3), channel_id=1, source_target_pairs={{0,14},{2,0},{4,2},{6,4},{8,6},{10,8},{12,10},{14,12},{1,15},{3,1}... | collective-permute-start | bytes 1105928 | tf_op jit(solution)/shard_map/ppermute | solution.py:29
  111.5 4.3 %collective-permute-start.17 = (bf16[288,640]{1,0:T(8,128)(2,1)S(1)}, bf16[288,640]{1,0:T(8,128)(2,1)}, u32[]{:S(2)}, u32[]{:S(2)}) collective-permute-start(bf16[288,640]{1,0:T(8,128)(2,1)S(1)} %collective-permute-done.15), channel_id=1, source_target_pairs={{0,14},{2,0},{4,2},{6,4},{8,6},{10,8},{12,10},{14,12},{1,15},{3,1}... | collective-permute-start | bytes 1105928 | tf_op jit(solution)/shard_map/ppermute | solution.py:29
  119.0 3.5 %collective-permute-start.6 = (bf16[288,640]{1,0:T(8,128)(2,1)S(1)}, bf16[288,640]{1,0:T(8,128)(2,1)S(1)}, u32[]{:S(2)}, u32[]{:S(2)}) collective-permute-start(bf16[288,640]{1,0:T(8,128)(2,1)S(1)} %collective-permute-done.4), channel_id=1, source_target_pairs={{0,2},{2,4},{4,6},{6,8},{8,10},{10,12},{12,14},{14,0},{1,3},{3,5},... | collective-permute-start | bytes 1105928 | tf_op jit(solution)/shard_map/ppermute | solution.py:32
  125.2 3.8 %collective-permute-start.18 = (bf16[288,640]{1,0:T(8,128)(2,1)}, bf16[288,640]{1,0:T(8,128)(2,1)}, u32[]{:S(2)}, u32[]{:S(2)}) collective-permute-start(bf16[288,640]{1,0:T(8,128)(2,1)} %collective-permute-done.17), channel_id=1, source_target_pairs={{0,14},{2,0},{4,2},{6,4},{8,6},{10,8},{12,10},{14,12},{1,15},{3,1}... | collective-permute-start | bytes 1105928 | tf_op jit(solution)/shard_map/ppermute | solution.py:32
  134.3 3.5 %all-to-all-start.1 = ((bf16[8,288,128]{2,1,0:T(8,128)(2,1)}), bf16[8,288,128]{2,1,0:T(8,128)(2,1)S(1)}, u32[]{:S(2)}, u32[]{:S(2)}) async-start(bf16[8,288,128]{2,1,0:T(8,128)(2,1)} %broadcast_in_dim.88), calls=%async_computation.1 | async-start | bytes 1179648 | tf_op jit(solution)/shard_map/all_to_all | solution.py:157
  140.6 30.2 %all-gather = bf16[2304,128]{1,0:T(8,128)(2,1)S(1)} all-gather(bf16[288,128]{1,0:T(8,128)(2,1)S(1)} %fusion.47), channel_id=2, replica_groups=mesh['expert_0'=4,'expert_1'=4,'expert_2'=2,'tensor'=8,'dp'=2] {'tensor'}, dimensions={0}, use_global_device_ids=true | all-gather | bytes 663552 | tf_op jit(solution)/shard_map/all_gather | solution.py:158
  173.4 9.6 %all-to-all-start.2 = ((bf16[32,9,2,640]{3,2,1,0:T(2,128)(2,1)}), bf16[32,9,2,640]{3,2,1,0:T(2,128)(2,1)S(1)}, u32[]{:S(2)}, u32[]{:S(2)}) async-start(bf16[32,9,2,640]{3,2,1,0:T(2,128)(2,1)} %reshape.119), calls=%async_computation.2 | async-start | bytes 1474560 | tf_op jit(solution)/shard_map/all_to_all | solution.py:136
  183.2 23.3 %all-to-all-done.2 = bf16[32,9,2,640]{3,2,1,0:T(2,128)(2,1)S(1)} async-done(((bf16[32,9,2,640]{3,2,1,0:T(2,128)(2,1)}), bf16[32,9,2,640]{3,2,1,0:T(2,128)(2,1)S(1)}, u32[]{:S(2)}, u32[]{:S(2)}) %all-to-all-start.2) | async-done | bytes 737312 | tf_op jit(solution)/shard_map/all_to_all | solution.py:136
  (86 shorter events, 43.5 us)
Async XLA Ops:
  3.7 63.8 %all-to-all-start = ((bf16[32,9,2,640]{3,2,1,0:T(2,128)(2,1)}), bf16[32,9,2,640]{3,2,1,0:T(2,128)(2,1)S(1)}, u32[]{:S(2)}, u32[]{:S(2)}) async-start(bf16[32,9,2,640]{3,2,1,0:T(2,128)(2,1)} %reshape.107), calls=%async_computation | async-start | bytes 1474560 | tf_op jit(solution)/shard_map/all_to_all | solution.py:136
  16.7 27.5 %collective-permute-start.7 = (bf16[640,128]{1,0:T(8,128)(2,1)S(1)}, bf16[640,128]{1,0:T(8,128)(2,1)S(1)}, u32[]{:S(2)}, u32[]{:S(2)}) collective-permute-start(bf16[640,128]{1,0:T(8,128)(2,1)S(1)} %get-tuple-element.15), channel_id=1, source_target_pairs={{0,2},{2,4},{4,6},{6,8},{8,10},{10,12},{12,14},{14,0},{1,15},{3,1}... | collective-permute-start | bytes 491528 | tf_op jit(solution)/shard_map/ppermute | solution.py:82
  22.1 22.1 %collective-permute-start.8 = (bf16[640,128]{1,0:T(8,128)(2,1)S(1)}, bf16[640,128]{1,0:T(8,128)(2,1)S(1)}, u32[]{:S(2)}, u32[]{:S(2)}) collective-permute-start(bf16[640,128]{1,0:T(8,128)(2,1)S(1)} %get-tuple-element.14), channel_id=1, source_target_pairs={{0,4},{2,6},{4,8},{6,10},{8,12},{10,14},{12,0},{14,2},{1,13},{3,15... | collective-permute-start | bytes 491528 | tf_op jit(solution)/shard_map/ppermute | solution.py:82
  26.1 19.2 %collective-permute-start.9 = (bf16[640,128]{1,0:T(8,128)(2,1)S(1)}, bf16[640,128]{1,0:T(8,128)(2,1)S(1)}, u32[]{:S(2)}, u32[]{:S(2)}) collective-permute-start(bf16[640,128]{1,0:T(8,128)(2,1)S(1)} %get-tuple-element.13), channel_id=1, source_target_pairs={{0,10},{2,12},{4,14},{6,0},{8,2},{10,4},{12,6},{14,8},{1,7},{3,9},... | collective-permute-start | bytes 491528 | tf_op jit(solution)/shard_map/ppermute | solution.py:82
  28.1 16.1 %collective-permute-start.10 = (bf16[320,128]{1,0:T(8,128)(2,1)S(1)}, bf16[320,128]{1,0:T(8,128)(2,1)S(1)}, u32[]{:S(2)}, u32[]{:S(2)}) collective-permute-start(bf16[320,128]{1,0:T(8,128)(2,1)S(1)} %dynamic-slice_bitcast_fusion.4), channel_id=1, source_target_pairs={{0,8},{2,10},{4,12},{6,14},{8,0},{10,2},{12,4},{14,6},{1,9},{3,11}... | collective-permute-start | bytes 245768 | tf_op jit(solution)/shard_map/ppermute | solution.py:86
  47.9 17.1 %collective-permute-start.11 = (bf16[2240,128]{1,0:T(8,128)(2,1)}, bf16[2240,128]{1,0:T(8,128)(2,1)}, u32[]{:S(2)}, u32[]{:S(2)}) collective-permute-start(bf16[2240,128]{1,0:T(8,128)(2,1)} %pack.1.mine), channel_id=1, source_target_pairs={{0,1},{1,0},{2,3},{3,2},{4,5},{5,4},{6,7},{7,6},{8,9},{9,8},{10,11... | collective-permute-start | bytes 1720328 | tf_op jit(solution)/shard_map/ppermute | solution.py:95
  68.7 15.4 %copy-start.1 = (bf16[576,640]{1,0:T(8,128)(2,1)S(1)}, bf16[576,640]{1,0:T(8,128)(2,1)}, u32[]{:S(2)}) copy-start(bf16[576,640]{1,0:T(8,128)(2,1)} %reshape.108) | copy-start | bytes 2211844
  69.9 20.9 %collective-permute-start = (bf16[288,640]{1,0:T(8,128)(2,1)S(1)}, bf16[288,640]{1,0:T(8,128)(2,1)S(1)}, u32[]{:S(2)}, u32[]{:S(2)}) collective-permute-start(bf16[288,640]{1,0:T(8,128)(2,1)S(1)} %get-tuple-element.17), channel_id=1, source_target_pairs={{0,2},{2,4},{4,6},{6,8},{8,10},{10,12},{12,14},{14,0},{1,3},{3,5},... | collective-permute-start | bytes 1105928 | tf_op jit(solution)/shard_map/ppermute | solution.py:28
  73.9 13.9 %collective-permute-start.1 = (bf16[288,640]{1,0:T(8,128)(2,1)S(1)}, bf16[288,640]{1,0:T(8,128)(2,1)S(1)}, u32[]{:S(2)}, u32[]{:S(2)}) collective-permute-start(bf16[288,640]{1,0:T(8,128)(2,1)S(1)} %get-tuple-element.17), channel_id=1, source_target_pairs={{0,14},{2,0},{4,2},{6,4},{8,6},{10,8},{12,10},{14,12},{1,15},{3,1}... | collective-permute-start | bytes 1105928 | tf_op jit(solution)/shard_map/ppermute | solution.py:29
  77.0 16.6 %collective-permute-start.12 = (bf16[288,640]{1,0:T(8,128)(2,1)S(1)}, bf16[288,640]{1,0:T(8,128)(2,1)S(1)}, u32[]{:S(2)}, u32[]{:S(2)}) collective-permute-start(bf16[288,640]{1,0:T(8,128)(2,1)S(1)} %get-tuple-element.18), channel_id=1, source_target_pairs={{0,2},{2,4},{4,6},{6,8},{8,10},{10,12},{12,14},{14,0},{1,3},{3,5},... | collective-permute-start | bytes 1105928 | tf_op jit(solution)/shard_map/ppermute | solution.py:28
  80.2 17.9 %collective-permute-start.13 = (bf16[288,640]{1,0:T(8,128)(2,1)S(1)}, bf16[288,640]{1,0:T(8,128)(2,1)S(1)}, u32[]{:S(2)}, u32[]{:S(2)}) collective-permute-start(bf16[288,640]{1,0:T(8,128)(2,1)S(1)} %get-tuple-element.18), channel_id=1, source_target_pairs={{0,14},{2,0},{4,2},{6,4},{8,6},{10,8},{12,10},{14,12},{1,15},{3,1}... | collective-permute-start | bytes 1105928 | tf_op jit(solution)/shard_map/ppermute | solution.py:29
  87.7 15.8 %collective-permute-start.3 = (bf16[288,640]{1,0:T(8,128)(2,1)S(1)}, bf16[288,640]{1,0:T(8,128)(2,1)S(1)}, u32[]{:S(2)}, u32[]{:S(2)}) collective-permute-start(bf16[288,640]{1,0:T(8,128)(2,1)S(1)} %collective-permute-done.1), channel_id=1, source_target_pairs={{0,14},{2,0},{4,2},{6,4},{8,6},{10,8},{12,10},{14,12},{1,15},{3,1}... | collective-permute-start | bytes 1105928 | tf_op jit(solution)/shard_map/ppermute | solution.py:29
  90.8 15.8 %collective-permute-start.2 = (bf16[288,640]{1,0:T(8,128)(2,1)S(1)}, bf16[288,640]{1,0:T(8,128)(2,1)S(1)}, u32[]{:S(2)}, u32[]{:S(2)}) collective-permute-start(bf16[288,640]{1,0:T(8,128)(2,1)S(1)} %collective-permute-done), channel_id=1, source_target_pairs={{0,2},{2,4},{4,6},{6,8},{8,10},{10,12},{12,14},{14,0},{1,3},{3,5},... | collective-permute-start | bytes 1105928 | tf_op jit(solution)/shard_map/ppermute | solution.py:28
  93.6 22.5 %collective-permute-start.14 = (bf16[288,640]{1,0:T(8,128)(2,1)S(1)}, bf16[288,640]{1,0:T(8,128)(2,1)S(1)}, u32[]{:S(2)}, u32[]{:S(2)}) collective-permute-start(bf16[288,640]{1,0:T(8,128)(2,1)S(1)} %collective-permute-done.12), channel_id=1, source_target_pairs={{0,2},{2,4},{4,6},{6,8},{8,10},{10,12},{12,14},{14,0},{1,3},{3,5},... | collective-permute-start | bytes 1105928 | tf_op jit(solution)/shard_map/ppermute | solution.py:28
  98.1 13.4 %collective-permute-start.15 = (bf16[288,640]{1,0:T(8,128)(2,1)S(1)}, bf16[288,640]{1,0:T(8,128)(2,1)S(1)}, u32[]{:S(2)}, u32[]{:S(2)}) collective-permute-start(bf16[288,640]{1,0:T(8,128)(2,1)S(1)} %collective-permute-done.13), channel_id=1, source_target_pairs={{0,14},{2,0},{4,2},{6,4},{8,6},{10,8},{12,10},{14,12},{1,15},{3,1}... | collective-permute-start | bytes 1105928 | tf_op jit(solution)/shard_map/ppermute | solution.py:29
  103.5 26.8 %collective-permute-start.5 = (bf16[288,640]{1,0:T(8,128)(2,1)S(1)}, bf16[288,640]{1,0:T(8,128)(2,1)S(1)}, u32[]{:S(2)}, u32[]{:S(2)}) collective-permute-start(bf16[288,640]{1,0:T(8,128)(2,1)S(1)} %collective-permute-done.3), channel_id=1, source_target_pairs={{0,14},{2,0},{4,2},{6,4},{8,6},{10,8},{12,10},{14,12},{1,15},{3,1}... | collective-permute-start | bytes 1105928 | tf_op jit(solution)/shard_map/ppermute | solution.py:29
  106.6 12.3 %collective-permute-start.4 = (bf16[288,640]{1,0:T(8,128)(2,1)S(1)}, bf16[288,640]{1,0:T(8,128)(2,1)S(1)}, u32[]{:S(2)}, u32[]{:S(2)}) collective-permute-start(bf16[288,640]{1,0:T(8,128)(2,1)S(1)} %collective-permute-done.2), channel_id=1, source_target_pairs={{0,2},{2,4},{4,6},{6,8},{8,10},{10,12},{12,14},{14,0},{1,3},{3,5},... | collective-permute-start | bytes 1105928 | tf_op jit(solution)/shard_map/ppermute | solution.py:28
  111.5 13.7 %collective-permute-start.17 = (bf16[288,640]{1,0:T(8,128)(2,1)S(1)}, bf16[288,640]{1,0:T(8,128)(2,1)}, u32[]{:S(2)}, u32[]{:S(2)}) collective-permute-start(bf16[288,640]{1,0:T(8,128)(2,1)S(1)} %collective-permute-done.15), channel_id=1, source_target_pairs={{0,14},{2,0},{4,2},{6,4},{8,6},{10,8},{12,10},{14,12},{1,15},{3,1}... | collective-permute-start | bytes 1105928 | tf_op jit(solution)/shard_map/ppermute | solution.py:29
  116.1 21.7 %collective-permute-start.16 = (bf16[288,640]{1,0:T(8,128)(2,1)S(1)}, bf16[288,640]{1,0:T(8,128)(2,1)}, u32[]{:S(2)}, u32[]{:S(2)}) collective-permute-start(bf16[288,640]{1,0:T(8,128)(2,1)S(1)} %collective-permute-done.14), channel_id=1, source_target_pairs={{0,2},{2,4},{4,6},{6,8},{8,10},{10,12},{12,14},{14,0},{1,3},{3,5},... | collective-permute-start | bytes 1105928 | tf_op jit(solution)/shard_map/ppermute | solution.py:28
  119.0 14.1 %collective-permute-start.6 = (bf16[288,640]{1,0:T(8,128)(2,1)S(1)}, bf16[288,640]{1,0:T(8,128)(2,1)S(1)}, u32[]{:S(2)}, u32[]{:S(2)}) collective-permute-start(bf16[288,640]{1,0:T(8,128)(2,1)S(1)} %collective-permute-done.4), channel_id=1, source_target_pairs={{0,2},{2,4},{4,6},{6,8},{8,10},{10,12},{12,14},{14,0},{1,3},{3,5},... | collective-permute-start | bytes 1105928 | tf_op jit(solution)/shard_map/ppermute | solution.py:32
  125.2 14.0 %collective-permute-start.18 = (bf16[288,640]{1,0:T(8,128)(2,1)}, bf16[288,640]{1,0:T(8,128)(2,1)}, u32[]{:S(2)}, u32[]{:S(2)}) collective-permute-start(bf16[288,640]{1,0:T(8,128)(2,1)} %collective-permute-done.17), channel_id=1, source_target_pairs={{0,14},{2,0},{4,2},{6,4},{8,6},{10,8},{12,10},{14,12},{1,15},{3,1}... | collective-permute-start | bytes 1105928 | tf_op jit(solution)/shard_map/ppermute | solution.py:32
  134.3 37.2 %all-to-all-start.1 = ((bf16[8,288,128]{2,1,0:T(8,128)(2,1)}), bf16[8,288,128]{2,1,0:T(8,128)(2,1)S(1)}, u32[]{:S(2)}, u32[]{:S(2)}) async-start(bf16[8,288,128]{2,1,0:T(8,128)(2,1)} %broadcast_in_dim.88), calls=%async_computation.1 | async-start | bytes 1179648 | tf_op jit(solution)/shard_map/all_to_all | solution.py:157
  139.2 31.7 %copy-start.2 = (bf16[8,640,128]{2,1,0:T(8,128)(2,1)S(1)}, bf16[8,640,128]{2,1,0:T(8,128)(2,1)}, u32[]{:S(2)}) copy-start(bf16[8,640,128]{2,1,0:T(8,128)(2,1)} %place.1) | copy-start | bytes 3932164
  173.4 33.1 %all-to-all-start.2 = ((bf16[32,9,2,640]{3,2,1,0:T(2,128)(2,1)}), bf16[32,9,2,640]{3,2,1,0:T(2,128)(2,1)S(1)}, u32[]{:S(2)}, u32[]{:S(2)}) async-start(bf16[32,9,2,640]{3,2,1,0:T(2,128)(2,1)} %reshape.119), calls=%async_computation.2 | async-start | bytes 1474560 | tf_op jit(solution)/shard_map/all_to_all | solution.py:136
  (7 other events, 30.3 us)

commit v5 on v4

--- a/solution.py
+++ b/solution.py
@@ -21,16 +21,36 @@
     return [(i, (i + step) % size) for i in range(size)]
 
 
-def ring(x, size, last, use):
-    use(x, 0)
+def hops(x, size, last):
+    found = [(0, x)]
     up = down = x
     for step in range(1, size // 2):
         up = lax.ppermute(up, "tensor", shift(size, 1))
         down = lax.ppermute(down, "tensor", shift(size, -1))
-        use(up, -step)
-        use(down, step)
-    far = lax.ppermute(up if last > 0 else down, "tensor", shift(size, last))
-    use(far, size // 2)
+        found += [(-step, up), (step, down)]
+    found.append((size // 2, lax.ppermute(up if last > 0 else down, "tensor", shift(size, last))))
+    return found
+
+
+def product_of(me, size, distances, blocks, weight):
+    return sum(
+        jnp.dot(x[...], weight[lax.rem(me + d + size, size)], preferred_element_type=jnp.float32)
+        for d, x in zip(distances, blocks)
+    )
+
+
+def first_kernel(size, distances, place, weight, *refs):
+    count = len(distances)
+    for chain in range(2):
+        blocks = refs[chain * count : (chain + 1) * count]
+        refs[2 * count + chain][...] = product_of(place[0], size, distances, blocks, weight)
+
+
+def last_kernel(size, distances, place, weight, begun, *refs):
+    *blocks, out = refs
+    total = begun[...] + product_of(place[0], size, distances, blocks, weight)
+    gate, up = total[:, : total.shape[1] // 2], total[:, total.shape[1] // 2 :]
+    out[...] = (gate / (1.0 + jnp.exp(-gate)) * up).astype(out.dtype)
 
 
 def pack_kernel(first, second, third, fourth, out):
@@ -69,7 +89,7 @@
         fill(other, mine)
 
 
-def down_rows(down_weight, size, part, hidden):
+def down_rows(down_weight, after, place, size, part, hidden):
     me, pair = lax.axis_index("tensor"), lax.axis_index("dp")
     blocks = down_weight.reshape(size, part, hidden)
     steps = ((1, 2, -3), (-1, -2, 3))
@@ -92,15 +112,17 @@
         out_specs=vmem,
         name="pack",
     )(*got)
+    mine, after = lax.optimization_barrier((mine, after))
     other = lax.ppermute(mine, "dp", [(0, 1), (1, 0)])
     own = lax.dynamic_index_in_dim(blocks, me, 0, keepdims=False)
-    return pl.pallas_call(
+    placed = pl.pallas_call(
         functools.partial(place_kernel, size),
         out_shape=jax.ShapeDtypeStruct(blocks.shape, blocks.dtype),
         in_specs=[pl.BlockSpec(memory_space=pltpu.SMEM)] + [vmem] * 3,
         out_specs=vmem,
         name="place",
-    )(jnp.stack([me, pair]).astype(jnp.int32), own, mine, other)
+    )(place, own, mine, other)
+    return placed, after
 
 
 def local(tokens, routes, gates, gate_up, down_weight, old_map, new_map):
@@ -137,25 +159,34 @@
         return x.reshape(rows, part)
 
     arrived = lax.optimization_barrier(exchange(outgoing))
-    down_mine = down_rows(down_weight, size, part, hidden)
-
-    weight_in = gate_up.reshape(size, part, 2, hidden)
-
-    def projected(x, last):
-        pieces = []
-
-        def use(block, distance):
-            w = lax.dynamic_index_in_dim(weight_in, lax.rem(me + distance + size, size), 0, keepdims=False)
-            pieces.append(dot(block, w.reshape(part, 2 * hidden)))
-
-        ring(x, size, last, use)
-        total = sum(pieces)
-        return (jax.nn.silu(total[:, :hidden]) * total[:, hidden:]).astype(bf16)
-
-    half = rows // 2
-    act_a, act_b = projected(arrived[:half], 1), projected(arrived[half:], -1)
-    all_a = lax.all_to_all(jnp.broadcast_to(act_a[None], (size, half, hidden)), "tensor", 0, 0, tiled=True)
-    all_b = lax.all_gather(act_b, "tensor")
+    place = jnp.stack([me, lax.axis_index("dp")]).astype(jnp.int32)
+    down_mine, weight_in = down_rows(down_weight, gate_up, place, size, part, hidden)
+
+    chains = [hops(arrived[: rows // 2], size, 1), hops(arrived[rows // 2 :], size, -1)]
+    weight_in = weight_in.reshape(size, part, 2 * hidden)
+    early = 5
+    smem, vmem = pl.BlockSpec(memory_space=pltpu.SMEM), pl.BlockSpec(memory_space=pltpu.VMEM)
+    begun = pl.pallas_call(
+        functools.partial(first_kernel, size, [d for d, _ in chains[0][:early]]),
+        out_shape=[jax.ShapeDtypeStruct((rows // 2, 2 * hidden), jnp.float32)] * 2,
+        in_specs=[smem] + [vmem] * (1 + 2 * early),
+        out_specs=[vmem] * 2,
+        name="first",
+    )(place, weight_in, *(x for chain in chains for _, x in chain[:early]))
+
+    def finished(chain, total):
+        return pl.pallas_call(
+            functools.partial(last_kernel, size, [d for d, _ in chain[early:]]),
+            out_shape=jax.ShapeDtypeStruct((rows // 2, hidden), bf16),
+            in_specs=[smem] + [vmem] * (2 + len(chain) - early),
+            out_specs=vmem,
+            name="last",
+        )(place, weight_in, total, *(x for _, x in chain[early:]))
+
+    act_a, act_b = finished(chains[0], begun[0]), finished(chains[1], begun[1])
+    some = 136
+    all_a = lax.all_to_all(jnp.broadcast_to(act_a[None, :some], (size, some, hidden)), "tensor", 0, 0, tiled=True)
+    all_b = lax.all_gather(jnp.concatenate([act_a[some:], act_b], axis=0), "tensor")
 
     def outputs(act):
         return dot(act, down_mine, ((0, 2), (0, 2))).astype(bf16)

time: 210 us -> 215 us (1.024)
  the two profiles are of different devices: /device:TPU:64 before, /device:TPU:80 now
where the time goes in v5:
time: 215 us; the launch traced here: 214 us
  starting transfers between devices  70.1 us (33%)
  blocking collectives  62.8 us (29%)
  waiting for transfers between devices  46 us (21%)
  Pallas kernels  16 us (7%)
  local copies, waits for them, and re-layouts  11.5 us (5%)
  matrix products  3.34 us (2%)
  other arithmetic  3.3 us (2%)
    all_to_all x1, blocking collectives, exchange(): x = lax.all_to_all(x, EXPERT, 0, 0, tiled=True)  35.4 us
    all_gather x1, blocking collectives, local(): lax.all_gather(jnp.concatenate([act_a[some:], act_b], axis=0), 'tensor')  27.5 us
    all_to_all x1, waiting for transfers between devices, exchange(): x = lax.all_to_all(x, EXPERT, 0, 0, tiled=True)  22.5 us
    ppermute x6, starting transfers between devices, hops(): up = lax.ppermute(up, 'tensor', shift(size, 1))  19.4 us
    ppermute x3, waiting for transfers between devices, down_rows(): got.append(lax.ppermute(block, ('tensor', 'dp'), perm))  18.9 us
    ppermute x6, starting transfers between devices, hops(): down = lax.ppermute(down, 'tensor', shift(size, -1))  14 us
    ppermute x3, starting transfers between devices, down_rows(): got.append(lax.ppermute(block, ('tensor', 'dp'), perm))  10.3 us
    ppermute x2, starting transfers between devices, hops(): lax.ppermute(up if last > 0 else down, 'tensor', shift(size, last))  7.34 us
  transfers between devices with their start and end apart: 21, of which 6 were waited for; matrix products, arithmetic and copies ran while one was open for 5% of the time, Pallas kernels for 7%

profile of v5, /device:TPU:80, one launch (start us, length us, event | category | flops | bytes accessed | tf_op | source)
XLA Modules:
  0.0 213.5 jit_solution(10149432377393335743)
XLA Ops:
  2.8 35.4 %all_to_all.15 = bf16[32,9,2,640]{3,2,1,0:T(2,128)(2,1)S(1)} all-to-all(bf16[32,9,2,640]{3,2,1,0:T(2,128)(2,1)S(1)} %reshape.69), channel_id=1, replica_groups=mesh['expert_0'=4,'expert_1'=4,'expert_2'=2,'tensor'=8,'dp'=2] {'expert_..., dimensions={0} | all-to-all | bytes 1474560 | tf_op jit(solution)/shard_map/all_to_all | solution.py:158
  40.9 3.5 %collective-permute-start.4 = (bf16[288,640]{1,0:T(8,128)(2,1)S(1)}, bf16[288,640]{1,0:T(8,128)(2,1)}, u32[]{:S(2)}, u32[]{:S(2)}) collective-permute-start(bf16[288,640]{1,0:T(8,128)(2,1)S(1)} %get-tuple-element.18.refs_0_), channel_id=1, source_target_pairs={{0,2},{2,4},{4,6},{6,8},{8,10},{10,12},{12,14},{14,0},{1,3},{3,5},... | collective-permute-start | bytes 1105928 | tf_op jit(solution)/shard_map/ppermute | solution.py:28
  46.1 5.9 %collective-permute-start.3 = (bf16[320,128]{1,0:T(8,128)(2,1)}, bf16[320,128]{1,0:T(8,128)(2,1)}, u32[]{:S(2)}, u32[]{:S(2)}) collective-permute-start(bf16[320,128]{1,0:T(8,128)(2,1)} %dynamic-slice_bitcast_fusion.4), channel_id=1, source_target_pairs={{0,8},{2,10},{4,12},{6,14},{8,0},{10,2},{12,4},{14,6},{1,9},{3,11}... | collective-permute-start | bytes 245768 | tf_op jit(solution)/shard_map/ppermute | solution.py:106
  52.1 3.8 %collective-permute-start.8 = (bf16[288,640]{1,0:T(8,128)(2,1)S(1)}, bf16[288,640]{1,0:T(8,128)(2,1)}, u32[]{:S(2)}, u32[]{:S(2)}) collective-permute-start(bf16[288,640]{1,0:T(8,128)(2,1)S(1)} %get-tuple-element.17.refs_5_), channel_id=1, source_target_pairs={{0,2},{2,4},{4,6},{6,8},{8,10},{10,12},{12,14},{14,0},{1,3},{3,5},... | collective-permute-start | bytes 1105928 | tf_op jit(solution)/shard_map/ppermute | solution.py:28
  58.0 3.3 %collective-permute-start.11 = (bf16[288,640]{1,0:T(8,128)(2,1)}, bf16[288,640]{1,0:T(8,128)(2,1)}, u32[]{:S(2)}, u32[]{:S(2)}) collective-permute-start(bf16[288,640]{1,0:T(8,128)(2,1)} %collective-permute-done.9.refs_7_), channel_id=1, source_target_pairs={{0,14},{2,0},{4,2},{6,4},{8,6},{10,8},{12,10},{14,12},{1,15},{3,1}... | collective-permute-start | bytes 1105928 | tf_op jit(solution)/shard_map/ppermute | solution.py:29
  61.2 2.6 %collective-permute-start.6 = (bf16[288,640]{1,0:T(8,128)(2,1)}, bf16[288,640]{1,0:T(8,128)(2,1)}, u32[]{:S(2)}, u32[]{:S(2)}) collective-permute-start(bf16[288,640]{1,0:T(8,128)(2,1)} %collective-permute-done.4.refs_1_), channel_id=1, source_target_pairs={{0,2},{2,4},{4,6},{6,8},{8,10},{10,12},{12,14},{14,0},{1,3},{3,5},... | collective-permute-start | bytes 1105928 | tf_op jit(solution)/shard_map/ppermute | solution.py:28
  65.7 3.8 %collective-permute-start = (bf16[640,128]{1,0:T(8,128)(2,1)S(1)}, bf16[640,128]{1,0:T(8,128)(2,1)S(1)}, u32[]{:S(2)}, u32[]{:S(2)}) collective-permute-start(bf16[640,128]{1,0:T(8,128)(2,1)S(1)} %get-tuple-element.16), channel_id=1, source_target_pairs={{0,2},{2,4},{4,6},{6,8},{8,10},{10,12},{12,14},{14,0},{1,15},{3,1}... | collective-permute-start | bytes 491528 | tf_op jit(solution)/shard_map/ppermute | solution.py:102
  69.5 9.4 %collective-permute-done.first = bf16[640,128]{1,0:T(8,128)(2,1)S(1)} collective-permute-done((bf16[640,128]{1,0:T(8,128)(2,1)S(1)}, bf16[640,128]{1,0:T(8,128)(2,1)S(1)}, u32[]{:S(2)}, u32[]{:S(2)}) %collective-permute-start) | collective-permute-done | bytes 163872 | tf_op jit(solution)/shard_map/ppermute | solution.py:102
  78.9 2.9 %collective-permute-start.1 = (bf16[640,128]{1,0:T(8,128)(2,1)S(1)}, bf16[640,128]{1,0:T(8,128)(2,1)S(1)}, u32[]{:S(2)}, u32[]{:S(2)}) collective-permute-start(bf16[640,128]{1,0:T(8,128)(2,1)S(1)} %get-tuple-element.15), channel_id=1, source_target_pairs={{0,4},{2,6},{4,8},{6,10},{8,12},{10,14},{12,0},{14,2},{1,13},{3,15... | collective-permute-start | bytes 491528 | tf_op jit(solution)/shard_map/ppermute | solution.py:102
  81.8 9.2 %collective-permute-done.1.second = bf16[640,128]{1,0:T(8,128)(2,1)S(1)} collective-permute-done((bf16[640,128]{1,0:T(8,128)(2,1)S(1)}, bf16[640,128]{1,0:T(8,128)(2,1)S(1)}, u32[]{:S(2)}, u32[]{:S(2)}) %collective-permute-start.1) | collective-permute-done | bytes 163872 | tf_op jit(solution)/shard_map/ppermute | solution.py:102
  91.0 3.7 %collective-permute-start.2 = (bf16[640,128]{1,0:T(8,128)(2,1)S(1)}, bf16[640,128]{1,0:T(8,128)(2,1)}, u32[]{:S(2)}, u32[]{:S(2)}) collective-permute-start(bf16[640,128]{1,0:T(8,128)(2,1)S(1)} %get-tuple-element.14), channel_id=1, source_target_pairs={{0,10},{2,12},{4,14},{6,0},{8,2},{10,4},{12,6},{14,8},{1,7},{3,9},... | collective-permute-start | bytes 491528 | tf_op jit(solution)/shard_map/ppermute | solution.py:102
  96.6 3.9 %collective-permute-start.12 = (bf16[288,640]{1,0:T(8,128)(2,1)}, bf16[288,640]{1,0:T(8,128)(2,1)}, u32[]{:S(2)}, u32[]{:S(2)}) collective-permute-start(bf16[288,640]{1,0:T(8,128)(2,1)} %collective-permute-done.6.refs_3_), channel_id=1, source_target_pairs={{0,2},{2,4},{4,6},{6,8},{8,10},{10,12},{12,14},{14,0},{1,3},{3,5},... | collective-permute-start | bytes 1105928 | tf_op jit(solution)/shard_map/ppermute | solution.py:28
  100.5 3.7 %collective-permute-start.10 = (bf16[288,640]{1,0:T(8,128)(2,1)}, bf16[288,640]{1,0:T(8,128)(2,1)}, u32[]{:S(2)}, u32[]{:S(2)}) collective-permute-start(bf16[288,640]{1,0:T(8,128)(2,1)} %collective-permute-done.8.refs_6_), channel_id=1, source_target_pairs={{0,2},{2,4},{4,6},{6,8},{8,10},{10,12},{12,14},{14,0},{1,3},{3,5},... | collective-permute-start | bytes 1105928 | tf_op jit(solution)/shard_map/ppermute | solution.py:28
  113.0 3.5 %collective-permute-start.14 = (bf16[288,640]{1,0:T(8,128)(2,1)}, bf16[288,640]{1,0:T(8,128)(2,1)}, u32[]{:S(2)}, u32[]{:S(2)}) collective-permute-start(bf16[288,640]{1,0:T(8,128)(2,1)} %collective-permute-done.12.refs_0_), channel_id=1, source_target_pairs={{0,2},{2,4},{4,6},{6,8},{8,10},{10,12},{12,14},{14,0},{1,3},{3,5},... | collective-permute-start | bytes 1105928 | tf_op jit(solution)/shard_map/ppermute | solution.py:31
  116.6 4.4 %collective-permute-done.10.refs_8_ = bf16[288,640]{1,0:T(8,128)(2,1)} collective-permute-done((bf16[288,640]{1,0:T(8,128)(2,1)}, bf16[288,640]{1,0:T(8,128)(2,1)}, u32[]{:S(2)}, u32[]{:S(2)}) %collective-permute-start.10) | collective-permute-done | bytes 368672 | tf_op jit(solution)/shard_map/ppermute | solution.py:28
  123.0 3.8 %collective-permute-start.18 = (bf16[288,640]{1,0:T(8,128)(2,1)}, bf16[288,640]{1,0:T(8,128)(2,1)}, u32[]{:S(2)}, u32[]{:S(2)}) collective-permute-start(bf16[288,640]{1,0:T(8,128)(2,1)} %collective-permute-done.17.refs_1_), channel_id=1, source_target_pairs={{0,14},{2,0},{4,2},{6,4},{8,6},{10,8},{12,10},{14,12},{1,15},{3,1}... | collective-permute-start | bytes 1105928 | tf_op jit(solution)/shard_map/ppermute | solution.py:31
  127.4 3.4 %reshape.68.weight = bf16[8,640,256]{2,1,0:T(8,128)(2,1)} reshape(bf16[1,5120,2,128]{3,2,1,0:T(2,128)(2,1)S(1)} %copy-done.2) | data formatting | bytes 5242880 | tf_op jit(solution)/shard_map/reshape | solution.py:166
  133.2 4.9 %first.1 = (f32[288,256]{1,0:T(8,128)}, f32[288,256]{1,0:T(8,128)}) custom-call(s32[2]{0:T(128)} %pad_add_fusion.place, bf16[8,640,256]{2,1,0:T(8,128)(2,1)} %reshape.68.weight, bf16[288,640]{1,0:T(8,128)(2,1)} %copy-done.4, bf16[288,640]{1,0:T(8,128)(2,1)} %collective-permute-done.4.refs_1_, bf16[288,640]{1,0:T(8,128)(2,1)} %collective-permute-done.5.refs_2_, ...), custom_call_target="tpu_custom_call" | custom-call | tf_op jit(solution)/shard_map/first/pallas_call | solution.py:169
  138.2 3.3 %last.2 = bf16[288,128]{1,0:T(8,128)(2,1)} custom-call(s32[2]{0:T(128)} %pad_add_fusion.place, bf16[8,640,256]{2,1,0:T(8,128)(2,1)} %reshape.68.weight, f32[288,256]{1,0:T(8,128)} %get-tuple-element.10.begun, bf16[288,640]{1,0:T(8,128)(2,1)} %collective-permute-done.12.refs_0_, bf16[288,640]{1,0:T(8,128)(2,1)} %collective-permute-done.13.refs_1_, ...), custom_call_target="tpu_custom_call" | custom-call | tf_op jit(solution)/shard_map/last/pallas_call | solution.py:178
  143.0 7.0 %all-to-all-start.1 = ((bf16[8,136,128]{2,1,0:T(8,128)(2,1)}), bf16[8,136,128]{2,1,0:T(8,128)(2,1)S(1)}, u32[]{:S(2)}, u32[]{:S(2)}) async-start(bf16[8,136,128]{2,1,0:T(8,128)(2,1)} %broadcast_in_dim.88), calls=%async_computation.1 | async-start | bytes 557056 | tf_op jit(solution)/shard_map/all_to_all | solution.py:188
  150.7 3.4 %last.3 = bf16[288,128]{1,0:T(8,128)(2,1)} custom-call(s32[2]{0:T(128)} %pad_add_fusion.place, bf16[8,640,256]{2,1,0:T(8,128)(2,1)} %reshape.68.weight, f32[288,256]{1,0:T(8,128)} %get-tuple-element.12.begun, bf16[288,640]{1,0:T(8,128)(2,1)} %copy-done.5, bf16[288,640]{1,0:T(8,128)(2,1)} %collective-permute-done.17.refs_1_, ...), custom_call_target="tpu_custom_call" | custom-call | tf_op jit(solution)/shard_map/last/pallas_call | solution.py:178
  155.0 27.5 %all-gather = bf16[3520,128]{1,0:T(8,128)(2,1)S(1)} all-gather(bf16[440,128]{1,0:T(8,128)(2,1)S(1)} %pad_maximum_fusion.1), channel_id=2, replica_groups=mesh['expert_0'=4,'expert_1'=4,'expert_2'=2,'tensor'=8,'dp'=2] {'tensor'}, dimensions={0}, use_global_device_ids=true | all-gather | bytes 1013760 | tf_op jit(solution)/shard_map/all_gather | solution.py:189
  185.2 4.1 %all-to-all-start.2 = ((bf16[32,9,2,640]{3,2,1,0:T(2,128)(2,1)}), bf16[32,9,2,640]{3,2,1,0:T(2,128)(2,1)S(1)}, u32[]{:S(2)}, u32[]{:S(2)}) async-start(bf16[32,9,2,640]{3,2,1,0:T(2,128)(2,1)} %reshape.71), calls=%async_computation.2 | async-start | bytes 1474560 | tf_op jit(solution)/shard_map/all_to_all | solution.py:158
  189.4 22.5 %all-to-all-done.2 = bf16[32,9,2,640]{3,2,1,0:T(2,128)(2,1)S(1)} async-done(((bf16[32,9,2,640]{3,2,1,0:T(2,128)(2,1)}), bf16[32,9,2,640]{3,2,1,0:T(2,128)(2,1)S(1)}, u32[]{:S(2)}, u32[]{:S(2)}) %all-to-all-start.2) | async-done | bytes 737312 | tf_op jit(solution)/shard_map/all_to_all | solution.py:158
  (74 shorter events, 34.4 us)
Async XLA Ops:
  38.5 70.2 %copy-start.3 = (bf16[288,640]{1,0:T(8,128)(2,1)}, bf16[288,640]{1,0:T(8,128)(2,1)S(1)}, u32[]{:S(2)}) copy-start(bf16[288,640]{1,0:T(8,128)(2,1)S(1)} %get-tuple-element.17.refs_5_) | copy-start | bytes 1105924
  38.5 70.2 %copy-start.4 = (bf16[288,640]{1,0:T(8,128)(2,1)}, bf16[288,640]{1,0:T(8,128)(2,1)S(1)}, u32[]{:S(2)}) copy-start(bf16[288,640]{1,0:T(8,128)(2,1)S(1)} %get-tuple-element.18.refs_0_) | copy-start | bytes 1105924
  38.5 19.4 %collective-permute-start.9 = (bf16[288,640]{1,0:T(8,128)(2,1)S(1)}, bf16[288,640]{1,0:T(8,128)(2,1)}, u32[]{:S(2)}, u32[]{:S(2)}) collective-permute-start(bf16[288,640]{1,0:T(8,128)(2,1)S(1)} %get-tuple-element.17.refs_5_), channel_id=1, source_target_pairs={{0,14},{2,0},{4,2},{6,4},{8,6},{10,8},{12,10},{14,12},{1,15},{3,1}... | collective-permute-start | bytes 1105928 | tf_op jit(solution)/shard_map/ppermute | solution.py:29
  40.9 20.3 %collective-permute-start.4 = (bf16[288,640]{1,0:T(8,128)(2,1)S(1)}, bf16[288,640]{1,0:T(8,128)(2,1)}, u32[]{:S(2)}, u32[]{:S(2)}) collective-permute-start(bf16[288,640]{1,0:T(8,128)(2,1)S(1)} %get-tuple-element.18.refs_0_), channel_id=1, source_target_pairs={{0,2},{2,4},{4,6},{6,8},{8,10},{10,12},{12,14},{14,0},{1,3},{3,5},... | collective-permute-start | bytes 1105928 | tf_op jit(solution)/shard_map/ppermute | solution.py:28
  44.4 83.0 %copy-start.2 = (bf16[1,5120,2,128]{3,2,1,0:T(2,128)(2,1)S(1)}, bf16[1,5120,2,128]{3,2,1,0:T(2,128)(2,1)}, u32[]{:S(2)}) copy-start(bf16[1,5120,2,128]{3,2,1,0:T(2,128)(2,1)} %param.10) | copy-start | bytes 7864324
  46.1 19.6 %collective-permute-start.3 = (bf16[320,128]{1,0:T(8,128)(2,1)}, bf16[320,128]{1,0:T(8,128)(2,1)}, u32[]{:S(2)}, u32[]{:S(2)}) collective-permute-start(bf16[320,128]{1,0:T(8,128)(2,1)} %dynamic-slice_bitcast_fusion.4), channel_id=1, source_target_pairs={{0,8},{2,10},{4,12},{6,14},{8,0},{10,2},{12,4},{14,6},{1,9},{3,11}... | collective-permute-start | bytes 245768 | tf_op jit(solution)/shard_map/ppermute | solution.py:106
  52.1 48.4 %collective-permute-start.8 = (bf16[288,640]{1,0:T(8,128)(2,1)S(1)}, bf16[288,640]{1,0:T(8,128)(2,1)}, u32[]{:S(2)}, u32[]{:S(2)}) collective-permute-start(bf16[288,640]{1,0:T(8,128)(2,1)S(1)} %get-tuple-element.17.refs_5_), channel_id=1, source_target_pairs={{0,2},{2,4},{4,6},{6,8},{8,10},{10,12},{12,14},{14,0},{1,3},{3,5},... | collective-permute-start | bytes 1105928 | tf_op jit(solution)/shard_map/ppermute | solution.py:28
  55.9 38.7 %collective-permute-start.5 = (bf16[288,640]{1,0:T(8,128)(2,1)S(1)}, bf16[288,640]{1,0:T(8,128)(2,1)}, u32[]{:S(2)}, u32[]{:S(2)}) collective-permute-start(bf16[288,640]{1,0:T(8,128)(2,1)S(1)} %get-tuple-element.18.refs_0_), channel_id=1, source_target_pairs={{0,14},{2,0},{4,2},{6,4},{8,6},{10,8},{12,10},{14,12},{1,15},{3,1}... | collective-permute-start | bytes 1105928 | tf_op jit(solution)/shard_map/ppermute | solution.py:29
  58.0 46.3 %collective-permute-start.11 = (bf16[288,640]{1,0:T(8,128)(2,1)}, bf16[288,640]{1,0:T(8,128)(2,1)}, u32[]{:S(2)}, u32[]{:S(2)}) collective-permute-start(bf16[288,640]{1,0:T(8,128)(2,1)} %collective-permute-done.9.refs_7_), channel_id=1, source_target_pairs={{0,14},{2,0},{4,2},{6,4},{8,6},{10,8},{12,10},{14,12},{1,15},{3,1}... | collective-permute-start | bytes 1105928 | tf_op jit(solution)/shard_map/ppermute | solution.py:29
  61.2 35.3 %collective-permute-start.6 = (bf16[288,640]{1,0:T(8,128)(2,1)}, bf16[288,640]{1,0:T(8,128)(2,1)}, u32[]{:S(2)}, u32[]{:S(2)}) collective-permute-start(bf16[288,640]{1,0:T(8,128)(2,1)} %collective-permute-done.4.refs_1_), channel_id=1, source_target_pairs={{0,2},{2,4},{4,6},{6,8},{8,10},{10,12},{12,14},{14,0},{1,3},{3,5},... | collective-permute-start | bytes 1105928 | tf_op jit(solution)/shard_map/ppermute | solution.py:28
  65.7 13.2 %collective-permute-start = (bf16[640,128]{1,0:T(8,128)(2,1)S(1)}, bf16[640,128]{1,0:T(8,128)(2,1)S(1)}, u32[]{:S(2)}, u32[]{:S(2)}) collective-permute-start(bf16[640,128]{1,0:T(8,128)(2,1)S(1)} %get-tuple-element.16), channel_id=1, source_target_pairs={{0,2},{2,4},{4,6},{6,8},{8,10},{10,12},{12,14},{14,0},{1,15},{3,1}... | collective-permute-start | bytes 491528 | tf_op jit(solution)/shard_map/ppermute | solution.py:102
  78.9 12.1 %collective-permute-start.1 = (bf16[640,128]{1,0:T(8,128)(2,1)S(1)}, bf16[640,128]{1,0:T(8,128)(2,1)S(1)}, u32[]{:S(2)}, u32[]{:S(2)}) collective-permute-start(bf16[640,128]{1,0:T(8,128)(2,1)S(1)} %get-tuple-element.15), channel_id=1, source_target_pairs={{0,4},{2,6},{4,8},{6,10},{8,12},{10,14},{12,0},{14,2},{1,13},{3,15... | collective-permute-start | bytes 491528 | tf_op jit(solution)/shard_map/ppermute | solution.py:102
  91.0 15.8 %collective-permute-start.2 = (bf16[640,128]{1,0:T(8,128)(2,1)S(1)}, bf16[640,128]{1,0:T(8,128)(2,1)}, u32[]{:S(2)}, u32[]{:S(2)}) collective-permute-start(bf16[640,128]{1,0:T(8,128)(2,1)S(1)} %get-tuple-element.14), channel_id=1, source_target_pairs={{0,10},{2,12},{4,14},{6,0},{8,2},{10,4},{12,6},{14,8},{1,7},{3,9},... | collective-permute-start | bytes 491528 | tf_op jit(solution)/shard_map/ppermute | solution.py:102
  94.6 16.0 %collective-permute-start.7 = (bf16[288,640]{1,0:T(8,128)(2,1)}, bf16[288,640]{1,0:T(8,128)(2,1)}, u32[]{:S(2)}, u32[]{:S(2)}) collective-permute-start(bf16[288,640]{1,0:T(8,128)(2,1)} %collective-permute-done.5.refs_2_), channel_id=1, source_target_pairs={{0,14},{2,0},{4,2},{6,4},{8,6},{10,8},{12,10},{14,12},{1,15},{3,1}... | collective-permute-start | bytes 1105928 | tf_op jit(solution)/shard_map/ppermute | solution.py:29
  96.6 16.5 %collective-permute-start.12 = (bf16[288,640]{1,0:T(8,128)(2,1)}, bf16[288,640]{1,0:T(8,128)(2,1)}, u32[]{:S(2)}, u32[]{:S(2)}) collective-permute-start(bf16[288,640]{1,0:T(8,128)(2,1)} %collective-permute-done.6.refs_3_), channel_id=1, source_target_pairs={{0,2},{2,4},{4,6},{6,8},{8,10},{10,12},{12,14},{14,0},{1,3},{3,5},... | collective-permute-start | bytes 1105928 | tf_op jit(solution)/shard_map/ppermute | solution.py:28
  100.5 20.4 %collective-permute-start.10 = (bf16[288,640]{1,0:T(8,128)(2,1)}, bf16[288,640]{1,0:T(8,128)(2,1)}, u32[]{:S(2)}, u32[]{:S(2)}) collective-permute-start(bf16[288,640]{1,0:T(8,128)(2,1)} %collective-permute-done.8.refs_6_), channel_id=1, source_target_pairs={{0,2},{2,4},{4,6},{6,8},{8,10},{10,12},{12,14},{14,0},{1,3},{3,5},... | collective-permute-start | bytes 1105928 | tf_op jit(solution)/shard_map/ppermute | solution.py:28
  104.2 18.7 %collective-permute-start.17 = (bf16[288,640]{1,0:T(8,128)(2,1)}, bf16[288,640]{1,0:T(8,128)(2,1)}, u32[]{:S(2)}, u32[]{:S(2)}) collective-permute-start(bf16[288,640]{1,0:T(8,128)(2,1)} %collective-permute-done.11.refs_9_), channel_id=1, source_target_pairs={{0,14},{2,0},{4,2},{6,4},{8,6},{10,8},{12,10},{14,12},{1,15},{3,1}... | collective-permute-start | bytes 1105928 | tf_op jit(solution)/shard_map/ppermute | solution.py:29
  108.8 22.0 %collective-permute-start.15 = (bf16[2240,128]{1,0:T(8,128)(2,1)}, bf16[2240,128]{1,0:T(8,128)(2,1)}, u32[]{:S(2)}, u32[]{:S(2)}) collective-permute-start(bf16[2240,128]{1,0:T(8,128)(2,1)} %pack.1.mine), channel_id=1, source_target_pairs={{0,1},{1,0},{2,3},{3,2},{4,5},{5,4},{6,7},{7,6},{8,9},{9,8},{10,11... | collective-permute-start | bytes 1720328 | tf_op jit(solution)/shard_map/ppermute | solution.py:116
  110.7 27.5 %collective-permute-start.13 = (bf16[288,640]{1,0:T(8,128)(2,1)}, bf16[288,640]{1,0:T(8,128)(2,1)}, u32[]{:S(2)}, u32[]{:S(2)}) collective-permute-start(bf16[288,640]{1,0:T(8,128)(2,1)} %collective-permute-done.7.refs_4_), channel_id=1, source_target_pairs={{0,14},{2,0},{4,2},{6,4},{8,6},{10,8},{12,10},{14,12},{1,15},{3,1}... | collective-permute-start | bytes 1105928 | tf_op jit(solution)/shard_map/ppermute | solution.py:29
  113.0 25.1 %collective-permute-start.14 = (bf16[288,640]{1,0:T(8,128)(2,1)}, bf16[288,640]{1,0:T(8,128)(2,1)}, u32[]{:S(2)}, u32[]{:S(2)}) collective-permute-start(bf16[288,640]{1,0:T(8,128)(2,1)} %collective-permute-done.12.refs_0_), channel_id=1, source_target_pairs={{0,2},{2,4},{4,6},{6,8},{8,10},{10,12},{12,14},{14,0},{1,3},{3,5},... | collective-permute-start | bytes 1105928 | tf_op jit(solution)/shard_map/ppermute | solution.py:31
  120.9 29.0 %collective-permute-start.16 = (bf16[288,640]{1,0:T(8,128)(2,1)}, bf16[288,640]{1,0:T(8,128)(2,1)S(1)}, u32[]{:S(2)}, u32[]{:S(2)}) collective-permute-start(bf16[288,640]{1,0:T(8,128)(2,1)} %collective-permute-done.10.refs_8_), channel_id=1, source_target_pairs={{0,2},{2,4},{4,6},{6,8},{8,10},{10,12},{12,14},{14,0},{1,3},{3,5},... | collective-permute-start | bytes 1105928 | tf_op jit(solution)/shard_map/ppermute | solution.py:28
  123.0 27.0 %collective-permute-start.18 = (bf16[288,640]{1,0:T(8,128)(2,1)}, bf16[288,640]{1,0:T(8,128)(2,1)}, u32[]{:S(2)}, u32[]{:S(2)}) collective-permute-start(bf16[288,640]{1,0:T(8,128)(2,1)} %collective-permute-done.17.refs_1_), channel_id=1, source_target_pairs={{0,14},{2,0},{4,2},{6,4},{8,6},{10,8},{12,10},{14,12},{1,15},{3,1}... | collective-permute-start | bytes 1105928 | tf_op jit(solution)/shard_map/ppermute | solution.py:31
  143.0 40.4 %all-to-all-start.1 = ((bf16[8,136,128]{2,1,0:T(8,128)(2,1)}), bf16[8,136,128]{2,1,0:T(8,128)(2,1)S(1)}, u32[]{:S(2)}, u32[]{:S(2)}) async-start(bf16[8,136,128]{2,1,0:T(8,128)(2,1)} %broadcast_in_dim.88), calls=%async_computation.1 | async-start | bytes 557056 | tf_op jit(solution)/shard_map/all_to_all | solution.py:188
  185.2 26.7 %all-to-all-start.2 = ((bf16[32,9,2,640]{3,2,1,0:T(2,128)(2,1)}), bf16[32,9,2,640]{3,2,1,0:T(2,128)(2,1)S(1)}, u32[]{:S(2)}, u32[]{:S(2)}) async-start(bf16[32,9,2,640]{3,2,1,0:T(2,128)(2,1)} %reshape.71), calls=%async_computation.2 | async-start | bytes 1474560 | tf_op jit(solution)/shard_map/all_to_all | solution.py:158
  (7 other events, 78.1 us)

commit v6 on v5

--- a/solution.py
+++ b/solution.py
@@ -10,6 +10,7 @@
 
 
 EXPERT = ("expert_0", "expert_1", "expert_2")
+SMALL = pltpu.CompilerParams(vmem_limit_bytes=12 * 1024 * 1024)
 DP_EXPERT = ("dp", "expert_0", "expert_1", "expert_2")
 
 
@@ -46,11 +47,25 @@
         refs[2 * count + chain][...] = product_of(place[0], size, distances, blocks, weight)
 
 
-def last_kernel(size, distances, place, weight, begun, *refs):
-    *blocks, out = refs
+def activation(size, distances, place, weight, begun, blocks):
     total = begun[...] + product_of(place[0], size, distances, blocks, weight)
     gate, up = total[:, : total.shape[1] // 2], total[:, total.shape[1] // 2 :]
-    out[...] = (gate / (1.0 + jnp.exp(-gate)) * up).astype(out.dtype)
+    return (gate / (1.0 + jnp.exp(-gate)) * up).astype(jnp.bfloat16)
+
+
+def last_a_kernel(size, distances, place, weight, begun, *refs):
+    *blocks, spread, rest = refs
+    act = activation(size, distances, place, weight, begun, blocks)
+    some = spread.shape[1]
+    for i in range(size):
+        spread[i] = act[:some, :]
+    rest[...] = act[some:, :]
+
+
+def last_b_kernel(size, distances, place, weight, begun, *refs):
+    *blocks, rest, out = refs
+    out[: rest.shape[0], :] = rest[...]
+    out[rest.shape[0] :, :] = activation(size, distances, place, weight, begun, blocks)
 
 
 def pack_kernel(first, second, third, fourth, out):
@@ -111,8 +126,8 @@
         in_specs=[vmem] * 4,
         out_specs=vmem,
         name="pack",
+        compiler_params=SMALL,
     )(*got)
-    mine, after = lax.optimization_barrier((mine, after))
     other = lax.ppermute(mine, "dp", [(0, 1), (1, 0)])
     own = lax.dynamic_index_in_dim(blocks, me, 0, keepdims=False)
     placed = pl.pallas_call(
@@ -121,6 +136,7 @@
         in_specs=[pl.BlockSpec(memory_space=pltpu.SMEM)] + [vmem] * 3,
         out_specs=vmem,
         name="place",
+        compiler_params=SMALL,
     )(place, own, mine, other)
     return placed, after
 
@@ -172,21 +188,33 @@
         in_specs=[smem] + [vmem] * (1 + 2 * early),
         out_specs=[vmem] * 2,
         name="first",
+        compiler_params=SMALL,
     )(place, weight_in, *(x for chain in chains for _, x in chain[:early]))
 
-    def finished(chain, total):
-        return pl.pallas_call(
-            functools.partial(last_kernel, size, [d for d, _ in chain[early:]]),
-            out_shape=jax.ShapeDtypeStruct((rows // 2, hidden), bf16),
-            in_specs=[smem] + [vmem] * (2 + len(chain) - early),
-            out_specs=vmem,
-            name="last",
-        )(place, weight_in, total, *(x for _, x in chain[early:]))
-
-    act_a, act_b = finished(chains[0], begun[0]), finished(chains[1], begun[1])
     some = 136
-    all_a = lax.all_to_all(jnp.broadcast_to(act_a[None, :some], (size, some, hidden)), "tensor", 0, 0, tiled=True)
-    all_b = lax.all_gather(jnp.concatenate([act_a[some:], act_b], axis=0), "tensor")
+    distances = [d for d, _ in chains[0][early:]]
+    late = [smem] + [vmem] * (2 + len(distances))
+    spread, rest = pl.pallas_call(
+        functools.partial(last_a_kernel, size, distances),
+        out_shape=[
+            jax.ShapeDtypeStruct((size, some, hidden), bf16),
+            jax.ShapeDtypeStruct((rows // 2 - some, hidden), bf16),
+        ],
+        in_specs=late,
+        out_specs=[vmem] * 2,
+        name="last_a",
+        compiler_params=SMALL,
+    )(place, weight_in, begun[0], *(x for _, x in chains[0][early:]))
+    all_a = lax.all_to_all(spread, "tensor", 0, 0, tiled=True)
+    act_b = pl.pallas_call(
+        functools.partial(last_b_kernel, size, distances),
+        out_shape=jax.ShapeDtypeStruct((rows - some, hidden), bf16),
+        in_specs=late + [vmem],
+        out_specs=vmem,
+        name="last_b",
+        compiler_params=SMALL,
+    )(place, weight_in, begun[1], *(x for _, x in chains[1][early:]), rest)
+    all_b = lax.all_gather(act_b, "tensor")
 
     def outputs(act):
         return dot(act, down_mine, ((0, 2), (0, 2))).astype(bf16)

time: 215 us -> 209 us (0.972)
  the two profiles are of different devices: /device:TPU:80 before, /device:TPU:64 now
where the time goes in v6:
time: 209 us; the launch traced here: 208 us
  starting transfers between devices  80.5 us (39%)
  blocking collectives  63.9 us (31%)
  waiting for transfers between devices  36.2 us (17%)
  local copies, waits for them, and re-layouts  12.7 us (6%)
  Pallas kernels  8.55 us (4%)
  matrix products  3.32 us (2%)
    all_to_all x1, blocking collectives, exchange(): x = lax.all_to_all(x, EXPERT, 0, 0, tiled=True)  35.4 us
    all_gather x1, blocking collectives, local(): all_b = lax.all_gather(act_b, 'tensor')  28.5 us
    ppermute x6, starting transfers between devices, hops(): down = lax.ppermute(down, 'tensor', shift(size, -1))  19.8 us
    all_to_all x1, waiting for transfers between devices, exchange(): x = lax.all_to_all(x, EXPERT, 0, 0, tiled=True)  19.8 us
    ppermute x6, starting transfers between devices, hops(): up = lax.ppermute(up, 'tensor', shift(size, 1))  18.4 us
    ppermute x3, starting transfers between devices, down_rows(): got.append(lax.ppermute(block, ('tensor', 'dp'), perm))  15.2 us
    ppermute x3, waiting for transfers between devices, down_rows(): got.append(lax.ppermute(block, ('tensor', 'dp'), perm))  13.4 us
    ppermute x2, starting transfers between devices, hops(): lax.ppermute(up if last > 0 else down, 'tensor', shift(size, last))  7.77 us
  transfers between devices with their start and end apart: 21, of which 4 were waited for; matrix products, arithmetic and copies ran while one was open for 4% of the time, Pallas kernels for 4%

profile of v6, /device:TPU:64, one launch (start us, length us, event | category | flops | bytes accessed | tf_op | source)
XLA Modules:
  0.0 207.7 jit_solution(10866881185912184204)
XLA Ops:
  2.8 35.4 %all_to_all.15 = bf16[32,9,2,640]{3,2,1,0:T(2,128)(2,1)S(1)} all-to-all(bf16[32,9,2,640]{3,2,1,0:T(2,128)(2,1)S(1)} %reshape.67), channel_id=1, replica_groups=mesh['expert_0'=4,'expert_1'=4,'expert_2'=2,'tensor'=8,'dp'=2] {'expert_..., dimensions={0} | all-to-all | bytes 1474560 | tf_op jit(solution)/shard_map/all_to_all | solution.py:174
  38.6 3.5 %collective-permute-start = (bf16[288,640]{1,0:T(8,128)(2,1)S(1)}, bf16[288,640]{1,0:T(8,128)(2,1)S(1)}, u32[]{:S(2)}, u32[]{:S(2)}) collective-permute-start(bf16[288,640]{1,0:T(8,128)(2,1)S(1)} %get-tuple-element.18.refs_0_), channel_id=1, source_target_pairs={{0,2},{2,4},{4,6},{6,8},{8,10},{10,12},{12,14},{14,0},{1,3},{3,5},... | collective-permute-start | bytes 1105928 | tf_op jit(solution)/shard_map/ppermute | solution.py:29
  42.0 3.8 %collective-permute-start.5 = (bf16[288,640]{1,0:T(8,128)(2,1)S(1)}, bf16[288,640]{1,0:T(8,128)(2,1)S(1)}, u32[]{:S(2)}, u32[]{:S(2)}) collective-permute-start(bf16[288,640]{1,0:T(8,128)(2,1)S(1)} %get-tuple-element.17.refs_5_), channel_id=1, source_target_pairs={{0,14},{2,0},{4,2},{6,4},{8,6},{10,8},{12,10},{14,12},{1,15},{3,1}... | collective-permute-start | bytes 1105928 | tf_op jit(solution)/shard_map/ppermute | solution.py:30
  46.8 7.5 %collective-permute-start.14 = (bf16[320,128]{1,0:T(8,128)(2,1)S(1)}, bf16[320,128]{1,0:T(8,128)(2,1)S(1)}, u32[]{:S(2)}, u32[]{:S(2)}) collective-permute-start(bf16[320,128]{1,0:T(8,128)(2,1)S(1)} %dynamic-slice_bitcast_fusion.4), channel_id=1, source_target_pairs={{0,8},{2,10},{4,12},{6,14},{8,0},{10,2},{12,4},{14,6},{1,9},{3,11}... | collective-permute-start | bytes 245768 | tf_op jit(solution)/shard_map/ppermute | solution.py:121
  56.2 3.9 %collective-permute-start.4 = (bf16[288,640]{1,0:T(8,128)(2,1)S(1)}, bf16[288,640]{1,0:T(8,128)(2,1)S(1)}, u32[]{:S(2)}, u32[]{:S(2)}) collective-permute-start(bf16[288,640]{1,0:T(8,128)(2,1)S(1)} %get-tuple-element.17.refs_5_), channel_id=1, source_target_pairs={{0,2},{2,4},{4,6},{6,8},{8,10},{10,12},{12,14},{14,0},{1,3},{3,5},... | collective-permute-start | bytes 1105928 | tf_op jit(solution)/shard_map/ppermute | solution.py:29
  62.1 5.1 %collective-permute-start.7 = (bf16[288,640]{1,0:T(8,128)(2,1)S(1)}, bf16[288,640]{1,0:T(8,128)(2,1)S(1)}, u32[]{:S(2)}, u32[]{:S(2)}) collective-permute-start(bf16[288,640]{1,0:T(8,128)(2,1)S(1)} %collective-permute-done.5.refs_7_), channel_id=1, source_target_pairs={{0,14},{2,0},{4,2},{6,4},{8,6},{10,8},{12,10},{14,12},{1,15},{3,1}... | collective-permute-start | bytes 1105928 | tf_op jit(solution)/shard_map/ppermute | solution.py:30
  71.0 7.7 %collective-permute-done.11.first = bf16[640,128]{1,0:T(8,128)(2,1)S(1)} collective-permute-done((bf16[640,128]{1,0:T(8,128)(2,1)S(1)}, bf16[640,128]{1,0:T(8,128)(2,1)S(1)}, u32[]{:S(2)}, u32[]{:S(2)}) %collective-permute-start.11) | collective-permute-done | bytes 163872 | tf_op jit(solution)/shard_map/ppermute | solution.py:117
  78.7 3.9 %collective-permute-start.12 = (bf16[640,128]{1,0:T(8,128)(2,1)S(1)}, bf16[640,128]{1,0:T(8,128)(2,1)S(1)}, u32[]{:S(2)}, u32[]{:S(2)}) collective-permute-start(bf16[640,128]{1,0:T(8,128)(2,1)S(1)} %get-tuple-element.14), channel_id=1, source_target_pairs={{0,4},{2,6},{4,8},{6,10},{8,12},{10,14},{12,0},{14,2},{1,13},{3,15... | collective-permute-start | bytes 491528 | tf_op jit(solution)/shard_map/ppermute | solution.py:117
  82.6 5.7 %collective-permute-done.12.second = bf16[640,128]{1,0:T(8,128)(2,1)S(1)} collective-permute-done((bf16[640,128]{1,0:T(8,128)(2,1)S(1)}, bf16[640,128]{1,0:T(8,128)(2,1)S(1)}, u32[]{:S(2)}, u32[]{:S(2)}) %collective-permute-start.12) | collective-permute-done | bytes 163872 | tf_op jit(solution)/shard_map/ppermute | solution.py:117
  88.3 9.4 %collective-permute-start.13 = (bf16[640,128]{1,0:T(8,128)(2,1)S(1)}, bf16[640,128]{1,0:T(8,128)(2,1)S(1)}, u32[]{:S(2)}, u32[]{:S(2)}) collective-permute-start(bf16[640,128]{1,0:T(8,128)(2,1)S(1)} %get-tuple-element.13), channel_id=1, source_target_pairs={{0,10},{2,12},{4,14},{6,0},{8,2},{10,4},{12,6},{14,8},{1,7},{3,9},... | collective-permute-start | bytes 491528 | tf_op jit(solution)/shard_map/ppermute | solution.py:117
  97.8 1.9 collective-permute-start.3
  99.7 3.9 %collective-permute-start.8 = (bf16[288,640]{1,0:T(8,128)(2,1)S(1)}, bf16[288,640]{1,0:T(8,128)(2,1)}, u32[]{:S(2)}, u32[]{:S(2)}) collective-permute-start(bf16[288,640]{1,0:T(8,128)(2,1)S(1)} %collective-permute-done.2.refs_3_), channel_id=1, source_target_pairs={{0,2},{2,4},{4,6},{6,8},{8,10},{10,12},{12,14},{14,0},{1,3},{3,5},... | collective-permute-start | bytes 1105928 | tf_op jit(solution)/shard_map/ppermute | solution.py:29
  105.6 5.1 %collective-permute-start.17 = (bf16[288,640]{1,0:T(8,128)(2,1)S(1)}, bf16[288,640]{1,0:T(8,128)(2,1)}, u32[]{:S(2)}, u32[]{:S(2)}) collective-permute-start(bf16[288,640]{1,0:T(8,128)(2,1)S(1)} %collective-permute-done.7.refs_9_), channel_id=1, source_target_pairs={{0,14},{2,0},{4,2},{6,4},{8,6},{10,8},{12,10},{14,12},{1,15},{3,1}... | collective-permute-start | bytes 1105928 | tf_op jit(solution)/shard_map/ppermute | solution.py:30
  116.3 3.9 %collective-permute-start.10 = (bf16[288,640]{1,0:T(8,128)(2,1)}, bf16[288,640]{1,0:T(8,128)(2,1)}, u32[]{:S(2)}, u32[]{:S(2)}) collective-permute-start(bf16[288,640]{1,0:T(8,128)(2,1)} %collective-permute-done.8.refs_0_), channel_id=1, source_target_pairs={{0,2},{2,4},{4,6},{6,8},{8,10},{10,12},{12,14},{14,0},{1,3},{3,5},... | collective-permute-start | bytes 1105928 | tf_op jit(solution)/shard_map/ppermute | solution.py:32
  120.3 2.9 %collective-permute-done.6.refs_8_ = bf16[288,640]{1,0:T(8,128)(2,1)} collective-permute-done((bf16[288,640]{1,0:T(8,128)(2,1)S(1)}, bf16[288,640]{1,0:T(8,128)(2,1)}, u32[]{:S(2)}, u32[]{:S(2)}) %collective-permute-start.6) | collective-permute-done | bytes 368672 | tf_op jit(solution)/shard_map/ppermute | solution.py:29
  123.2 3.2 %collective-permute-start.16 = (bf16[288,640]{1,0:T(8,128)(2,1)}, bf16[288,640]{1,0:T(8,128)(2,1)}, u32[]{:S(2)}, u32[]{:S(2)}) collective-permute-start(bf16[288,640]{1,0:T(8,128)(2,1)} %collective-permute-done.6.refs_8_), channel_id=1, source_target_pairs={{0,2},{2,4},{4,6},{6,8},{8,10},{10,12},{12,14},{14,0},{1,3},{3,5},... | collective-permute-start | bytes 1105928 | tf_op jit(solution)/shard_map/ppermute | solution.py:29
  126.5 3.8 %collective-permute-start.18 = (bf16[288,640]{1,0:T(8,128)(2,1)}, bf16[288,640]{1,0:T(8,128)(2,1)}, u32[]{:S(2)}, u32[]{:S(2)}) collective-permute-start(bf16[288,640]{1,0:T(8,128)(2,1)} %collective-permute-done.17.refs_1_), channel_id=1, source_target_pairs={{0,14},{2,0},{4,2},{6,4},{8,6},{10,8},{12,10},{14,12},{1,15},{3,1}... | collective-permute-start | bytes 1105928 | tf_op jit(solution)/shard_map/ppermute | solution.py:32
  130.3 4.2 %reshape.66.weight = bf16[8,640,256]{2,1,0:T(8,128)(2,1)S(1)} reshape(bf16[1,5120,2,128]{3,2,1,0:T(2,128)(2,1)} %param.10) | data formatting | bytes 5242880 | tf_op jit(solution)/shard_map/reshape | solution.py:182
  137.4 2.9 %first.1 = (f32[288,256]{1,0:T(8,128)S(1)}, f32[288,256]{1,0:T(8,128)S(1)}) custom-call(s32[2]{0:T(128)S(1)} %pad_add_fusion.place, bf16[8,640,256]{2,1,0:T(8,128)(2,1)S(1)} %reshape.66.weight, bf16[288,640]{1,0:T(8,128)(2,1)S(1)} %copy-done.7, bf16[288,640]{1,0:T(8,128)(2,1)S(1)} %copy-done.9, bf16[288,640]{1,0:T(8,128)(2,1)S(1)} %copy-done.13, ...), custom_call_target="tpu_custom_call" | custom-call | tf_op jit(solution)/shard_map/first/pallas_call | solution.py:185
  140.3 2.4 %last_a.1 = (bf16[8,136,128]{2,1,0:T(8,128)(2,1)}, bf16[152,128]{1,0:T(8,128)(2,1)S(1)}) custom-call(s32[2]{0:T(128)S(1)} %pad_add_fusion.place, bf16[8,640,256]{2,1,0:T(8,128)(2,1)S(1)} %reshape.66.weight, f32[288,256]{1,0:T(8,128)S(1)} %get-tuple-element.9.begun, bf16[288,640]{1,0:T(8,128)(2,1)} %collective-permute-done.8.refs_0_, ...), custom_call_target="tpu_custom_call" | custom-call | tf_op jit(solution)/shard_map/last_a/pallas_call | solution.py:197
  142.8 6.0 %all-to-all-start.1 = ((bf16[8,136,128]{2,1,0:T(8,128)(2,1)}), bf16[8,136,128]{2,1,0:T(8,128)(2,1)S(1)}, u32[]{:S(2)}, u32[]{:S(2)}) async-start(bf16[8,136,128]{2,1,0:T(8,128)(2,1)} %get-tuple-element.10), calls=%async_computation.1 | async-start | bytes 557056 | tf_op jit(solution)/shard_map/all_to_all | solution.py:208
  150.6 28.5 %all-gather = bf16[3520,128]{1,0:T(8,128)(2,1)S(1)} all-gather(bf16[440,128]{1,0:T(8,128)(2,1)S(1)} %last_b.1), channel_id=2, replica_groups=mesh['expert_0'=4,'expert_1'=4,'expert_2'=2,'tensor'=8,'dp'=2] {'tensor'}, dimensions={0}, use_global_device_ids=true | all-gather | bytes 1013760 | tf_op jit(solution)/shard_map/all_gather | solution.py:217
  182.3 3.9 %all-to-all-start.2 = ((bf16[32,9,2,640]{3,2,1,0:T(2,128)(2,1)}), bf16[32,9,2,640]{3,2,1,0:T(2,128)(2,1)S(1)}, u32[]{:S(2)}, u32[]{:S(2)}) async-start(bf16[32,9,2,640]{3,2,1,0:T(2,128)(2,1)} %reshape.70), calls=%async_computation.2 | async-start | bytes 1474560 | tf_op jit(solution)/shard_map/all_to_all | solution.py:174
  186.3 19.8 %all-to-all-done.2 = bf16[32,9,2,640]{3,2,1,0:T(2,128)(2,1)S(1)} async-done(((bf16[32,9,2,640]{3,2,1,0:T(2,128)(2,1)}), bf16[32,9,2,640]{3,2,1,0:T(2,128)(2,1)S(1)}, u32[]{:S(2)}, u32[]{:S(2)}) %all-to-all-start.2) | async-done | bytes 737312 | tf_op jit(solution)/shard_map/all_to_all | solution.py:174
  (97 shorter events, 28.5 us)
Async XLA Ops:
  38.5 73.9 %copy-start.4 = (bf16[288,640]{1,0:T(8,128)(2,1)}, bf16[288,640]{1,0:T(8,128)(2,1)S(1)}, u32[]{:S(2)}) copy-start(bf16[288,640]{1,0:T(8,128)(2,1)S(1)} %get-tuple-element.17.refs_5_) | copy-start | bytes 1105924
  38.5 73.9 %copy-start.6 = (bf16[288,640]{1,0:T(8,128)(2,1)}, bf16[288,640]{1,0:T(8,128)(2,1)S(1)}, u32[]{:S(2)}) copy-start(bf16[288,640]{1,0:T(8,128)(2,1)S(1)} %get-tuple-element.18.refs_0_) | copy-start | bytes 1105924
  38.6 21.6 %collective-permute-start = (bf16[288,640]{1,0:T(8,128)(2,1)S(1)}, bf16[288,640]{1,0:T(8,128)(2,1)S(1)}, u32[]{:S(2)}, u32[]{:S(2)}) collective-permute-start(bf16[288,640]{1,0:T(8,128)(2,1)S(1)} %get-tuple-element.18.refs_0_), channel_id=1, source_target_pairs={{0,2},{2,4},{4,6},{6,8},{8,10},{10,12},{12,14},{14,0},{1,3},{3,5},... | collective-permute-start | bytes 1105928 | tf_op jit(solution)/shard_map/ppermute | solution.py:29
  42.0 20.1 %collective-permute-start.5 = (bf16[288,640]{1,0:T(8,128)(2,1)S(1)}, bf16[288,640]{1,0:T(8,128)(2,1)S(1)}, u32[]{:S(2)}, u32[]{:S(2)}) collective-permute-start(bf16[288,640]{1,0:T(8,128)(2,1)S(1)} %get-tuple-element.17.refs_5_), channel_id=1, source_target_pairs={{0,14},{2,0},{4,2},{6,4},{8,6},{10,8},{12,10},{14,12},{1,15},{3,1}... | collective-permute-start | bytes 1105928 | tf_op jit(solution)/shard_map/ppermute | solution.py:30
  46.8 21.7 %collective-permute-start.14 = (bf16[320,128]{1,0:T(8,128)(2,1)S(1)}, bf16[320,128]{1,0:T(8,128)(2,1)S(1)}, u32[]{:S(2)}, u32[]{:S(2)}) collective-permute-start(bf16[320,128]{1,0:T(8,128)(2,1)S(1)} %dynamic-slice_bitcast_fusion.4), channel_id=1, source_target_pairs={{0,8},{2,10},{4,12},{6,14},{8,0},{10,2},{12,4},{14,6},{1,9},{3,11}... | collective-permute-start | bytes 245768 | tf_op jit(solution)/shard_map/ppermute | solution.py:121
  54.3 43.4 %collective-permute-start.1 = (bf16[288,640]{1,0:T(8,128)(2,1)S(1)}, bf16[288,640]{1,0:T(8,128)(2,1)S(1)}, u32[]{:S(2)}, u32[]{:S(2)}) collective-permute-start(bf16[288,640]{1,0:T(8,128)(2,1)S(1)} %get-tuple-element.18.refs_0_), channel_id=1, source_target_pairs={{0,14},{2,0},{4,2},{6,4},{8,6},{10,8},{12,10},{14,12},{1,15},{3,1}... | collective-permute-start | bytes 1105928 | tf_op jit(solution)/shard_map/ppermute | solution.py:30
  56.2 47.4 %collective-permute-start.4 = (bf16[288,640]{1,0:T(8,128)(2,1)S(1)}, bf16[288,640]{1,0:T(8,128)(2,1)S(1)}, u32[]{:S(2)}, u32[]{:S(2)}) collective-permute-start(bf16[288,640]{1,0:T(8,128)(2,1)S(1)} %get-tuple-element.17.refs_5_), channel_id=1, source_target_pairs={{0,2},{2,4},{4,6},{6,8},{8,10},{10,12},{12,14},{14,0},{1,3},{3,5},... | collective-permute-start | bytes 1105928 | tf_op jit(solution)/shard_map/ppermute | solution.py:29
  60.2 66.2 %copy-start.8 = (bf16[288,640]{1,0:T(8,128)(2,1)}, bf16[288,640]{1,0:T(8,128)(2,1)S(1)}, u32[]{:S(2)}) copy-start(bf16[288,640]{1,0:T(8,128)(2,1)S(1)} %collective-permute-done.refs_1_) | copy-start | bytes 1105924
  60.2 39.5 %collective-permute-start.2 = (bf16[288,640]{1,0:T(8,128)(2,1)S(1)}, bf16[288,640]{1,0:T(8,128)(2,1)S(1)}, u32[]{:S(2)}, u32[]{:S(2)}) collective-permute-start(bf16[288,640]{1,0:T(8,128)(2,1)S(1)} %collective-permute-done.refs_1_), channel_id=1, source_target_pairs={{0,2},{2,4},{4,6},{6,8},{8,10},{10,12},{12,14},{14,0},{1,3},{3,5},... | collective-permute-start | bytes 1105928 | tf_op jit(solution)/shard_map/ppermute | solution.py:29
  62.1 43.5 %collective-permute-start.7 = (bf16[288,640]{1,0:T(8,128)(2,1)S(1)}, bf16[288,640]{1,0:T(8,128)(2,1)S(1)}, u32[]{:S(2)}, u32[]{:S(2)}) collective-permute-start(bf16[288,640]{1,0:T(8,128)(2,1)S(1)} %collective-permute-done.5.refs_7_), channel_id=1, source_target_pairs={{0,14},{2,0},{4,2},{6,4},{8,6},{10,8},{12,10},{14,12},{1,15},{3,1}... | collective-permute-start | bytes 1105928 | tf_op jit(solution)/shard_map/ppermute | solution.py:30
  69.1 9.6 %collective-permute-start.11 = (bf16[640,128]{1,0:T(8,128)(2,1)S(1)}, bf16[640,128]{1,0:T(8,128)(2,1)S(1)}, u32[]{:S(2)}, u32[]{:S(2)}) collective-permute-start(bf16[640,128]{1,0:T(8,128)(2,1)S(1)} %get-tuple-element.15), channel_id=1, source_target_pairs={{0,2},{2,4},{4,6},{6,8},{8,10},{10,12},{12,14},{14,0},{1,15},{3,1}... | collective-permute-start | bytes 491528 | tf_op jit(solution)/shard_map/ppermute | solution.py:117
  78.7 9.6 %collective-permute-start.12 = (bf16[640,128]{1,0:T(8,128)(2,1)S(1)}, bf16[640,128]{1,0:T(8,128)(2,1)S(1)}, u32[]{:S(2)}, u32[]{:S(2)}) collective-permute-start(bf16[640,128]{1,0:T(8,128)(2,1)S(1)} %get-tuple-element.14), channel_id=1, source_target_pairs={{0,4},{2,6},{4,8},{6,10},{8,12},{10,14},{12,0},{14,2},{1,13},{3,15... | collective-permute-start | bytes 491528 | tf_op jit(solution)/shard_map/ppermute | solution.py:117
  88.3 23.2 %collective-permute-start.13 = (bf16[640,128]{1,0:T(8,128)(2,1)S(1)}, bf16[640,128]{1,0:T(8,128)(2,1)S(1)}, u32[]{:S(2)}, u32[]{:S(2)}) collective-permute-start(bf16[640,128]{1,0:T(8,128)(2,1)S(1)} %get-tuple-element.13), channel_id=1, source_target_pairs={{0,10},{2,12},{4,14},{6,0},{8,2},{10,4},{12,6},{14,8},{1,7},{3,9},... | collective-permute-start | bytes 491528 | tf_op jit(solution)/shard_map/ppermute | solution.py:117
  97.8 16.6 %collective-permute-start.3 = (bf16[288,640]{1,0:T(8,128)(2,1)S(1)}, bf16[288,640]{1,0:T(8,128)(2,1)}, u32[]{:S(2)}, u32[]{:S(2)}) collective-permute-start(bf16[288,640]{1,0:T(8,128)(2,1)S(1)} %collective-permute-done.1.refs_2_), channel_id=1, source_target_pairs={{0,14},{2,0},{4,2},{6,4},{8,6},{10,8},{12,10},{14,12},{1,15},{3,1}... | collective-permute-start | bytes 1105928 | tf_op jit(solution)/shard_map/ppermute | solution.py:30
  99.7 16.6 %collective-permute-start.8 = (bf16[288,640]{1,0:T(8,128)(2,1)S(1)}, bf16[288,640]{1,0:T(8,128)(2,1)}, u32[]{:S(2)}, u32[]{:S(2)}) collective-permute-start(bf16[288,640]{1,0:T(8,128)(2,1)S(1)} %collective-permute-done.2.refs_3_), channel_id=1, source_target_pairs={{0,2},{2,4},{4,6},{6,8},{8,10},{10,12},{12,14},{14,0},{1,3},{3,5},... | collective-permute-start | bytes 1105928 | tf_op jit(solution)/shard_map/ppermute | solution.py:29
  103.7 19.5 %collective-permute-start.6 = (bf16[288,640]{1,0:T(8,128)(2,1)S(1)}, bf16[288,640]{1,0:T(8,128)(2,1)}, u32[]{:S(2)}, u32[]{:S(2)}) collective-permute-start(bf16[288,640]{1,0:T(8,128)(2,1)S(1)} %collective-permute-done.4.refs_6_), channel_id=1, source_target_pairs={{0,2},{2,4},{4,6},{6,8},{8,10},{10,12},{12,14},{14,0},{1,3},{3,5},... | collective-permute-start | bytes 1105928 | tf_op jit(solution)/shard_map/ppermute | solution.py:29
  105.6 20.8 %collective-permute-start.17 = (bf16[288,640]{1,0:T(8,128)(2,1)S(1)}, bf16[288,640]{1,0:T(8,128)(2,1)}, u32[]{:S(2)}, u32[]{:S(2)}) collective-permute-start(bf16[288,640]{1,0:T(8,128)(2,1)S(1)} %collective-permute-done.7.refs_9_), channel_id=1, source_target_pairs={{0,14},{2,0},{4,2},{6,4},{8,6},{10,8},{12,10},{14,12},{1,15},{3,1}... | collective-permute-start | bytes 1105928 | tf_op jit(solution)/shard_map/ppermute | solution.py:30
  112.5 22.1 %collective-permute-start.15 = (bf16[2240,128]{1,0:T(8,128)(2,1)S(1)}, bf16[2240,128]{1,0:T(8,128)(2,1)}, u32[]{:S(2)}, u32[]{:S(2)}) collective-permute-start(bf16[2240,128]{1,0:T(8,128)(2,1)S(1)} %pack.1.mine), channel_id=1, source_target_pairs={{0,1},{1,0},{2,3},{3,2},{4,5},{5,4},{6,7},{7,6},{8,9},{9,8},{10,11... | collective-permute-start | bytes 1720328 | tf_op jit(solution)/shard_map/ppermute | solution.py:131
  114.4 25.9 %collective-permute-start.9 = (bf16[288,640]{1,0:T(8,128)(2,1)}, bf16[288,640]{1,0:T(8,128)(2,1)}, u32[]{:S(2)}, u32[]{:S(2)}) collective-permute-start(bf16[288,640]{1,0:T(8,128)(2,1)} %collective-permute-done.3.refs_4_), channel_id=1, source_target_pairs={{0,14},{2,0},{4,2},{6,4},{8,6},{10,8},{12,10},{14,12},{1,15},{3,1}... | collective-permute-start | bytes 1105928 | tf_op jit(solution)/shard_map/ppermute | solution.py:30
  116.3 24.0 %collective-permute-start.10 = (bf16[288,640]{1,0:T(8,128)(2,1)}, bf16[288,640]{1,0:T(8,128)(2,1)}, u32[]{:S(2)}, u32[]{:S(2)}) collective-permute-start(bf16[288,640]{1,0:T(8,128)(2,1)} %collective-permute-done.8.refs_0_), channel_id=1, source_target_pairs={{0,2},{2,4},{4,6},{6,8},{8,10},{10,12},{12,14},{14,0},{1,3},{3,5},... | collective-permute-start | bytes 1105928 | tf_op jit(solution)/shard_map/ppermute | solution.py:32
  123.2 25.6 %collective-permute-start.16 = (bf16[288,640]{1,0:T(8,128)(2,1)}, bf16[288,640]{1,0:T(8,128)(2,1)}, u32[]{:S(2)}, u32[]{:S(2)}) collective-permute-start(bf16[288,640]{1,0:T(8,128)(2,1)} %collective-permute-done.6.refs_8_), channel_id=1, source_target_pairs={{0,2},{2,4},{4,6},{6,8},{8,10},{10,12},{12,14},{14,0},{1,3},{3,5},... | collective-permute-start | bytes 1105928 | tf_op jit(solution)/shard_map/ppermute | solution.py:29
  126.5 22.3 %collective-permute-start.18 = (bf16[288,640]{1,0:T(8,128)(2,1)}, bf16[288,640]{1,0:T(8,128)(2,1)}, u32[]{:S(2)}, u32[]{:S(2)}) collective-permute-start(bf16[288,640]{1,0:T(8,128)(2,1)} %collective-permute-done.17.refs_1_), channel_id=1, source_target_pairs={{0,14},{2,0},{4,2},{6,4},{8,6},{10,8},{12,10},{14,12},{1,15},{3,1}... | collective-permute-start | bytes 1105928 | tf_op jit(solution)/shard_map/ppermute | solution.py:32
  142.8 37.3 %all-to-all-start.1 = ((bf16[8,136,128]{2,1,0:T(8,128)(2,1)}), bf16[8,136,128]{2,1,0:T(8,128)(2,1)S(1)}, u32[]{:S(2)}, u32[]{:S(2)}) async-start(bf16[8,136,128]{2,1,0:T(8,128)(2,1)} %get-tuple-element.10), calls=%async_computation.1 | async-start | bytes 557056 | tf_op jit(solution)/shard_map/all_to_all | solution.py:208
  182.3 23.8 %all-to-all-start.2 = ((bf16[32,9,2,640]{3,2,1,0:T(2,128)(2,1)}), bf16[32,9,2,640]{3,2,1,0:T(2,128)(2,1)S(1)}, u32[]{:S(2)}, u32[]{:S(2)}) async-start(bf16[32,9,2,640]{3,2,1,0:T(2,128)(2,1)} %reshape.70), calls=%async_computation.2 | async-start | bytes 1474560 | tf_op jit(solution)/shard_map/all_to_all | solution.py:174
  (20 other events, 198.4 us)

commit v7 on v6

--- a/solution.py
+++ b/solution.py
@@ -31,6 +31,10 @@
         found += [(-step, up), (step, down)]
     found.append((size // 2, lax.ppermute(up if last > 0 else down, "tensor", shift(size, last))))
     return found
+
+
+def relayout_kernel(x, out):
+    out[0] = x[0].reshape(out.shape[1:])
 
 
 def product_of(me, size, distances, blocks, weight):
@@ -179,7 +183,15 @@
     down_mine, weight_in = down_rows(down_weight, gate_up, place, size, part, hidden)
 
     chains = [hops(arrived[: rows // 2], size, 1), hops(arrived[rows // 2 :], size, -1)]
-    weight_in = weight_in.reshape(size, part, 2 * hidden)
+    weight_in = pl.pallas_call(
+        relayout_kernel,
+        grid=(size,),
+        out_shape=jax.ShapeDtypeStruct((size, part, 2 * hidden), bf16),
+        in_specs=[pl.BlockSpec((1, part, 2, hidden), lambda i: (0, i, 0, 0))],
+        out_specs=pl.BlockSpec((1, part, 2 * hidden), lambda i: (i, 0, 0)),
+        name="relayout",
+        compiler_params=SMALL,
+    )(weight_in)
     early = 5
     smem, vmem = pl.BlockSpec(memory_space=pltpu.SMEM), pl.BlockSpec(memory_space=pltpu.VMEM)
     begun = pl.pallas_call(
@@ -191,7 +203,7 @@
         compiler_params=SMALL,
     )(place, weight_in, *(x for chain in chains for _, x in chain[:early]))
 
-    some = 136
+    some = 80
     distances = [d for d, _ in chains[0][early:]]
     late = [smem] + [vmem] * (2 + len(distances))
     spread, rest = pl.pallas_call(

time: 209 us -> 215 us (1.029)
  the two profiles are of different devices: /device:TPU:64 before, /device:TPU:1 now
where the time goes in v7:
time: 215 us; the launch traced here: 214 us
  starting transfers between devices  83.8 us (39%)
  blocking collectives  56.4 us (26%)
  waiting for transfers between devices  55.5 us (26%)
  Pallas kernels  7.08 us (3%)
  local copies, waits for them, and re-layouts  5.17 us (2%)
  matrix products  3.37 us (2%)
    all_to_all x1, blocking collectives, exchange(): x = lax.all_to_all(x, EXPERT, 0, 0, tiled=True)  34.5 us
    all_to_all x1, waiting for transfers between devices, exchange(): x = lax.all_to_all(x, EXPERT, 0, 0, tiled=True)  22.4 us
    all_gather x1, blocking collectives, local(): all_b = lax.all_gather(act_b, 'tensor')  21.9 us
    ppermute x6, starting transfers between devices, hops(): down = lax.ppermute(down, 'tensor', shift(size, -1))  20.7 us
    ppermute x3, waiting for transfers between devices, down_rows(): got.append(lax.ppermute(block, ('tensor', 'dp'), perm))  20.6 us
    all_to_all x1, starting transfers between devices, exchange(): x = lax.all_to_all(x, EXPERT, 0, 0, tiled=True)  17.4 us
    ppermute x6, starting transfers between devices, hops(): up = lax.ppermute(up, 'tensor', shift(size, 1))  16 us
    all_to_all x1, waiting for transfers between devices, local(): all_a = lax.all_to_all(spread, 'tensor', 0, 0, tiled=True)  7.2 us
  transfers between devices with their start and end apart: 21, of which 5 were waited for; matrix products, arithmetic and copies ran while one was open for 2% of the time, Pallas kernels for 3%

profile of v7, /device:TPU:1, one launch (start us, length us, event | category | flops | bytes accessed | tf_op | source)
XLA Modules:
  0.0 213.7 jit_solution(12957869536300378803)
XLA Ops:
  2.8 34.5 %all_to_all.15 = bf16[32,9,2,640]{3,2,1,0:T(2,128)(2,1)S(1)} all-to-all(bf16[32,9,2,640]{3,2,1,0:T(2,128)(2,1)S(1)} %reshape.63), channel_id=1, replica_groups=mesh['expert_0'=4,'expert_1'=4,'expert_2'=2,'tensor'=8,'dp'=2] {'expert_..., dimensions={0} | all-to-all | bytes 1474560 | tf_op jit(solution)/shard_map/all_to_all | solution.py:178
  37.7 3.2 %collective-permute-start = (bf16[288,640]{1,0:T(8,128)(2,1)S(1)}, bf16[288,640]{1,0:T(8,128)(2,1)}, u32[]{:S(2)}, u32[]{:S(2)}) collective-permute-start(bf16[288,640]{1,0:T(8,128)(2,1)S(1)} %get-tuple-element.18.refs_0_), channel_id=1, source_target_pairs={{0,2},{2,4},{4,6},{6,8},{8,10},{10,12},{12,14},{14,0},{1,3},{3,5},... | collective-permute-start | bytes 1105928 | tf_op jit(solution)/shard_map/ppermute | solution.py:29
  40.9 3.8 %collective-permute-start.5 = (bf16[288,640]{1,0:T(8,128)(2,1)S(1)}, bf16[288,640]{1,0:T(8,128)(2,1)}, u32[]{:S(2)}, u32[]{:S(2)}) collective-permute-start(bf16[288,640]{1,0:T(8,128)(2,1)S(1)} %get-tuple-element.17.refs_5_), channel_id=1, source_target_pairs={{0,14},{2,0},{4,2},{6,4},{8,6},{10,8},{12,10},{14,12},{1,15},{3,1}... | collective-permute-start | bytes 1105928 | tf_op jit(solution)/shard_map/ppermute | solution.py:30
  46.4 6.9 %collective-permute-start.14 = (bf16[320,128]{1,0:T(8,128)(2,1)}, bf16[320,128]{1,0:T(8,128)(2,1)}, u32[]{:S(2)}, u32[]{:S(2)}) collective-permute-start(bf16[320,128]{1,0:T(8,128)(2,1)} %dynamic-slice_bitcast_fusion.4), channel_id=1, source_target_pairs={{0,8},{2,10},{4,12},{6,14},{8,0},{10,2},{12,4},{14,6},{1,9},{3,11}... | collective-permute-start | bytes 245768 | tf_op jit(solution)/shard_map/ppermute | solution.py:125
  53.4 1.9 collective-permute-start.1
  55.3 3.4 %collective-permute-start.4 = (bf16[288,640]{1,0:T(8,128)(2,1)S(1)}, bf16[288,640]{1,0:T(8,128)(2,1)S(1)}, u32[]{:S(2)}, u32[]{:S(2)}) collective-permute-start(bf16[288,640]{1,0:T(8,128)(2,1)S(1)} %get-tuple-element.17.refs_5_), channel_id=1, source_target_pairs={{0,2},{2,4},{4,6},{6,8},{8,10},{10,12},{12,14},{14,0},{1,3},{3,5},... | collective-permute-start | bytes 1105928 | tf_op jit(solution)/shard_map/ppermute | solution.py:29
  60.6 4.6 %collective-permute-start.7 = (bf16[288,640]{1,0:T(8,128)(2,1)}, bf16[288,640]{1,0:T(8,128)(2,1)S(1)}, u32[]{:S(2)}, u32[]{:S(2)}) collective-permute-start(bf16[288,640]{1,0:T(8,128)(2,1)} %collective-permute-done.5.refs_7_), channel_id=1, source_target_pairs={{0,14},{2,0},{4,2},{6,4},{8,6},{10,8},{12,10},{14,12},{1,15},{3,1}... | collective-permute-start | bytes 1105928 | tf_op jit(solution)/shard_map/ppermute | solution.py:30
  66.4 1.9 collective-permute-start.11
  68.3 10.7 %collective-permute-done.11.first = bf16[640,128]{1,0:T(8,128)(2,1)S(1)} collective-permute-done((bf16[640,128]{1,0:T(8,128)(2,1)S(1)}, bf16[640,128]{1,0:T(8,128)(2,1)S(1)}, u32[]{:S(2)}, u32[]{:S(2)}) %collective-permute-start.11) | collective-permute-done | bytes 163872 | tf_op jit(solution)/shard_map/ppermute | solution.py:121
  80.9 9.9 %collective-permute-done.12.second = bf16[640,128]{1,0:T(8,128)(2,1)S(1)} collective-permute-done((bf16[640,128]{1,0:T(8,128)(2,1)S(1)}, bf16[640,128]{1,0:T(8,128)(2,1)S(1)}, u32[]{:S(2)}, u32[]{:S(2)}) %collective-permute-start.12) | collective-permute-done | bytes 163872 | tf_op jit(solution)/shard_map/ppermute | solution.py:121
  94.7 3.4 %collective-permute-start.8 = (bf16[288,640]{1,0:T(8,128)(2,1)S(1)}, bf16[288,640]{1,0:T(8,128)(2,1)S(1)}, u32[]{:S(2)}, u32[]{:S(2)}) collective-permute-start(bf16[288,640]{1,0:T(8,128)(2,1)S(1)} %collective-permute-done.2.refs_3_), channel_id=1, source_target_pairs={{0,2},{2,4},{4,6},{6,8},{8,10},{10,12},{12,14},{14,0},{1,3},{3,5},... | collective-permute-start | bytes 1105928 | tf_op jit(solution)/shard_map/ppermute | solution.py:29
  98.1 2.2 %collective-permute-start.6 = (bf16[288,640]{1,0:T(8,128)(2,1)S(1)}, bf16[288,640]{1,0:T(8,128)(2,1)S(1)}, u32[]{:S(2)}, u32[]{:S(2)}) collective-permute-start(bf16[288,640]{1,0:T(8,128)(2,1)S(1)} %collective-permute-done.4.refs_6_), channel_id=1, source_target_pairs={{0,2},{2,4},{4,6},{6,8},{8,10},{10,12},{12,14},{14,0},{1,3},{3,5},... | collective-permute-start | bytes 1105928 | tf_op jit(solution)/shard_map/ppermute | solution.py:29
  100.3 4.3 %collective-permute-start.17 = (bf16[288,640]{1,0:T(8,128)(2,1)S(1)}, bf16[288,640]{1,0:T(8,128)(2,1)S(1)}, u32[]{:S(2)}, u32[]{:S(2)}) collective-permute-start(bf16[288,640]{1,0:T(8,128)(2,1)S(1)} %collective-permute-done.7.refs_9_), channel_id=1, source_target_pairs={{0,14},{2,0},{4,2},{6,4},{8,6},{10,8},{12,10},{14,12},{1,15},{3,1}... | collective-permute-start | bytes 1105928 | tf_op jit(solution)/shard_map/ppermute | solution.py:30
  105.5 7.1 %collective-permute-start.15 = (bf16[2240,128]{1,0:T(8,128)(2,1)S(1)}, bf16[2240,128]{1,0:T(8,128)(2,1)S(1)}, u32[]{:S(2)}, u32[]{:S(2)}) collective-permute-start(bf16[2240,128]{1,0:T(8,128)(2,1)S(1)} %pack.1.mine), channel_id=1, source_target_pairs={{0,1},{1,0},{2,3},{3,2},{4,5},{5,4},{6,7},{7,6},{8,9},{9,8},{10,11... | collective-permute-start | bytes 1720328 | tf_op jit(solution)/shard_map/ppermute | solution.py:135
  112.6 4.2 %collective-permute-start.9 = (bf16[288,640]{1,0:T(8,128)(2,1)S(1)}, bf16[288,640]{1,0:T(8,128)(2,1)S(1)}, u32[]{:S(2)}, u32[]{:S(2)}) collective-permute-start(bf16[288,640]{1,0:T(8,128)(2,1)S(1)} %collective-permute-done.3.refs_4_), channel_id=1, source_target_pairs={{0,14},{2,0},{4,2},{6,4},{8,6},{10,8},{12,10},{14,12},{1,15},{3,1}... | collective-permute-start | bytes 1105928 | tf_op jit(solution)/shard_map/ppermute | solution.py:30
  118.8 1.9 collective-permute-start.16
  120.8 4.6 %collective-permute-start.18 = (bf16[288,640]{1,0:T(8,128)(2,1)S(1)}, bf16[288,640]{1,0:T(8,128)(2,1)S(1)}, u32[]{:S(2)}, u32[]{:S(2)}) collective-permute-start(bf16[288,640]{1,0:T(8,128)(2,1)S(1)} %collective-permute-done.17.refs_1_), channel_id=1, source_target_pairs={{0,14},{2,0},{4,2},{6,4},{8,6},{10,8},{12,10},{14,12},{1,15},{3,1}... | collective-permute-start | bytes 1105928 | tf_op jit(solution)/shard_map/ppermute | solution.py:32
  126.4 2.4 %first.1 = (f32[288,256]{1,0:T(8,128)S(1)}, f32[288,256]{1,0:T(8,128)S(1)}) custom-call(s32[2]{0:T(128)S(1)} %pad_add_fusion.place, bf16[8,640,256]{2,1,0:T(8,128)(2,1)S(1)} %relayout.1.weight, bf16[288,640]{1,0:T(8,128)(2,1)S(1)} %get-tuple-element.18.refs_0_, bf16[288,640]{1,0:T(8,128)(2,1)} %collective-permute-done.refs_1_, ...), custom_call_target="tpu_custom_call" | custom-call | tf_op jit(solution)/shard_map/first/pallas_call | solution.py:197
  130.6 5.2 %collective-permute-done.16.refs_0_ = bf16[288,640]{1,0:T(8,128)(2,1)S(1)} collective-permute-done((bf16[288,640]{1,0:T(8,128)(2,1)S(1)}, bf16[288,640]{1,0:T(8,128)(2,1)S(1)}, u32[]{:S(2)}, u32[]{:S(2)}) %collective-permute-start.16) | collective-permute-done | bytes 368672 | tf_op jit(solution)/shard_map/ppermute | solution.py:29
  136.9 21.9 %all-gather = bf16[3968,128]{1,0:T(8,128)(2,1)S(1)} all-gather(bf16[496,128]{1,0:T(8,128)(2,1)S(1)} %last_b.1), channel_id=2, replica_groups=mesh['expert_0'=4,'expert_1'=4,'expert_2'=2,'tensor'=8,'dp'=2] {'tensor'}, dimensions={0}, use_global_device_ids=true | all-gather | bytes 1142784 | tf_op jit(solution)/shard_map/all_gather | solution.py:229
  158.8 3.4 %all-to-all-start.1 = ((bf16[8,80,128]{2,1,0:T(8,128)(2,1)}), bf16[8,80,128]{2,1,0:T(8,128)(2,1)S(1)}, u32[]{:S(2)}, u32[]{:S(2)}) async-start(bf16[8,80,128]{2,1,0:T(8,128)(2,1)} %get-tuple-element.10), calls=%async_computation.1 | async-start | bytes 327680 | tf_op jit(solution)/shard_map/all_to_all | solution.py:220
  163.2 7.2 %all-to-all-done.1 = bf16[8,80,128]{2,1,0:T(8,128)(2,1)S(1)} async-done(((bf16[8,80,128]{2,1,0:T(8,128)(2,1)}), bf16[8,80,128]{2,1,0:T(8,128)(2,1)S(1)}, u32[]{:S(2)}, u32[]{:S(2)}) %all-to-all-start.1) | async-done | bytes 163872 | tf_op jit(solution)/shard_map/all_to_all | solution.py:220
  172.1 17.4 %all-to-all-start.2 = ((bf16[32,9,2,640]{3,2,1,0:T(2,128)(2,1)}), bf16[32,9,2,640]{3,2,1,0:T(2,128)(2,1)S(1)}, u32[]{:S(2)}, u32[]{:S(2)}) async-start(bf16[32,9,2,640]{3,2,1,0:T(2,128)(2,1)} %reshape.66), calls=%async_computation.2 | async-start | bytes 1474560 | tf_op jit(solution)/shard_map/all_to_all | solution.py:178
  189.7 22.4 %all-to-all-done.2 = bf16[32,9,2,640]{3,2,1,0:T(2,128)(2,1)S(1)} async-done(((bf16[32,9,2,640]{3,2,1,0:T(2,128)(2,1)}), bf16[32,9,2,640]{3,2,1,0:T(2,128)(2,1)S(1)}, u32[]{:S(2)}, u32[]{:S(2)}) %all-to-all-start.2) | async-done | bytes 737312 | tf_op jit(solution)/shard_map/all_to_all | solution.py:178
  (57 shorter events, 24.7 us)
Async XLA Ops:
  0.0 2.1 copy-start
  37.7 21.0 %collective-permute-start = (bf16[288,640]{1,0:T(8,128)(2,1)S(1)}, bf16[288,640]{1,0:T(8,128)(2,1)}, u32[]{:S(2)}, u32[]{:S(2)}) collective-permute-start(bf16[288,640]{1,0:T(8,128)(2,1)S(1)} %get-tuple-element.18.refs_0_), channel_id=1, source_target_pairs={{0,2},{2,4},{4,6},{6,8},{8,10},{10,12},{12,14},{14,0},{1,3},{3,5},... | collective-permute-start | bytes 1105928 | tf_op jit(solution)/shard_map/ppermute | solution.py:29
  40.9 19.7 %collective-permute-start.5 = (bf16[288,640]{1,0:T(8,128)(2,1)S(1)}, bf16[288,640]{1,0:T(8,128)(2,1)}, u32[]{:S(2)}, u32[]{:S(2)}) collective-permute-start(bf16[288,640]{1,0:T(8,128)(2,1)S(1)} %get-tuple-element.17.refs_5_), channel_id=1, source_target_pairs={{0,14},{2,0},{4,2},{6,4},{8,6},{10,8},{12,10},{14,12},{1,15},{3,1}... | collective-permute-start | bytes 1105928 | tf_op jit(solution)/shard_map/ppermute | solution.py:30
  44.7 80.6 %copy-start.1 = (bf16[1,5120,2,128]{3,2,1,0:T(2,128)(2,1)S(1)}, bf16[1,5120,2,128]{3,2,1,0:T(2,128)(2,1)}, u32[]{:S(2)}) copy-start(bf16[1,5120,2,128]{3,2,1,0:T(2,128)(2,1)} %x.1) | copy-start | bytes 7864324
  46.4 20.0 %collective-permute-start.14 = (bf16[320,128]{1,0:T(8,128)(2,1)}, bf16[320,128]{1,0:T(8,128)(2,1)}, u32[]{:S(2)}, u32[]{:S(2)}) collective-permute-start(bf16[320,128]{1,0:T(8,128)(2,1)} %dynamic-slice_bitcast_fusion.4), channel_id=1, source_target_pairs={{0,8},{2,10},{4,12},{6,14},{8,0},{10,2},{12,4},{14,6},{1,9},{3,11}... | collective-permute-start | bytes 245768 | tf_op jit(solution)/shard_map/ppermute | solution.py:125
  53.4 39.4 %collective-permute-start.1 = (bf16[288,640]{1,0:T(8,128)(2,1)S(1)}, bf16[288,640]{1,0:T(8,128)(2,1)S(1)}, u32[]{:S(2)}, u32[]{:S(2)}) collective-permute-start(bf16[288,640]{1,0:T(8,128)(2,1)S(1)} %get-tuple-element.18.refs_0_), channel_id=1, source_target_pairs={{0,14},{2,0},{4,2},{6,4},{8,6},{10,8},{12,10},{14,12},{1,15},{3,1}... | collective-permute-start | bytes 1105928 | tf_op jit(solution)/shard_map/ppermute | solution.py:30
  55.3 42.8 %collective-permute-start.4 = (bf16[288,640]{1,0:T(8,128)(2,1)S(1)}, bf16[288,640]{1,0:T(8,128)(2,1)S(1)}, u32[]{:S(2)}, u32[]{:S(2)}) collective-permute-start(bf16[288,640]{1,0:T(8,128)(2,1)S(1)} %get-tuple-element.17.refs_5_), channel_id=1, source_target_pairs={{0,2},{2,4},{4,6},{6,8},{8,10},{10,12},{12,14},{14,0},{1,3},{3,5},... | collective-permute-start | bytes 1105928 | tf_op jit(solution)/shard_map/ppermute | solution.py:29
  58.7 36.0 %collective-permute-start.2 = (bf16[288,640]{1,0:T(8,128)(2,1)}, bf16[288,640]{1,0:T(8,128)(2,1)S(1)}, u32[]{:S(2)}, u32[]{:S(2)}) collective-permute-start(bf16[288,640]{1,0:T(8,128)(2,1)} %collective-permute-done.refs_1_), channel_id=1, source_target_pairs={{0,2},{2,4},{4,6},{6,8},{8,10},{10,12},{12,14},{14,0},{1,3},{3,5},... | collective-permute-start | bytes 1105928 | tf_op jit(solution)/shard_map/ppermute | solution.py:29
  60.6 39.7 %collective-permute-start.7 = (bf16[288,640]{1,0:T(8,128)(2,1)}, bf16[288,640]{1,0:T(8,128)(2,1)S(1)}, u32[]{:S(2)}, u32[]{:S(2)}) collective-permute-start(bf16[288,640]{1,0:T(8,128)(2,1)} %collective-permute-done.5.refs_7_), channel_id=1, source_target_pairs={{0,14},{2,0},{4,2},{6,4},{8,6},{10,8},{12,10},{14,12},{1,15},{3,1}... | collective-permute-start | bytes 1105928 | tf_op jit(solution)/shard_map/ppermute | solution.py:30
  66.4 12.6 %collective-permute-start.11 = (bf16[640,128]{1,0:T(8,128)(2,1)S(1)}, bf16[640,128]{1,0:T(8,128)(2,1)S(1)}, u32[]{:S(2)}, u32[]{:S(2)}) collective-permute-start(bf16[640,128]{1,0:T(8,128)(2,1)S(1)} %get-tuple-element.15), channel_id=1, source_target_pairs={{0,2},{2,4},{4,6},{6,8},{8,10},{10,12},{12,14},{14,0},{1,15},{3,1}... | collective-permute-start | bytes 491528 | tf_op jit(solution)/shard_map/ppermute | solution.py:121
  79.0 11.8 %collective-permute-start.12 = (bf16[640,128]{1,0:T(8,128)(2,1)S(1)}, bf16[640,128]{1,0:T(8,128)(2,1)S(1)}, u32[]{:S(2)}, u32[]{:S(2)}) collective-permute-start(bf16[640,128]{1,0:T(8,128)(2,1)S(1)} %get-tuple-element.14), channel_id=1, source_target_pairs={{0,4},{2,6},{4,8},{6,10},{8,12},{10,14},{12,0},{14,2},{1,13},{3,15... | collective-permute-start | bytes 491528 | tf_op jit(solution)/shard_map/ppermute | solution.py:121
  90.8 13.8 %collective-permute-start.13 = (bf16[640,128]{1,0:T(8,128)(2,1)S(1)}, bf16[640,128]{1,0:T(8,128)(2,1)S(1)}, u32[]{:S(2)}, u32[]{:S(2)}) collective-permute-start(bf16[640,128]{1,0:T(8,128)(2,1)S(1)} %get-tuple-element.13), channel_id=1, source_target_pairs={{0,10},{2,12},{4,14},{6,0},{8,2},{10,4},{12,6},{14,8},{1,7},{3,9},... | collective-permute-start | bytes 491528 | tf_op jit(solution)/shard_map/ppermute | solution.py:121
  92.8 19.9 %collective-permute-start.3 = (bf16[288,640]{1,0:T(8,128)(2,1)S(1)}, bf16[288,640]{1,0:T(8,128)(2,1)S(1)}, u32[]{:S(2)}, u32[]{:S(2)}) collective-permute-start(bf16[288,640]{1,0:T(8,128)(2,1)S(1)} %collective-permute-done.1.refs_2_), channel_id=1, source_target_pairs={{0,14},{2,0},{4,2},{6,4},{8,6},{10,8},{12,10},{14,12},{1,15},{3,1}... | collective-permute-start | bytes 1105928 | tf_op jit(solution)/shard_map/ppermute | solution.py:30
  94.7 22.2 %collective-permute-start.8 = (bf16[288,640]{1,0:T(8,128)(2,1)S(1)}, bf16[288,640]{1,0:T(8,128)(2,1)S(1)}, u32[]{:S(2)}, u32[]{:S(2)}) collective-permute-start(bf16[288,640]{1,0:T(8,128)(2,1)S(1)} %collective-permute-done.2.refs_3_), channel_id=1, source_target_pairs={{0,2},{2,4},{4,6},{6,8},{8,10},{10,12},{12,14},{14,0},{1,3},{3,5},... | collective-permute-start | bytes 1105928 | tf_op jit(solution)/shard_map/ppermute | solution.py:29
  98.1 20.7 %collective-permute-start.6 = (bf16[288,640]{1,0:T(8,128)(2,1)S(1)}, bf16[288,640]{1,0:T(8,128)(2,1)S(1)}, u32[]{:S(2)}, u32[]{:S(2)}) collective-permute-start(bf16[288,640]{1,0:T(8,128)(2,1)S(1)} %collective-permute-done.4.refs_6_), channel_id=1, source_target_pairs={{0,2},{2,4},{4,6},{6,8},{8,10},{10,12},{12,14},{14,0},{1,3},{3,5},... | collective-permute-start | bytes 1105928 | tf_op jit(solution)/shard_map/ppermute | solution.py:29
  100.3 20.5 %collective-permute-start.17 = (bf16[288,640]{1,0:T(8,128)(2,1)S(1)}, bf16[288,640]{1,0:T(8,128)(2,1)S(1)}, u32[]{:S(2)}, u32[]{:S(2)}) collective-permute-start(bf16[288,640]{1,0:T(8,128)(2,1)S(1)} %collective-permute-done.7.refs_9_), channel_id=1, source_target_pairs={{0,14},{2,0},{4,2},{6,4},{8,6},{10,8},{12,10},{14,12},{1,15},{3,1}... | collective-permute-start | bytes 1105928 | tf_op jit(solution)/shard_map/ppermute | solution.py:30
  105.5 20.2 %collective-permute-start.15 = (bf16[2240,128]{1,0:T(8,128)(2,1)S(1)}, bf16[2240,128]{1,0:T(8,128)(2,1)S(1)}, u32[]{:S(2)}, u32[]{:S(2)}) collective-permute-start(bf16[2240,128]{1,0:T(8,128)(2,1)S(1)} %pack.1.mine), channel_id=1, source_target_pairs={{0,1},{1,0},{2,3},{3,2},{4,5},{5,4},{6,7},{7,6},{8,9},{9,8},{10,11... | collective-permute-start | bytes 1720328 | tf_op jit(solution)/shard_map/ppermute | solution.py:135
  112.6 16.2 %collective-permute-start.9 = (bf16[288,640]{1,0:T(8,128)(2,1)S(1)}, bf16[288,640]{1,0:T(8,128)(2,1)S(1)}, u32[]{:S(2)}, u32[]{:S(2)}) collective-permute-start(bf16[288,640]{1,0:T(8,128)(2,1)S(1)} %collective-permute-done.3.refs_4_), channel_id=1, source_target_pairs={{0,14},{2,0},{4,2},{6,4},{8,6},{10,8},{12,10},{14,12},{1,15},{3,1}... | collective-permute-start | bytes 1105928 | tf_op jit(solution)/shard_map/ppermute | solution.py:30
  116.9 12.0 %collective-permute-start.10 = (bf16[288,640]{1,0:T(8,128)(2,1)S(1)}, bf16[288,640]{1,0:T(8,128)(2,1)S(1)}, u32[]{:S(2)}, u32[]{:S(2)}) collective-permute-start(bf16[288,640]{1,0:T(8,128)(2,1)S(1)} %collective-permute-done.8.refs_0_), channel_id=1, source_target_pairs={{0,2},{2,4},{4,6},{6,8},{8,10},{10,12},{12,14},{14,0},{1,3},{3,5},... | collective-permute-start | bytes 1105928 | tf_op jit(solution)/shard_map/ppermute | solution.py:32
  118.8 17.0 %collective-permute-start.16 = (bf16[288,640]{1,0:T(8,128)(2,1)S(1)}, bf16[288,640]{1,0:T(8,128)(2,1)S(1)}, u32[]{:S(2)}, u32[]{:S(2)}) collective-permute-start(bf16[288,640]{1,0:T(8,128)(2,1)S(1)} %collective-permute-done.6.refs_8_), channel_id=1, source_target_pairs={{0,2},{2,4},{4,6},{6,8},{8,10},{10,12},{12,14},{14,0},{1,3},{3,5},... | collective-permute-start | bytes 1105928 | tf_op jit(solution)/shard_map/ppermute | solution.py:29
  120.8 15.0 %collective-permute-start.18 = (bf16[288,640]{1,0:T(8,128)(2,1)S(1)}, bf16[288,640]{1,0:T(8,128)(2,1)S(1)}, u32[]{:S(2)}, u32[]{:S(2)}) collective-permute-start(bf16[288,640]{1,0:T(8,128)(2,1)S(1)} %collective-permute-done.17.refs_1_), channel_id=1, source_target_pairs={{0,14},{2,0},{4,2},{6,4},{8,6},{10,8},{12,10},{14,12},{1,15},{3,1}... | collective-permute-start | bytes 1105928 | tf_op jit(solution)/shard_map/ppermute | solution.py:32
  158.8 11.6 %all-to-all-start.1 = ((bf16[8,80,128]{2,1,0:T(8,128)(2,1)}), bf16[8,80,128]{2,1,0:T(8,128)(2,1)S(1)}, u32[]{:S(2)}, u32[]{:S(2)}) async-start(bf16[8,80,128]{2,1,0:T(8,128)(2,1)} %get-tuple-element.10), calls=%async_computation.1 | async-start | bytes 327680 | tf_op jit(solution)/shard_map/all_to_all | solution.py:220
  170.9 18.6 %copy-start.2 = (f32[96,6]{0,1:T(8,128)S(1)}, f32[96,6]{0,1:T(8,128)}, u32[]{:S(2)}) copy-start(f32[96,6]{0,1:T(8,128)} %param.9) | copy-start | bytes 6916
  172.1 40.0 %all-to-all-start.2 = ((bf16[32,9,2,640]{3,2,1,0:T(2,128)(2,1)}), bf16[32,9,2,640]{3,2,1,0:T(2,128)(2,1)S(1)}, u32[]{:S(2)}, u32[]{:S(2)}) async-start(bf16[32,9,2,640]{3,2,1,0:T(2,128)(2,1)} %reshape.66), calls=%async_computation.2 | async-start | bytes 1474560 | tf_op jit(solution)/shard_map/all_to_all | solution.py:178

commit v8 on v7

--- a/solution.py
+++ b/solution.py
@@ -22,15 +22,20 @@
     return [(i, (i + step) % size) for i in range(size)]
 
 
-def hops(x, size, last):
-    found = [(0, x)]
-    up = down = x
-    for step in range(1, size // 2):
-        up = lax.ppermute(up, "tensor", shift(size, 1))
-        down = lax.ppermute(down, "tensor", shift(size, -1))
-        found += [(-step, up), (step, down)]
-    found.append((size // 2, lax.ppermute(up if last > 0 else down, "tensor", shift(size, last))))
-    return found
+def hops(x, size):
+    half = x.shape[0] // 2
+    up = lax.ppermute(x, "tensor", shift(size, 1))
+    down = lax.ppermute(x, "tensor", shift(size, -1))
+    near = [(0, x), (-1, up), (1, down)]
+    ups, downs, far = [up[:half], up[half:]], [down[:half], down[half:]], [[], []]
+    for step in range(2, size // 2):
+        for i in range(2):
+            ups[i] = lax.ppermute(ups[i], "tensor", shift(size, 1))
+            downs[i] = lax.ppermute(downs[i], "tensor", shift(size, -1))
+            far[i] += [(-step, ups[i]), (step, downs[i])]
+    far[0].append((size // 2, lax.ppermute(ups[0], "tensor", shift(size, 1))))
+    far[1].append((size // 2, lax.ppermute(downs[1], "tensor", shift(size, -1))))
+    return near, far
 
 
 def relayout_kernel(x, out):
@@ -44,11 +49,13 @@
     )
 
 
-def first_kernel(size, distances, place, weight, *refs):
-    count = len(distances)
+def first_kernel(size, near, far, place, weight, *refs):
+    half = refs[-1].shape[0]
     for chain in range(2):
-        blocks = refs[chain * count : (chain + 1) * count]
-        refs[2 * count + chain][...] = product_of(place[0], size, distances, blocks, weight)
+        blocks = [x.at[chain * half : (chain + 1) * half] for x in refs[: len(near)]]
+        start = len(near) + chain * len(far)
+        blocks += refs[start : start + len(far)]
+        refs[chain - 2][...] = product_of(place[0], size, near + far, blocks, weight)
 
 
 def activation(size, distances, place, weight, begun, blocks):
@@ -182,7 +189,7 @@
     place = jnp.stack([me, lax.axis_index("dp")]).astype(jnp.int32)
     down_mine, weight_in = down_rows(down_weight, gate_up, place, size, part, hidden)
 
-    chains = [hops(arrived[: rows // 2], size, 1), hops(arrived[rows // 2 :], size, -1)]
+    near, far = hops(arrived, size)
     weight_in = pl.pallas_call(
         relayout_kernel,
         grid=(size,),
@@ -192,19 +199,19 @@
         name="relayout",
         compiler_params=SMALL,
     )(weight_in)
-    early = 5
+    early = 2
     smem, vmem = pl.BlockSpec(memory_space=pltpu.SMEM), pl.BlockSpec(memory_space=pltpu.VMEM)
     begun = pl.pallas_call(
-        functools.partial(first_kernel, size, [d for d, _ in chains[0][:early]]),
+        functools.partial(first_kernel, size, [d for d, _ in near], [d for d, _ in far[0][:early]]),
         out_shape=[jax.ShapeDtypeStruct((rows // 2, 2 * hidden), jnp.float32)] * 2,
-        in_specs=[smem] + [vmem] * (1 + 2 * early),
+        in_specs=[smem] + [vmem] * (1 + len(near) + 2 * early),
         out_specs=[vmem] * 2,
         name="first",
         compiler_params=SMALL,
-    )(place, weight_in, *(x for chain in chains for _, x in chain[:early]))
+    )(place, weight_in, *(x for _, x in near), *(x for chain in far for _, x in chain[:early]))
 
     some = 80
-    distances = [d for d, _ in chains[0][early:]]
+    distances = [d for d, _ in far[0][early:]]
     late = [smem] + [vmem] * (2 + len(distances))
     spread, rest = pl.pallas_call(
         functools.partial(last_a_kernel, size, distances),
@@ -216,7 +223,7 @@
         out_specs=[vmem] * 2,
         name="last_a",
         compiler_params=SMALL,
-    )(place, weight_in, begun[0], *(x for _, x in chains[0][early:]))
+    )(place, weight_in, begun[0], *(x for _, x in far[0][early:]))
     all_a = lax.all_to_all(spread, "tensor", 0, 0, tiled=True)
     act_b = pl.pallas_call(
         functools.partial(last_b_kernel, size, distances),
@@ -225,7 +232,7 @@
         out_specs=vmem,
         name="last_b",
         compiler_params=SMALL,
-    )(place, weight_in, begun[1], *(x for _, x in chains[1][early:]), rest)
+    )(place, weight_in, begun[1], *(x for _, x in far[1][early:]), rest)
     all_b = lax.all_gather(act_b, "tensor")
 
     def outputs(act):

time: 215 us -> 214 us (level)
  the two profiles are of different devices: /device:TPU:1 before, /device:TPU:64 now
where the time goes in v8:
time: 214 us; the launch traced here: 212 us
  starting transfers between devices  68.6 us (32%)
  blocking collectives  62.3 us (29%)
  waiting for transfers between devices  60.6 us (28%)
  local copies, waits for them, and re-layouts  9.33 us (4%)
  Pallas kernels  5.57 us (3%)
  matrix products  3.37 us (2%)
    all_to_all x1, blocking collectives, exchange(): x = lax.all_to_all(x, EXPERT, 0, 0, tiled=True)  35.4 us
    all_gather x1, blocking collectives, local(): all_b = lax.all_gather(act_b, 'tensor')  27 us
    all_to_all x1, waiting for transfers between devices, exchange(): x = lax.all_to_all(x, EXPERT, 0, 0, tiled=True)  23.5 us
    ppermute x4, starting transfers between devices, hops(): downs[i] = lax.ppermute(downs[i], 'tensor', shift(size, -1))  15.9 us
    ppermute x1, waiting for transfers between devices, hops(): up = lax.ppermute(x, 'tensor', shift(size, 1))  15 us
    ppermute x4, starting transfers between devices, hops(): ups[i] = lax.ppermute(ups[i], 'tensor', shift(size, 1))  12 us
    ppermute x3, starting transfers between devices, down_rows(): got.append(lax.ppermute(block, ('tensor', 'dp'), perm))  10.9 us
    all_to_all x1, waiting for transfers between devices, local(): all_a = lax.all_to_all(spread, 'tensor', 0, 0, tiled=True)  8.44 us
  transfers between devices with their start and end apart: 19, of which 6 were waited for; matrix products, arithmetic and copies ran while one was open for 3% of the time, Pallas kernels for 2%

profile of v8, /device:TPU:64, one launch (start us, length us, event | category | flops | bytes accessed | tf_op | source)
XLA Modules:
  0.0 212.2 jit_solution(17509440089216590315)
XLA Ops:
  2.8 35.4 %all_to_all.15 = bf16[32,9,2,640]{3,2,1,0:T(2,128)(2,1)S(1)} all-to-all(bf16[32,9,2,640]{3,2,1,0:T(2,128)(2,1)S(1)} %reshape.63), channel_id=1, replica_groups=mesh['expert_0'=4,'expert_1'=4,'expert_2'=2,'tensor'=8,'dp'=2] {'expert_..., dimensions={0} | all-to-all | bytes 1474560 | tf_op jit(solution)/shard_map/all_to_all | solution.py:185
  38.5 3.5 %collective-permute-start = (bf16[576,640]{1,0:T(8,128)(2,1)S(1)}, bf16[576,640]{1,0:T(8,128)(2,1)S(1)}, u32[]{:S(2)}, u32[]{:S(2)}) collective-permute-start(bf16[576,640]{1,0:T(8,128)(2,1)S(1)} %reshape.64.refs_0_), channel_id=1, source_target_pairs={{0,2},{2,4},{4,6},{6,8},{8,10},{10,12},{12,14},{14,0},{1,3},{3,5},... | collective-permute-start | bytes 2211848 | tf_op jit(solution)/shard_map/ppermute | solution.py:27
  42.0 3.8 %collective-permute-start.1 = (bf16[576,640]{1,0:T(8,128)(2,1)S(1)}, bf16[576,640]{1,0:T(8,128)(2,1)S(1)}, u32[]{:S(2)}, u32[]{:S(2)}) collective-permute-start(bf16[576,640]{1,0:T(8,128)(2,1)S(1)} %reshape.64.refs_0_), channel_id=1, source_target_pairs={{0,14},{2,0},{4,2},{6,4},{8,6},{10,8},{12,10},{14,12},{1,15},{3,1}... | collective-permute-start | bytes 2211848 | tf_op jit(solution)/shard_map/ppermute | solution.py:28
  45.8 15.0 %collective-permute-done.refs_1_ = bf16[576,640]{1,0:T(8,128)(2,1)S(1)} collective-permute-done((bf16[576,640]{1,0:T(8,128)(2,1)S(1)}, bf16[576,640]{1,0:T(8,128)(2,1)S(1)}, u32[]{:S(2)}, u32[]{:S(2)}) %collective-permute-start) | collective-permute-done | bytes 737312 | tf_op jit(solution)/shard_map/ppermute | solution.py:27
  64.7 5.1 %collective-permute-start.5 = (bf16[288,640]{1,0:T(8,128)(2,1)}, bf16[288,640]{1,0:T(8,128)(2,1)S(1)}, u32[]{:S(2)}, u32[]{:S(2)}) collective-permute-start(bf16[288,640]{1,0:T(8,128)(2,1)} %get-tuple-element.17), channel_id=1, source_target_pairs={{0,14},{2,0},{4,2},{6,4},{8,6},{10,8},{12,10},{14,12},{1,15},{3,1}... | collective-permute-start | bytes 1105928 | tf_op jit(solution)/shard_map/ppermute | solution.py:34
  69.9 2.0 dynamic-slice_bitcast_fusion
  71.8 2.4 %collective-permute-start.9 = (bf16[640,128]{1,0:T(8,128)(2,1)}, bf16[640,128]{1,0:T(8,128)(2,1)S(1)}, u32[]{:S(2)}, u32[]{:S(2)}) collective-permute-start(bf16[640,128]{1,0:T(8,128)(2,1)} %get-tuple-element.15), channel_id=1, source_target_pairs={{0,2},{2,4},{4,6},{6,8},{8,10},{10,12},{12,14},{14,0},{1,15},{3,1}... | collective-permute-start | bytes 491528 | tf_op jit(solution)/shard_map/ppermute | solution.py:128
  74.3 4.6 %collective-permute-start.10 = (bf16[640,128]{1,0:T(8,128)(2,1)}, bf16[640,128]{1,0:T(8,128)(2,1)S(1)}, u32[]{:S(2)}, u32[]{:S(2)}) collective-permute-start(bf16[640,128]{1,0:T(8,128)(2,1)} %get-tuple-element.14), channel_id=1, source_target_pairs={{0,4},{2,6},{4,8},{6,10},{8,12},{10,14},{12,0},{14,2},{1,13},{3,15... | collective-permute-start | bytes 491528 | tf_op jit(solution)/shard_map/ppermute | solution.py:128
  79.8 4.0 %collective-permute-start.12 = (bf16[320,128]{1,0:T(8,128)(2,1)S(1)}, bf16[320,128]{1,0:T(8,128)(2,1)S(1)}, u32[]{:S(2)}, u32[]{:S(2)}) collective-permute-start(bf16[320,128]{1,0:T(8,128)(2,1)S(1)} %dynamic-slice_bitcast_fusion.4), channel_id=1, source_target_pairs={{0,8},{2,10},{4,12},{6,14},{8,0},{10,2},{12,4},{14,6},{1,9},{3,11}... | collective-permute-start | bytes 245768 | tf_op jit(solution)/shard_map/ppermute | solution.py:132
  83.8 7.1 %collective-permute-done.12.fourth = bf16[320,128]{1,0:T(8,128)(2,1)S(1)} collective-permute-done((bf16[320,128]{1,0:T(8,128)(2,1)S(1)}, bf16[320,128]{1,0:T(8,128)(2,1)S(1)}, u32[]{:S(2)}, u32[]{:S(2)}) %collective-permute-start.12) | collective-permute-done | bytes 81952 | tf_op jit(solution)/shard_map/ppermute | solution.py:132
  90.8 3.9 %collective-permute-start.11 = (bf16[640,128]{1,0:T(8,128)(2,1)}, bf16[640,128]{1,0:T(8,128)(2,1)S(1)}, u32[]{:S(2)}, u32[]{:S(2)}) collective-permute-start(bf16[640,128]{1,0:T(8,128)(2,1)} %get-tuple-element.13), channel_id=1, source_target_pairs={{0,10},{2,12},{4,14},{6,0},{8,2},{10,4},{12,6},{14,8},{1,7},{3,9},... | collective-permute-start | bytes 491528 | tf_op jit(solution)/shard_map/ppermute | solution.py:128
  94.7 2.9 %collective-permute-start.3 = (bf16[288,640]{1,0:T(8,128)(2,1)}, bf16[288,640]{1,0:T(8,128)(2,1)S(1)}, u32[]{:S(2)}, u32[]{:S(2)}) collective-permute-start(bf16[288,640]{1,0:T(8,128)(2,1)} %get-tuple-element.18), channel_id=1, source_target_pairs={{0,14},{2,0},{4,2},{6,4},{8,6},{10,8},{12,10},{14,12},{1,15},{3,1}... | collective-permute-start | bytes 1105928 | tf_op jit(solution)/shard_map/ppermute | solution.py:34
  97.6 4.2 %collective-permute-start.6 = (bf16[288,640]{1,0:T(8,128)(2,1)S(1)}, bf16[288,640]{1,0:T(8,128)(2,1)S(1)}, u32[]{:S(2)}, u32[]{:S(2)}) collective-permute-start(bf16[288,640]{1,0:T(8,128)(2,1)S(1)} %collective-permute-done.2.refs_3_), channel_id=1, source_target_pairs={{0,2},{2,4},{4,6},{6,8},{8,10},{10,12},{12,14},{14,0},{1,3},{3,5},... | collective-permute-start | bytes 1105928 | tf_op jit(solution)/shard_map/ppermute | solution.py:33
  101.9 3.9 %collective-permute-start.4 = (bf16[288,640]{1,0:T(8,128)(2,1)}, bf16[288,640]{1,0:T(8,128)(2,1)S(1)}, u32[]{:S(2)}, u32[]{:S(2)}) collective-permute-start(bf16[288,640]{1,0:T(8,128)(2,1)} %get-tuple-element.19), channel_id=1, source_target_pairs={{0,2},{2,4},{4,6},{6,8},{8,10},{10,12},{12,14},{14,0},{1,3},{3,5},... | collective-permute-start | bytes 1105928 | tf_op jit(solution)/shard_map/ppermute | solution.py:33
  105.8 4.0 %collective-permute-start.15 = (bf16[288,640]{1,0:T(8,128)(2,1)S(1)}, bf16[288,640]{1,0:T(8,128)(2,1)S(1)}, u32[]{:S(2)}, u32[]{:S(2)}) collective-permute-start(bf16[288,640]{1,0:T(8,128)(2,1)S(1)} %collective-permute-done.5.refs_6_), channel_id=1, source_target_pairs={{0,14},{2,0},{4,2},{6,4},{8,6},{10,8},{12,10},{14,12},{1,15},{3,1}... | collective-permute-start | bytes 1105928 | tf_op jit(solution)/shard_map/ppermute | solution.py:34
  109.9 1.9 collective-permute-start.13
  111.9 3.9 %collective-permute-start.7 = (bf16[288,640]{1,0:T(8,128)(2,1)S(1)}, bf16[288,640]{1,0:T(8,128)(2,1)S(1)}, u32[]{:S(2)}, u32[]{:S(2)}) collective-permute-start(bf16[288,640]{1,0:T(8,128)(2,1)S(1)} %collective-permute-done.3.refs_4_), channel_id=1, source_target_pairs={{0,14},{2,0},{4,2},{6,4},{8,6},{10,8},{12,10},{14,12},{1,15},{3,1}... | collective-permute-start | bytes 1105928 | tf_op jit(solution)/shard_map/ppermute | solution.py:34
  118.2 6.0 %collective-permute-done.4.refs_5_ = bf16[288,640]{1,0:T(8,128)(2,1)S(1)} collective-permute-done((bf16[288,640]{1,0:T(8,128)(2,1)}, bf16[288,640]{1,0:T(8,128)(2,1)S(1)}, u32[]{:S(2)}, u32[]{:S(2)}) %collective-permute-start.4) | collective-permute-done | bytes 368672 | tf_op jit(solution)/shard_map/ppermute | solution.py:33
  126.1 5.1 %collective-permute-start.16 = (bf16[288,640]{1,0:T(8,128)(2,1)S(1)}, bf16[288,640]{1,0:T(8,128)(2,1)S(1)}, u32[]{:S(2)}, u32[]{:S(2)}) collective-permute-start(bf16[288,640]{1,0:T(8,128)(2,1)S(1)} %collective-permute-done.15.refs_1_), channel_id=1, source_target_pairs={{0,14},{2,0},{4,2},{6,4},{8,6},{10,8},{12,10},{14,12},{1,15},{3,1}... | collective-permute-start | bytes 1105928 | tf_op jit(solution)/shard_map/ppermute | solution.py:37
  139.2 27.0 %all-gather = bf16[3968,128]{1,0:T(8,128)(2,1)S(1)} all-gather(bf16[496,128]{1,0:T(8,128)(2,1)S(1)} %last_b.1), channel_id=2, replica_groups=mesh['expert_0'=4,'expert_1'=4,'expert_2'=2,'tensor'=8,'dp'=2] {'tensor'}, dimensions={0}, use_global_device_ids=true | all-gather | bytes 1142784 | tf_op jit(solution)/shard_map/all_gather | solution.py:236
  166.2 4.2 %all-to-all-start.1 = ((bf16[8,80,128]{2,1,0:T(8,128)(2,1)}), bf16[8,80,128]{2,1,0:T(8,128)(2,1)S(1)}, u32[]{:S(2)}, u32[]{:S(2)}) async-start(bf16[8,80,128]{2,1,0:T(8,128)(2,1)} %get-tuple-element.10), calls=%async_computation.1 | async-start | bytes 327680 | tf_op jit(solution)/shard_map/all_to_all | solution.py:227
  171.4 8.4 %all-to-all-done.1 = bf16[8,80,128]{2,1,0:T(8,128)(2,1)S(1)} async-done(((bf16[8,80,128]{2,1,0:T(8,128)(2,1)}), bf16[8,80,128]{2,1,0:T(8,128)(2,1)S(1)}, u32[]{:S(2)}, u32[]{:S(2)}) %all-to-all-start.1) | async-done | bytes 163872 | tf_op jit(solution)/shard_map/all_to_all | solution.py:227
  181.6 5.3 %all-to-all-start.2 = ((bf16[32,9,2,640]{3,2,1,0:T(2,128)(2,1)}), bf16[32,9,2,640]{3,2,1,0:T(2,128)(2,1)S(1)}, u32[]{:S(2)}, u32[]{:S(2)}) async-start(bf16[32,9,2,640]{3,2,1,0:T(2,128)(2,1)} %reshape.66), calls=%async_computation.2 | async-start | bytes 1474560 | tf_op jit(solution)/shard_map/all_to_all | solution.py:185
  187.1 23.5 %all-to-all-done.2 = bf16[32,9,2,640]{3,2,1,0:T(2,128)(2,1)S(1)} async-done(((bf16[32,9,2,640]{3,2,1,0:T(2,128)(2,1)}), bf16[32,9,2,640]{3,2,1,0:T(2,128)(2,1)S(1)}, u32[]{:S(2)}, u32[]{:S(2)}) %all-to-all-start.2) | async-done | bytes 737312 | tf_op jit(solution)/shard_map/all_to_all | solution.py:185
  (62 shorter events, 24.5 us)
Async XLA Ops:
  0.0 2.1 copy-start
  38.5 22.3 %collective-permute-start = (bf16[576,640]{1,0:T(8,128)(2,1)S(1)}, bf16[576,640]{1,0:T(8,128)(2,1)S(1)}, u32[]{:S(2)}, u32[]{:S(2)}) collective-permute-start(bf16[576,640]{1,0:T(8,128)(2,1)S(1)} %reshape.64.refs_0_), channel_id=1, source_target_pairs={{0,2},{2,4},{4,6},{6,8},{8,10},{10,12},{12,14},{14,0},{1,3},{3,5},... | collective-permute-start | bytes 2211848 | tf_op jit(solution)/shard_map/ppermute | solution.py:27
  42.0 21.7 %collective-permute-start.1 = (bf16[576,640]{1,0:T(8,128)(2,1)S(1)}, bf16[576,640]{1,0:T(8,128)(2,1)S(1)}, u32[]{:S(2)}, u32[]{:S(2)}) collective-permute-start(bf16[576,640]{1,0:T(8,128)(2,1)S(1)} %reshape.64.refs_0_), channel_id=1, source_target_pairs={{0,14},{2,0},{4,2},{6,4},{8,6},{10,8},{12,10},{14,12},{1,15},{3,1}... | collective-permute-start | bytes 2211848 | tf_op jit(solution)/shard_map/ppermute | solution.py:28
  61.7 35.9 %collective-permute-start.2 = (bf16[288,640]{1,0:T(8,128)(2,1)}, bf16[288,640]{1,0:T(8,128)(2,1)S(1)}, u32[]{:S(2)}, u32[]{:S(2)}) collective-permute-start(bf16[288,640]{1,0:T(8,128)(2,1)} %get-tuple-element.20), channel_id=1, source_target_pairs={{0,2},{2,4},{4,6},{6,8},{8,10},{10,12},{12,14},{14,0},{1,3},{3,5},... | collective-permute-start | bytes 1105928 | tf_op jit(solution)/shard_map/ppermute | solution.py:33
  63.7 8.2 %copy-start.1 = (bf16[576,640]{1,0:T(8,128)(2,1)}, bf16[576,640]{1,0:T(8,128)(2,1)S(1)}, u32[]{:S(2)}) copy-start(bf16[576,640]{1,0:T(8,128)(2,1)S(1)} %collective-permute-done.1.refs_2_) | copy-start | bytes 2211844
  64.7 41.1 %collective-permute-start.5 = (bf16[288,640]{1,0:T(8,128)(2,1)}, bf16[288,640]{1,0:T(8,128)(2,1)S(1)}, u32[]{:S(2)}, u32[]{:S(2)}) collective-permute-start(bf16[288,640]{1,0:T(8,128)(2,1)} %get-tuple-element.17), channel_id=1, source_target_pairs={{0,14},{2,0},{4,2},{6,4},{8,6},{10,8},{12,10},{14,12},{1,15},{3,1}... | collective-permute-start | bytes 1105928 | tf_op jit(solution)/shard_map/ppermute | solution.py:34
  71.8 22.9 %collective-permute-start.9 = (bf16[640,128]{1,0:T(8,128)(2,1)}, bf16[640,128]{1,0:T(8,128)(2,1)S(1)}, u32[]{:S(2)}, u32[]{:S(2)}) collective-permute-start(bf16[640,128]{1,0:T(8,128)(2,1)} %get-tuple-element.15), channel_id=1, source_target_pairs={{0,2},{2,4},{4,6},{6,8},{8,10},{10,12},{12,14},{14,0},{1,15},{3,1}... | collective-permute-start | bytes 491528 | tf_op jit(solution)/shard_map/ppermute | solution.py:128
  74.3 27.6 %collective-permute-start.10 = (bf16[640,128]{1,0:T(8,128)(2,1)}, bf16[640,128]{1,0:T(8,128)(2,1)S(1)}, u32[]{:S(2)}, u32[]{:S(2)}) collective-permute-start(bf16[640,128]{1,0:T(8,128)(2,1)} %get-tuple-element.14), channel_id=1, source_target_pairs={{0,4},{2,6},{4,8},{6,10},{8,12},{10,14},{12,0},{14,2},{1,13},{3,15... | collective-permute-start | bytes 491528 | tf_op jit(solution)/shard_map/ppermute | solution.py:128
  79.8 11.1 %collective-permute-start.12 = (bf16[320,128]{1,0:T(8,128)(2,1)S(1)}, bf16[320,128]{1,0:T(8,128)(2,1)S(1)}, u32[]{:S(2)}, u32[]{:S(2)}) collective-permute-start(bf16[320,128]{1,0:T(8,128)(2,1)S(1)} %dynamic-slice_bitcast_fusion.4), channel_id=1, source_target_pairs={{0,8},{2,10},{4,12},{6,14},{8,0},{10,2},{12,4},{14,6},{1,9},{3,11}... | collective-permute-start | bytes 245768 | tf_op jit(solution)/shard_map/ppermute | solution.py:132
  90.8 19.0 %collective-permute-start.11 = (bf16[640,128]{1,0:T(8,128)(2,1)}, bf16[640,128]{1,0:T(8,128)(2,1)S(1)}, u32[]{:S(2)}, u32[]{:S(2)}) collective-permute-start(bf16[640,128]{1,0:T(8,128)(2,1)} %get-tuple-element.13), channel_id=1, source_target_pairs={{0,10},{2,12},{4,14},{6,0},{8,2},{10,4},{12,6},{14,8},{1,7},{3,9},... | collective-permute-start | bytes 491528 | tf_op jit(solution)/shard_map/ppermute | solution.py:128
  94.7 17.1 %collective-permute-start.3 = (bf16[288,640]{1,0:T(8,128)(2,1)}, bf16[288,640]{1,0:T(8,128)(2,1)S(1)}, u32[]{:S(2)}, u32[]{:S(2)}) collective-permute-start(bf16[288,640]{1,0:T(8,128)(2,1)} %get-tuple-element.18), channel_id=1, source_target_pairs={{0,14},{2,0},{4,2},{6,4},{8,6},{10,8},{12,10},{14,12},{1,15},{3,1}... | collective-permute-start | bytes 1105928 | tf_op jit(solution)/shard_map/ppermute | solution.py:34
  97.6 18.7 %collective-permute-start.6 = (bf16[288,640]{1,0:T(8,128)(2,1)S(1)}, bf16[288,640]{1,0:T(8,128)(2,1)S(1)}, u32[]{:S(2)}, u32[]{:S(2)}) collective-permute-start(bf16[288,640]{1,0:T(8,128)(2,1)S(1)} %collective-permute-done.2.refs_3_), channel_id=1, source_target_pairs={{0,2},{2,4},{4,6},{6,8},{8,10},{10,12},{12,14},{14,0},{1,3},{3,5},... | collective-permute-start | bytes 1105928 | tf_op jit(solution)/shard_map/ppermute | solution.py:33
  101.9 22.3 %collective-permute-start.4 = (bf16[288,640]{1,0:T(8,128)(2,1)}, bf16[288,640]{1,0:T(8,128)(2,1)S(1)}, u32[]{:S(2)}, u32[]{:S(2)}) collective-permute-start(bf16[288,640]{1,0:T(8,128)(2,1)} %get-tuple-element.19), channel_id=1, source_target_pairs={{0,2},{2,4},{4,6},{6,8},{8,10},{10,12},{12,14},{14,0},{1,3},{3,5},... | collective-permute-start | bytes 1105928 | tf_op jit(solution)/shard_map/ppermute | solution.py:33
  105.8 27.5 %copy-start.4 = (bf16[288,640]{1,0:T(8,128)(2,1)}, bf16[288,640]{1,0:T(8,128)(2,1)S(1)}, u32[]{:S(2)}) copy-start(bf16[288,640]{1,0:T(8,128)(2,1)S(1)} %collective-permute-done.5.refs_6_) | copy-start | bytes 1105924
  105.8 20.3 %collective-permute-start.15 = (bf16[288,640]{1,0:T(8,128)(2,1)S(1)}, bf16[288,640]{1,0:T(8,128)(2,1)S(1)}, u32[]{:S(2)}, u32[]{:S(2)}) collective-permute-start(bf16[288,640]{1,0:T(8,128)(2,1)S(1)} %collective-permute-done.5.refs_6_), channel_id=1, source_target_pairs={{0,14},{2,0},{4,2},{6,4},{8,6},{10,8},{12,10},{14,12},{1,15},{3,1}... | collective-permute-start | bytes 1105928 | tf_op jit(solution)/shard_map/ppermute | solution.py:34
  109.9 23.5 %collective-permute-start.13 = (bf16[2240,128]{1,0:T(8,128)(2,1)S(1)}, bf16[2240,128]{1,0:T(8,128)(2,1)S(1)}, u32[]{:S(2)}, u32[]{:S(2)}) collective-permute-start(bf16[2240,128]{1,0:T(8,128)(2,1)S(1)} %pack.1.mine), channel_id=1, source_target_pairs={{0,1},{1,0},{2,3},{3,2},{4,5},{5,4},{6,7},{7,6},{8,9},{9,8},{10,11... | collective-permute-start | bytes 1720328 | tf_op jit(solution)/shard_map/ppermute | solution.py:142
  111.9 24.6 %collective-permute-start.7 = (bf16[288,640]{1,0:T(8,128)(2,1)S(1)}, bf16[288,640]{1,0:T(8,128)(2,1)S(1)}, u32[]{:S(2)}, u32[]{:S(2)}) collective-permute-start(bf16[288,640]{1,0:T(8,128)(2,1)S(1)} %collective-permute-done.3.refs_4_), channel_id=1, source_target_pairs={{0,14},{2,0},{4,2},{6,4},{8,6},{10,8},{12,10},{14,12},{1,15},{3,1}... | collective-permute-start | bytes 1105928 | tf_op jit(solution)/shard_map/ppermute | solution.py:34
  116.3 20.2 %collective-permute-start.8 = (bf16[288,640]{1,0:T(8,128)(2,1)S(1)}, bf16[288,640]{1,0:T(8,128)(2,1)S(1)}, u32[]{:S(2)}, u32[]{:S(2)}) collective-permute-start(bf16[288,640]{1,0:T(8,128)(2,1)S(1)} %collective-permute-done.6.refs_0_), channel_id=1, source_target_pairs={{0,2},{2,4},{4,6},{6,8},{8,10},{10,12},{12,14},{14,0},{1,3},{3,5},... | collective-permute-start | bytes 1105928 | tf_op jit(solution)/shard_map/ppermute | solution.py:36
  124.2 14.0 %collective-permute-start.14 = (bf16[288,640]{1,0:T(8,128)(2,1)S(1)}, bf16[288,640]{1,0:T(8,128)(2,1)S(1)}, u32[]{:S(2)}, u32[]{:S(2)}) collective-permute-start(bf16[288,640]{1,0:T(8,128)(2,1)S(1)} %collective-permute-done.4.refs_5_), channel_id=1, source_target_pairs={{0,2},{2,4},{4,6},{6,8},{8,10},{10,12},{12,14},{14,0},{1,3},{3,5},... | collective-permute-start | bytes 1105928 | tf_op jit(solution)/shard_map/ppermute | solution.py:33
  126.1 12.1 %collective-permute-start.16 = (bf16[288,640]{1,0:T(8,128)(2,1)S(1)}, bf16[288,640]{1,0:T(8,128)(2,1)S(1)}, u32[]{:S(2)}, u32[]{:S(2)}) collective-permute-start(bf16[288,640]{1,0:T(8,128)(2,1)S(1)} %collective-permute-done.15.refs_1_), channel_id=1, source_target_pairs={{0,14},{2,0},{4,2},{6,4},{8,6},{10,8},{12,10},{14,12},{1,15},{3,1}... | collective-permute-start | bytes 1105928 | tf_op jit(solution)/shard_map/ppermute | solution.py:37
  131.3 1.7 copy-start.3
  166.2 13.7 %all-to-all-start.1 = ((bf16[8,80,128]{2,1,0:T(8,128)(2,1)}), bf16[8,80,128]{2,1,0:T(8,128)(2,1)S(1)}, u32[]{:S(2)}, u32[]{:S(2)}) async-start(bf16[8,80,128]{2,1,0:T(8,128)(2,1)} %get-tuple-element.10), calls=%async_computation.1 | async-start | bytes 327680 | tf_op jit(solution)/shard_map/all_to_all | solution.py:227
  180.5 6.5 %copy-start.6 = (f32[96,6]{0,1:T(8,128)S(1)}, f32[96,6]{0,1:T(8,128)}, u32[]{:S(2)}) copy-start(f32[96,6]{0,1:T(8,128)} %param.9) | copy-start | bytes 6916
  181.6 29.0 %all-to-all-start.2 = ((bf16[32,9,2,640]{3,2,1,0:T(2,128)(2,1)}), bf16[32,9,2,640]{3,2,1,0:T(2,128)(2,1)S(1)}, u32[]{:S(2)}, u32[]{:S(2)}) async-start(bf16[32,9,2,640]{3,2,1,0:T(2,128)(2,1)} %reshape.66), calls=%async_computation.2 | async-start | bytes 1474560 | tf_op jit(solution)/shard_map/all_to_all | solution.py:185
  (2 other events, 2.3 us)

commit v9 on v7

--- a/solution.py
+++ b/solution.py
@@ -70,6 +70,34 @@
     *blocks, rest, out = refs
     out[: rest.shape[0], :] = rest[...]
     out[rest.shape[0] :, :] = activation(size, distances, place, weight, begun, blocks)
+
+
+def route_kernel(capacity, routes, old_map, new_map, tokens, out, place):
+    picks, count = routes.shape
+    experts = old_map.shape[1]
+    rows = experts * capacity
+    bf16 = jnp.bfloat16
+
+    def ids(shape, axis):
+        return lax.broadcasted_iota(jnp.int32, shape, axis)
+
+    def ones(hit):
+        return jnp.where(hit, 1.0, 0.0).astype(bf16)
+
+    named = routes[...]
+    slots = ids((experts, count), 0)
+    chosen = sum(jnp.where(named[k : k + 1, :] == slots, 1.0, 0.0) for k in range(picks)).astype(bf16)
+    values = ids((experts, experts), 0)
+    chosen = dot(ones(values == new_map[...]), chosen).astype(bf16)
+    chosen = dot(ones(values == old_map[...]), chosen, ((0,), (0,)))
+    before = ones(ids((count, count), 0) < ids((count, count), 1))
+    position = jnp.where(chosen > 0.5, dot(chosen.astype(bf16), before), -1.0)
+    place[...] = position.astype(jnp.int32)
+    row = ids((rows, experts), 0) - capacity * ids((rows, experts), 1)
+    inside = (row >= 0) & (row < capacity)
+    wanted = jnp.sum(jnp.where(inside, row, 0).astype(jnp.float32), axis=1, keepdims=True)
+    assign = ones(dot(ones(inside), position.astype(bf16)) == wanted)
+    out[...] = dot(assign, tokens[...]).astype(out.dtype)
 
 
 def pack_kernel(first, second, third, fourth, out):
@@ -156,22 +184,18 @@
     rows = experts * capacity
     bf16 = jnp.bfloat16
 
-    slot_ids = jnp.arange(experts, dtype=jnp.int32)
-    holder = jnp.sum(jnp.where(new_map[:, None] == old_map[None, :], slot_ids[None, :], 0), axis=1)
-    target = jnp.sum(
-        jnp.where(routes[:, :, None] == slot_ids[None, None, :], holder[None, None, :], 0), axis=2
-    )
-    hits = target[:, :, None] == slot_ids[None, None, :]
-    member = jnp.any(hits, axis=1)
-    weight = jnp.sum(jnp.where(hits, gates[:, :, None], 0.0), axis=1)
-    ones = jnp.tril(jnp.ones((tok_rows, tok_rows), bf16), -1)
-    position = dot(ones, member.astype(bf16)).astype(jnp.int32)
-    place = jnp.where(member, position, -1)
-    cap_ids = jnp.arange(capacity, dtype=jnp.int32)
-    matches = place[:, :, None] == cap_ids[None, None, :]
-    assign = matches.astype(bf16).reshape(tok_rows, rows)
-    combine = jnp.where(matches, weight[:, :, None], 0.0).reshape(tok_rows, rows)
-    outgoing = dot(assign, tokens, ((0,), (0,))).astype(bf16)
+    vmem = pl.BlockSpec(memory_space=pltpu.VMEM)
+    outgoing, position = pl.pallas_call(
+        functools.partial(route_kernel, capacity),
+        out_shape=[
+            jax.ShapeDtypeStruct((rows, part), bf16),
+            jax.ShapeDtypeStruct((experts, tok_rows), jnp.int32),
+        ],
+        in_specs=[vmem] * 4,
+        out_specs=[vmem] * 2,
+        name="route",
+        compiler_params=SMALL,
+    )(routes.T, old_map.reshape(1, experts), new_map.reshape(1, experts), tokens)
 
     def exchange(x):
         x = x.reshape(experts, capacity // 2, 2, part)
@@ -193,7 +217,7 @@
         compiler_params=SMALL,
     )(weight_in)
     early = 5
-    smem, vmem = pl.BlockSpec(memory_space=pltpu.SMEM), pl.BlockSpec(memory_space=pltpu.VMEM)
+    smem = pl.BlockSpec(memory_space=pltpu.SMEM)
     begun = pl.pallas_call(
         functools.partial(first_kernel, size, [d for d, _ in chains[0][:early]]),
         out_shape=[jax.ShapeDtypeStruct((rows // 2, 2 * hidden), jnp.float32)] * 2,
@@ -232,7 +256,19 @@
         return dot(act, down_mine, ((0, 2), (0, 2))).astype(bf16)
 
     expert_out = jnp.concatenate([outputs(all_a), outputs(all_b)], axis=0)
+    expert_out, routes, gates, position, old_map, new_map = lax.optimization_barrier(
+        (expert_out, routes, gates, position, old_map, new_map)
+    )
     returned = exchange(expert_out)
+    slot_ids = jnp.arange(experts, dtype=jnp.int32)
+    holder = jnp.sum(jnp.where(new_map[:, None] == old_map[None, :], slot_ids[None, :], 0), axis=1)
+    target = jnp.sum(
+        jnp.where(routes[:, :, None] == slot_ids[None, None, :], holder[None, None, :], 0), axis=2
+    )
+    hits = target[:, :, None] == slot_ids[None, None, :]
+    weight = jnp.sum(jnp.where(hits, gates[:, :, None], 0.0), axis=1)
+    matches = position.T[:, :, None] == jnp.arange(capacity, dtype=jnp.int32)[None, None, :]
+    combine = jnp.where(matches, weight[:, :, None], 0.0).reshape(tok_rows, rows)
     mixed = jnp.dot(
         combine,
         returned.astype(jnp.float32),

time: 215 us -> 214 us (level)
  the two profiles are of different devices: /device:TPU:1 before, /device:TPU:64 now
where the time goes in v9:
time: 214 us; the launch traced here: 213 us
  starting transfers between devices  79 us (37%)
  blocking collectives  62 us (29%)
  waiting for transfers between devices  54 us (25%)
  local copies, waits for them, and re-layouts  7.25 us (3%)
  Pallas kernels  7.05 us (3%)
  matrix products  2.77 us (1%)
    all_to_all x1, blocking collectives, exchange(): x = lax.all_to_all(x, EXPERT, 0, 0, tiled=True)  35.4 us
    all_gather x1, blocking collectives, local(): all_b = lax.all_gather(act_b, 'tensor')  26.7 us
    all_to_all x1, waiting for transfers between devices, exchange(): x = lax.all_to_all(x, EXPERT, 0, 0, tiled=True)  22.9 us
    ppermute x6, starting transfers between devices, hops(): down = lax.ppermute(down, 'tensor', shift(size, -1))  19.8 us
    ppermute x6, starting transfers between devices, hops(): up = lax.ppermute(up, 'tensor', shift(size, 1))  18.5 us
    ppermute x3, starting transfers between devices, down_rows(): got.append(lax.ppermute(block, ('tensor', 'dp'), perm))  14.3 us
    ppermute x3, waiting for transfers between devices, down_rows(): got.append(lax.ppermute(block, ('tensor', 'dp'), perm))  14.1 us
    ppermute x6, waiting for transfers between devices, hops(): up = lax.ppermute(up, 'tensor', shift(size, 1))  8.46 us
  transfers between devices with their start and end apart: 21, of which 7 were waited for; matrix products, arithmetic and copies ran while one was open for 2% of the time, Pallas kernels for 2%

profile of v9, /device:TPU:64, one launch (start us, length us, event | category | flops | bytes accessed | tf_op | source)
XLA Modules:
  0.0 213.1 jit_solution(12240238593041084241)
XLA Ops:
  4.1 35.4 %all_to_all.15 = bf16[32,9,2,640]{3,2,1,0:T(2,128)(2,1)S(1)} all-to-all(bf16[32,9,2,640]{3,2,1,0:T(2,128)(2,1)S(1)} %reshape.68), channel_id=1, replica_groups=mesh['expert_0'=4,'expert_1'=4,'expert_2'=2,'tensor'=8,'dp'=2] {'expert_..., dimensions={0} | all-to-all | bytes 1474560 | tf_op jit(solution)/shard_map/all_to_all | solution.py:202
  39.8 3.5 %collective-permute-start = (bf16[288,640]{1,0:T(8,128)(2,1)S(1)}, bf16[288,640]{1,0:T(8,128)(2,1)}, u32[]{:S(2)}, u32[]{:S(2)}) collective-permute-start(bf16[288,640]{1,0:T(8,128)(2,1)S(1)} %get-tuple-element.34.refs_0_), channel_id=1, source_target_pairs={{0,2},{2,4},{4,6},{6,8},{8,10},{10,12},{12,14},{14,0},{1,3},{3,5},... | collective-permute-start | bytes 1105928 | tf_op jit(solution)/shard_map/ppermute | solution.py:29
  43.3 3.8 %collective-permute-start.5 = (bf16[288,640]{1,0:T(8,128)(2,1)S(1)}, bf16[288,640]{1,0:T(8,128)(2,1)}, u32[]{:S(2)}, u32[]{:S(2)}) collective-permute-start(bf16[288,640]{1,0:T(8,128)(2,1)S(1)} %get-tuple-element.33.refs_5_), channel_id=1, source_target_pairs={{0,14},{2,0},{4,2},{6,4},{8,6},{10,8},{12,10},{14,12},{1,15},{3,1}... | collective-permute-start | bytes 1105928 | tf_op jit(solution)/shard_map/ppermute | solution.py:30
  48.2 7.5 %collective-permute-start.14 = (bf16[320,128]{1,0:T(8,128)(2,1)S(1)}, bf16[320,128]{1,0:T(8,128)(2,1)S(1)}, u32[]{:S(2)}, u32[]{:S(2)}) collective-permute-start(bf16[320,128]{1,0:T(8,128)(2,1)S(1)} %dynamic-slice_bitcast_fusion.4), channel_id=1, source_target_pairs={{0,8},{2,10},{4,12},{6,14},{8,0},{10,2},{12,4},{14,6},{1,9},{3,11}... | collective-permute-start | bytes 245768 | tf_op jit(solution)/shard_map/ppermute | solution.py:153
  55.7 1.9 collective-permute-start.1
  57.6 3.9 %collective-permute-start.4 = (bf16[288,640]{1,0:T(8,128)(2,1)S(1)}, bf16[288,640]{1,0:T(8,128)(2,1)S(1)}, u32[]{:S(2)}, u32[]{:S(2)}) collective-permute-start(bf16[288,640]{1,0:T(8,128)(2,1)S(1)} %get-tuple-element.33.refs_5_), channel_id=1, source_target_pairs={{0,2},{2,4},{4,6},{6,8},{8,10},{10,12},{12,14},{14,0},{1,3},{3,5},... | collective-permute-start | bytes 1105928 | tf_op jit(solution)/shard_map/ppermute | solution.py:29
  63.5 5.1 %collective-permute-start.7 = (bf16[288,640]{1,0:T(8,128)(2,1)}, bf16[288,640]{1,0:T(8,128)(2,1)S(1)}, u32[]{:S(2)}, u32[]{:S(2)}) collective-permute-start(bf16[288,640]{1,0:T(8,128)(2,1)} %collective-permute-done.5.refs_7_), channel_id=1, source_target_pairs={{0,14},{2,0},{4,2},{6,4},{8,6},{10,8},{12,10},{14,12},{1,15},{3,1}... | collective-permute-start | bytes 1105928 | tf_op jit(solution)/shard_map/ppermute | solution.py:30
  71.8 8.2 %collective-permute-done.11.first = bf16[640,128]{1,0:T(8,128)(2,1)S(1)} collective-permute-done((bf16[640,128]{1,0:T(8,128)(2,1)S(1)}, bf16[640,128]{1,0:T(8,128)(2,1)S(1)}, u32[]{:S(2)}, u32[]{:S(2)}) %collective-permute-start.11) | collective-permute-done | bytes 163872 | tf_op jit(solution)/shard_map/ppermute | solution.py:149
  80.0 3.8 %collective-permute-start.12 = (bf16[640,128]{1,0:T(8,128)(2,1)S(1)}, bf16[640,128]{1,0:T(8,128)(2,1)S(1)}, u32[]{:S(2)}, u32[]{:S(2)}) collective-permute-start(bf16[640,128]{1,0:T(8,128)(2,1)S(1)} %get-tuple-element.30), channel_id=1, source_target_pairs={{0,4},{2,6},{4,8},{6,10},{8,12},{10,14},{12,0},{14,2},{1,13},{3,15... | collective-permute-start | bytes 491528 | tf_op jit(solution)/shard_map/ppermute | solution.py:149
  83.8 5.8 %collective-permute-done.12.second = bf16[640,128]{1,0:T(8,128)(2,1)S(1)} collective-permute-done((bf16[640,128]{1,0:T(8,128)(2,1)S(1)}, bf16[640,128]{1,0:T(8,128)(2,1)S(1)}, u32[]{:S(2)}, u32[]{:S(2)}) %collective-permute-start.12) | collective-permute-done | bytes 163872 | tf_op jit(solution)/shard_map/ppermute | solution.py:149
  89.6 8.7 %collective-permute-start.13 = (bf16[640,128]{1,0:T(8,128)(2,1)S(1)}, bf16[640,128]{1,0:T(8,128)(2,1)S(1)}, u32[]{:S(2)}, u32[]{:S(2)}) collective-permute-start(bf16[640,128]{1,0:T(8,128)(2,1)S(1)} %get-tuple-element.29), channel_id=1, source_target_pairs={{0,10},{2,12},{4,14},{6,0},{8,2},{10,4},{12,6},{14,8},{1,7},{3,9},... | collective-permute-start | bytes 491528 | tf_op jit(solution)/shard_map/ppermute | solution.py:149
  100.2 3.9 %collective-permute-start.8 = (bf16[288,640]{1,0:T(8,128)(2,1)S(1)}, bf16[288,640]{1,0:T(8,128)(2,1)S(1)}, u32[]{:S(2)}, u32[]{:S(2)}) collective-permute-start(bf16[288,640]{1,0:T(8,128)(2,1)S(1)} %collective-permute-done.2.refs_3_), channel_id=1, source_target_pairs={{0,2},{2,4},{4,6},{6,8},{8,10},{10,12},{12,14},{14,0},{1,3},{3,5},... | collective-permute-start | bytes 1105928 | tf_op jit(solution)/shard_map/ppermute | solution.py:29
  106.1 5.1 %collective-permute-start.17 = (bf16[288,640]{1,0:T(8,128)(2,1)S(1)}, bf16[288,640]{1,0:T(8,128)(2,1)S(1)}, u32[]{:S(2)}, u32[]{:S(2)}) collective-permute-start(bf16[288,640]{1,0:T(8,128)(2,1)S(1)} %collective-permute-done.7.refs_9_), channel_id=1, source_target_pairs={{0,14},{2,0},{4,2},{6,4},{8,6},{10,8},{12,10},{14,12},{1,15},{3,1}... | collective-permute-start | bytes 1105928 | tf_op jit(solution)/shard_map/ppermute | solution.py:30
  115.7 3.4 %collective-permute-start.10 = (bf16[288,640]{1,0:T(8,128)(2,1)S(1)}, bf16[288,640]{1,0:T(8,128)(2,1)S(1)}, u32[]{:S(2)}, u32[]{:S(2)}) collective-permute-start(bf16[288,640]{1,0:T(8,128)(2,1)S(1)} %collective-permute-done.8.refs_0_), channel_id=1, source_target_pairs={{0,2},{2,4},{4,6},{6,8},{8,10},{10,12},{12,14},{14,0},{1,3},{3,5},... | collective-permute-start | bytes 1105928 | tf_op jit(solution)/shard_map/ppermute | solution.py:32
  119.1 4.5 %collective-permute-done.6.refs_8_ = bf16[288,640]{1,0:T(8,128)(2,1)S(1)} collective-permute-done((bf16[288,640]{1,0:T(8,128)(2,1)S(1)}, bf16[288,640]{1,0:T(8,128)(2,1)S(1)}, u32[]{:S(2)}, u32[]{:S(2)}) %collective-permute-start.6) | collective-permute-done | bytes 368672 | tf_op jit(solution)/shard_map/ppermute | solution.py:29
  123.6 3.3 %collective-permute-start.16 = (bf16[288,640]{1,0:T(8,128)(2,1)S(1)}, bf16[288,640]{1,0:T(8,128)(2,1)S(1)}, u32[]{:S(2)}, u32[]{:S(2)}) collective-permute-start(bf16[288,640]{1,0:T(8,128)(2,1)S(1)} %collective-permute-done.6.refs_8_), channel_id=1, source_target_pairs={{0,2},{2,4},{4,6},{6,8},{8,10},{10,12},{12,14},{14,0},{1,3},{3,5},... | collective-permute-start | bytes 1105928 | tf_op jit(solution)/shard_map/ppermute | solution.py:29
  126.9 3.7 %collective-permute-start.18 = (bf16[288,640]{1,0:T(8,128)(2,1)S(1)}, bf16[288,640]{1,0:T(8,128)(2,1)S(1)}, u32[]{:S(2)}, u32[]{:S(2)}) collective-permute-start(bf16[288,640]{1,0:T(8,128)(2,1)S(1)} %collective-permute-done.17.refs_1_), channel_id=1, source_target_pairs={{0,14},{2,0},{4,2},{6,4},{8,6},{10,8},{12,10},{14,12},{1,15},{3,1}... | collective-permute-start | bytes 1105928 | tf_op jit(solution)/shard_map/ppermute | solution.py:32
  131.7 2.4 %first.1 = (f32[288,256]{1,0:T(8,128)S(1)}, f32[288,256]{1,0:T(8,128)S(1)}) custom-call(s32[2]{0:T(128)S(1)} %pad_add_fusion.place, bf16[8,640,256]{2,1,0:T(8,128)(2,1)S(1)} %relayout.1.weight, bf16[288,640]{1,0:T(8,128)(2,1)S(1)} %get-tuple-element.34.refs_0_, bf16[288,640]{1,0:T(8,128)(2,1)} %collective-permute-done.refs_1_, ...), custom_call_target="tpu_custom_call" | custom-call | tf_op jit(solution)/shard_map/first/pallas_call | solution.py:221
  135.9 3.4 %collective-permute-done.16.refs_0_ = bf16[288,640]{1,0:T(8,128)(2,1)S(1)} collective-permute-done((bf16[288,640]{1,0:T(8,128)(2,1)S(1)}, bf16[288,640]{1,0:T(8,128)(2,1)S(1)}, u32[]{:S(2)}, u32[]{:S(2)}) %collective-permute-start.16) | collective-permute-done | bytes 368672 | tf_op jit(solution)/shard_map/ppermute | solution.py:29
  140.4 26.7 %all-gather = bf16[3968,128]{1,0:T(8,128)(2,1)S(1)} all-gather(bf16[496,128]{1,0:T(8,128)(2,1)S(1)} %last_b.1), channel_id=2, replica_groups=mesh['expert_0'=4,'expert_1'=4,'expert_2'=2,'tensor'=8,'dp'=2] {'tensor'}, dimensions={0}, use_global_device_ids=true | all-gather | bytes 1142784 | tf_op jit(solution)/shard_map/all_gather | solution.py:253
  167.0 6.0 %all-to-all-start.1 = ((bf16[8,80,128]{2,1,0:T(8,128)(2,1)}), bf16[8,80,128]{2,1,0:T(8,128)(2,1)S(1)}, u32[]{:S(2)}, u32[]{:S(2)}) async-start(bf16[8,80,128]{2,1,0:T(8,128)(2,1)} %get-tuple-element.19), calls=%async_computation.1 | async-start | bytes 327680 | tf_op jit(solution)/shard_map/all_to_all | solution.py:244
  174.0 8.4 %all-to-all-done.1 = bf16[8,80,128]{2,1,0:T(8,128)(2,1)S(1)} async-done(((bf16[8,80,128]{2,1,0:T(8,128)(2,1)}), bf16[8,80,128]{2,1,0:T(8,128)(2,1)S(1)}, u32[]{:S(2)}, u32[]{:S(2)}) %all-to-all-start.1) | async-done | bytes 163872 | tf_op jit(solution)/shard_map/all_to_all | solution.py:244
  184.2 3.9 %all-to-all-start.2 = ((bf16[32,9,2,640]{3,2,1,0:T(2,128)(2,1)}), bf16[32,9,2,640]{3,2,1,0:T(2,128)(2,1)S(1)}, u32[]{:S(2)}, u32[]{:S(2)}) async-start(bf16[32,9,2,640]{3,2,1,0:T(2,128)(2,1)} %reshape.71), calls=%async_computation.2 | async-start | bytes 1474560 | tf_op jit(solution)/shard_map/all_to_all | solution.py:202
  188.6 22.9 %all-to-all-done.2 = bf16[32,9,2,640]{3,2,1,0:T(2,128)(2,1)S(1)} async-done(((bf16[32,9,2,640]{3,2,1,0:T(2,128)(2,1)}), bf16[32,9,2,640]{3,2,1,0:T(2,128)(2,1)S(1)}, u32[]{:S(2)}, u32[]{:S(2)}) %all-to-all-start.2) | async-done | bytes 737312 | tf_op jit(solution)/shard_map/all_to_all | solution.py:202
  (62 shorter events, 27.2 us)
Async XLA Ops:
  39.8 21.8 %collective-permute-start = (bf16[288,640]{1,0:T(8,128)(2,1)S(1)}, bf16[288,640]{1,0:T(8,128)(2,1)}, u32[]{:S(2)}, u32[]{:S(2)}) collective-permute-start(bf16[288,640]{1,0:T(8,128)(2,1)S(1)} %get-tuple-element.34.refs_0_), channel_id=1, source_target_pairs={{0,2},{2,4},{4,6},{6,8},{8,10},{10,12},{12,14},{14,0},{1,3},{3,5},... | collective-permute-start | bytes 1105928 | tf_op jit(solution)/shard_map/ppermute | solution.py:29
  43.3 20.2 %collective-permute-start.5 = (bf16[288,640]{1,0:T(8,128)(2,1)S(1)}, bf16[288,640]{1,0:T(8,128)(2,1)}, u32[]{:S(2)}, u32[]{:S(2)}) collective-permute-start(bf16[288,640]{1,0:T(8,128)(2,1)S(1)} %get-tuple-element.33.refs_5_), channel_id=1, source_target_pairs={{0,14},{2,0},{4,2},{6,4},{8,6},{10,8},{12,10},{14,12},{1,15},{3,1}... | collective-permute-start | bytes 1105928 | tf_op jit(solution)/shard_map/ppermute | solution.py:30
  47.1 83.6 %copy-start = (bf16[1,5120,2,128]{3,2,1,0:T(2,128)(2,1)S(1)}, bf16[1,5120,2,128]{3,2,1,0:T(2,128)(2,1)}, u32[]{:S(2)}) copy-start(bf16[1,5120,2,128]{3,2,1,0:T(2,128)(2,1)} %x.1) | copy-start | bytes 7864324
  48.2 21.7 %collective-permute-start.14 = (bf16[320,128]{1,0:T(8,128)(2,1)S(1)}, bf16[320,128]{1,0:T(8,128)(2,1)S(1)}, u32[]{:S(2)}, u32[]{:S(2)}) collective-permute-start(bf16[320,128]{1,0:T(8,128)(2,1)S(1)} %dynamic-slice_bitcast_fusion.4), channel_id=1, source_target_pairs={{0,8},{2,10},{4,12},{6,14},{8,0},{10,2},{12,4},{14,6},{1,9},{3,11}... | collective-permute-start | bytes 245768 | tf_op jit(solution)/shard_map/ppermute | solution.py:153
  55.7 42.6 %collective-permute-start.1 = (bf16[288,640]{1,0:T(8,128)(2,1)S(1)}, bf16[288,640]{1,0:T(8,128)(2,1)S(1)}, u32[]{:S(2)}, u32[]{:S(2)}) collective-permute-start(bf16[288,640]{1,0:T(8,128)(2,1)S(1)} %get-tuple-element.34.refs_0_), channel_id=1, source_target_pairs={{0,14},{2,0},{4,2},{6,4},{8,6},{10,8},{12,10},{14,12},{1,15},{3,1}... | collective-permute-start | bytes 1105928 | tf_op jit(solution)/shard_map/ppermute | solution.py:30
  57.6 46.5 %collective-permute-start.4 = (bf16[288,640]{1,0:T(8,128)(2,1)S(1)}, bf16[288,640]{1,0:T(8,128)(2,1)S(1)}, u32[]{:S(2)}, u32[]{:S(2)}) collective-permute-start(bf16[288,640]{1,0:T(8,128)(2,1)S(1)} %get-tuple-element.33.refs_5_), channel_id=1, source_target_pairs={{0,2},{2,4},{4,6},{6,8},{8,10},{10,12},{12,14},{14,0},{1,3},{3,5},... | collective-permute-start | bytes 1105928 | tf_op jit(solution)/shard_map/ppermute | solution.py:29
  61.5 38.7 %collective-permute-start.2 = (bf16[288,640]{1,0:T(8,128)(2,1)}, bf16[288,640]{1,0:T(8,128)(2,1)S(1)}, u32[]{:S(2)}, u32[]{:S(2)}) collective-permute-start(bf16[288,640]{1,0:T(8,128)(2,1)} %collective-permute-done.refs_1_), channel_id=1, source_target_pairs={{0,2},{2,4},{4,6},{6,8},{8,10},{10,12},{12,14},{14,0},{1,3},{3,5},... | collective-permute-start | bytes 1105928 | tf_op jit(solution)/shard_map/ppermute | solution.py:29
  63.5 42.6 %collective-permute-start.7 = (bf16[288,640]{1,0:T(8,128)(2,1)}, bf16[288,640]{1,0:T(8,128)(2,1)S(1)}, u32[]{:S(2)}, u32[]{:S(2)}) collective-permute-start(bf16[288,640]{1,0:T(8,128)(2,1)} %collective-permute-done.5.refs_7_), channel_id=1, source_target_pairs={{0,14},{2,0},{4,2},{6,4},{8,6},{10,8},{12,10},{14,12},{1,15},{3,1}... | collective-permute-start | bytes 1105928 | tf_op jit(solution)/shard_map/ppermute | solution.py:30
  69.8 10.2 %collective-permute-start.11 = (bf16[640,128]{1,0:T(8,128)(2,1)S(1)}, bf16[640,128]{1,0:T(8,128)(2,1)S(1)}, u32[]{:S(2)}, u32[]{:S(2)}) collective-permute-start(bf16[640,128]{1,0:T(8,128)(2,1)S(1)} %get-tuple-element.31), channel_id=1, source_target_pairs={{0,2},{2,4},{4,6},{6,8},{8,10},{10,12},{12,14},{14,0},{1,15},{3,1}... | collective-permute-start | bytes 491528 | tf_op jit(solution)/shard_map/ppermute | solution.py:149
  80.0 9.6 %collective-permute-start.12 = (bf16[640,128]{1,0:T(8,128)(2,1)S(1)}, bf16[640,128]{1,0:T(8,128)(2,1)S(1)}, u32[]{:S(2)}, u32[]{:S(2)}) collective-permute-start(bf16[640,128]{1,0:T(8,128)(2,1)S(1)} %get-tuple-element.30), channel_id=1, source_target_pairs={{0,4},{2,6},{4,8},{6,10},{8,12},{10,14},{12,0},{14,2},{1,13},{3,15... | collective-permute-start | bytes 491528 | tf_op jit(solution)/shard_map/ppermute | solution.py:149
  89.6 21.6 %collective-permute-start.13 = (bf16[640,128]{1,0:T(8,128)(2,1)S(1)}, bf16[640,128]{1,0:T(8,128)(2,1)S(1)}, u32[]{:S(2)}, u32[]{:S(2)}) collective-permute-start(bf16[640,128]{1,0:T(8,128)(2,1)S(1)} %get-tuple-element.29), channel_id=1, source_target_pairs={{0,10},{2,12},{4,14},{6,0},{8,2},{10,4},{12,6},{14,8},{1,7},{3,9},... | collective-permute-start | bytes 491528 | tf_op jit(solution)/shard_map/ppermute | solution.py:149
  98.3 14.9 %collective-permute-start.3 = (bf16[288,640]{1,0:T(8,128)(2,1)S(1)}, bf16[288,640]{1,0:T(8,128)(2,1)S(1)}, u32[]{:S(2)}, u32[]{:S(2)}) collective-permute-start(bf16[288,640]{1,0:T(8,128)(2,1)S(1)} %collective-permute-done.1.refs_2_), channel_id=1, source_target_pairs={{0,14},{2,0},{4,2},{6,4},{8,6},{10,8},{12,10},{14,12},{1,15},{3,1}... | collective-permute-start | bytes 1105928 | tf_op jit(solution)/shard_map/ppermute | solution.py:30
  100.2 15.5 %collective-permute-start.8 = (bf16[288,640]{1,0:T(8,128)(2,1)S(1)}, bf16[288,640]{1,0:T(8,128)(2,1)S(1)}, u32[]{:S(2)}, u32[]{:S(2)}) collective-permute-start(bf16[288,640]{1,0:T(8,128)(2,1)S(1)} %collective-permute-done.2.refs_3_), channel_id=1, source_target_pairs={{0,2},{2,4},{4,6},{6,8},{8,10},{10,12},{12,14},{14,0},{1,3},{3,5},... | collective-permute-start | bytes 1105928 | tf_op jit(solution)/shard_map/ppermute | solution.py:29
  104.1 19.4 %collective-permute-start.6 = (bf16[288,640]{1,0:T(8,128)(2,1)S(1)}, bf16[288,640]{1,0:T(8,128)(2,1)S(1)}, u32[]{:S(2)}, u32[]{:S(2)}) collective-permute-start(bf16[288,640]{1,0:T(8,128)(2,1)S(1)} %collective-permute-done.4.refs_6_), channel_id=1, source_target_pairs={{0,2},{2,4},{4,6},{6,8},{8,10},{10,12},{12,14},{14,0},{1,3},{3,5},... | collective-permute-start | bytes 1105928 | tf_op jit(solution)/shard_map/ppermute | solution.py:29
  106.1 20.8 %collective-permute-start.17 = (bf16[288,640]{1,0:T(8,128)(2,1)S(1)}, bf16[288,640]{1,0:T(8,128)(2,1)S(1)}, u32[]{:S(2)}, u32[]{:S(2)}) collective-permute-start(bf16[288,640]{1,0:T(8,128)(2,1)S(1)} %collective-permute-done.7.refs_9_), channel_id=1, source_target_pairs={{0,14},{2,0},{4,2},{6,4},{8,6},{10,8},{12,10},{14,12},{1,15},{3,1}... | collective-permute-start | bytes 1105928 | tf_op jit(solution)/shard_map/ppermute | solution.py:30
  111.3 19.8 %collective-permute-start.15 = (bf16[2240,128]{1,0:T(8,128)(2,1)S(1)}, bf16[2240,128]{1,0:T(8,128)(2,1)S(1)}, u32[]{:S(2)}, u32[]{:S(2)}) collective-permute-start(bf16[2240,128]{1,0:T(8,128)(2,1)S(1)} %pack.1.mine), channel_id=1, source_target_pairs={{0,1},{1,0},{2,3},{3,2},{4,5},{5,4},{6,7},{7,6},{8,9},{9,8},{10,11... | collective-permute-start | bytes 1720328 | tf_op jit(solution)/shard_map/ppermute | solution.py:163
  113.2 20.9 %collective-permute-start.9 = (bf16[288,640]{1,0:T(8,128)(2,1)S(1)}, bf16[288,640]{1,0:T(8,128)(2,1)S(1)}, u32[]{:S(2)}, u32[]{:S(2)}) collective-permute-start(bf16[288,640]{1,0:T(8,128)(2,1)S(1)} %collective-permute-done.3.refs_4_), channel_id=1, source_target_pairs={{0,14},{2,0},{4,2},{6,4},{8,6},{10,8},{12,10},{14,12},{1,15},{3,1}... | collective-permute-start | bytes 1105928 | tf_op jit(solution)/shard_map/ppermute | solution.py:30
  115.7 18.5 %collective-permute-start.10 = (bf16[288,640]{1,0:T(8,128)(2,1)S(1)}, bf16[288,640]{1,0:T(8,128)(2,1)S(1)}, u32[]{:S(2)}, u32[]{:S(2)}) collective-permute-start(bf16[288,640]{1,0:T(8,128)(2,1)S(1)} %collective-permute-done.8.refs_0_), channel_id=1, source_target_pairs={{0,2},{2,4},{4,6},{6,8},{8,10},{10,12},{12,14},{14,0},{1,3},{3,5},... | collective-permute-start | bytes 1105928 | tf_op jit(solution)/shard_map/ppermute | solution.py:32
  123.6 15.7 %collective-permute-start.16 = (bf16[288,640]{1,0:T(8,128)(2,1)S(1)}, bf16[288,640]{1,0:T(8,128)(2,1)S(1)}, u32[]{:S(2)}, u32[]{:S(2)}) collective-permute-start(bf16[288,640]{1,0:T(8,128)(2,1)S(1)} %collective-permute-done.6.refs_8_), channel_id=1, source_target_pairs={{0,2},{2,4},{4,6},{6,8},{8,10},{10,12},{12,14},{14,0},{1,3},{3,5},... | collective-permute-start | bytes 1105928 | tf_op jit(solution)/shard_map/ppermute | solution.py:29
  126.9 12.4 %collective-permute-start.18 = (bf16[288,640]{1,0:T(8,128)(2,1)S(1)}, bf16[288,640]{1,0:T(8,128)(2,1)S(1)}, u32[]{:S(2)}, u32[]{:S(2)}) collective-permute-start(bf16[288,640]{1,0:T(8,128)(2,1)S(1)} %collective-permute-done.17.refs_1_), channel_id=1, source_target_pairs={{0,14},{2,0},{4,2},{6,4},{8,6},{10,8},{12,10},{14,12},{1,15},{3,1}... | collective-permute-start | bytes 1105928 | tf_op jit(solution)/shard_map/ppermute | solution.py:32
  167.0 15.4 %all-to-all-start.1 = ((bf16[8,80,128]{2,1,0:T(8,128)(2,1)}), bf16[8,80,128]{2,1,0:T(8,128)(2,1)S(1)}, u32[]{:S(2)}, u32[]{:S(2)}) async-start(bf16[8,80,128]{2,1,0:T(8,128)(2,1)} %get-tuple-element.19), calls=%async_computation.1 | async-start | bytes 327680 | tf_op jit(solution)/shard_map/all_to_all | solution.py:244
  183.1 5.3 %copy-start.3 = (s32[96,6]{0,1:T(8,128)S(1)}, s32[96,6]{0,1:T(8,128)}, u32[]{:S(2)}) copy-start(s32[96,6]{0,1:T(8,128)} %param.8) | copy-start | bytes 6916
  183.1 5.4 %copy-start.8 = (f32[96,6]{0,1:T(8,128)S(1)}, f32[96,6]{0,1:T(8,128)}, u32[]{:S(2)}) copy-start(f32[96,6]{0,1:T(8,128)} %param.9) | copy-start | bytes 6916
  184.2 27.3 %all-to-all-start.2 = ((bf16[32,9,2,640]{3,2,1,0:T(2,128)(2,1)}), bf16[32,9,2,640]{3,2,1,0:T(2,128)(2,1)S(1)}, u32[]{:S(2)}, u32[]{:S(2)}) async-start(bf16[32,9,2,640]{3,2,1,0:T(2,128)(2,1)} %reshape.71), calls=%async_computation.2 | async-start | bytes 1474560 | tf_op jit(solution)/shard_map/all_to_all | solution.py:202
  (6 other events, 13.1 us)
